TPU v7x, 128 devices: a whole 4x4x4 slice. The times are simulated.
128 devices in a mesh: seq: 16 (over z, y_lo, core), head: 8 (over x, y_hi).
Axes of the slice: x: 4, y: 4 (y_hi: 2, y_lo: 2; y = y_hi * 2 + y_lo), z: 4, core: 2. Of those that a mesh axis runs over, the one named last changes fastest.
Arguments:
- tokens: bfloat16 [128, 512, 1024], P('seq'), may hold values from -36 to 36
- lengths: int32 [128], P('seq'), may hold values from 1 to 512, 32768 in all
- attn_in: float32 [1024, 3, 1024], P(('seq', 'head')), may hold values from -0.4 to 0.4
- attn_out: float32 [1024, 1024], P(None, ('seq', 'head')), may hold values from -0.1875 to 0.1875
- mlp_in: float32 [1024, 4096], P(('seq', 'head')), may hold values from -0.1875 to 0.1875
- mlp_out: float32 [4096, 1024], P(None, ('seq', 'head')), may hold values from -0.09375 to 0.09375
- norm_gain: float32 [2, 1024], replicated, may hold values from 0.5 to 1.5
- norm_shift: float32 [2, 1024], replicated, may hold values from -3 to 3
Outputs:
- encoded: bfloat16 [128, 512, 1024], P('seq', 'head')
- key_cache: bfloat16 [128, 512, 1024], P('seq', None, 'head')
- value_cache: bfloat16 [128, 512, 1024], P('seq', None, 'head')
Inputs may be any that keep to these rules, and one draw needn't show every extreme that they name: `lengths`: some prompt has exactly 512 tokens.
All inputs are finite; a program needn't handle non-finite values. No bound on the sum of `lengths` on one device may be relied on, other than what follows from the above.
Results may differ from a plain program's by a relative error of at most 0.02.
Values may be sent and summed in bfloat16 or wider, within the bound.
A program may use at most 128 MiB of HBM per device.

v0:
```python
import math

import jax
import jax.numpy as jnp
from jax import lax
from jax.sharding import PartitionSpec as P

DH = 64


EPSILON = 1e-05
CHUNKS = 1


def layer_norm(values, gain, shift):
    center = values - jnp.mean(values, axis=-1, keepdims=True)
    spread = jnp.mean(center * center, axis=-1, keepdims=True)
    return center * lax.rsqrt(spread + EPSILON) * gain + shift


def regroup_weights(attn_in, attn_out, mlp_in, mlp_out, heads_axis, seq_axis):
    rows = attn_in.shape[0]
    model_width = attn_in.shape[2]
    hidden_width = mlp_in.shape[1]
    block_width = model_width // heads_axis
    in_piece = attn_in.astype(jnp.bfloat16).reshape(rows, 3, heads_axis, block_width)
    in_piece = jnp.transpose(in_piece, (0, 2, 1, 3)).reshape(rows, heads_axis, 3 * block_width)
    out_piece = attn_out.astype(jnp.bfloat16).T.reshape(rows, heads_axis, block_width)
    mlp_rows = jnp.concatenate(
        [mlp_in.astype(jnp.bfloat16), mlp_out.astype(jnp.bfloat16).T], axis=1)
    mlp_piece = jnp.broadcast_to(mlp_rows[:, None], (rows, heads_axis, 2 * hidden_width))
    packed = jnp.concatenate([in_piece, out_piece, mlp_piece], axis=2)
    packed = lax.all_to_all(packed, "head", 1, 0, tiled=True)
    packed = packed.reshape(rows * heads_axis, packed.shape[2])
    attn_part = packed[:, :4 * block_width]
    attn_part = jnp.broadcast_to(attn_part[None], (seq_axis,) + attn_part.shape)
    attn_whole = lax.all_to_all(attn_part, "seq", 0, 0, tiled=True)
    attn_whole = attn_whole.reshape(-1, 4 * block_width)
    qkv_weight = attn_whole[:, :3 * block_width].reshape(-1, 3, block_width)
    proj_weight_t = attn_whole[:, 3 * block_width:]
    up_weight = lax.all_gather(
        packed[:, 4 * block_width:4 * block_width + hidden_width], "seq", axis=0, tiled=True)
    down_weight_t = lax.all_gather(
        packed[:, 4 * block_width + hidden_width:], "seq", axis=0, tiled=True)
    return qkv_weight, proj_weight_t, up_weight, down_weight_t


def encode_chunk(tokens, lengths, qkv_weight, proj_weight_t, up_weight, down_weight_t,
                 norm_gain, norm_shift, heads_axis, head_index):
    prompts = tokens.shape[0]
    seq_len = tokens.shape[1]
    model_width = tokens.shape[2]
    hidden_width = up_weight.shape[1]
    block_width = model_width // heads_axis
    hidden_block = hidden_width // heads_axis
    local_heads = block_width // DH
    row_count = seq_len // heads_axis
    row_start = head_index * row_count
    projected = jnp.einsum(
        "pld,dte->plte", tokens, qkv_weight, preferred_element_type=jnp.float32
    ).astype(jnp.bfloat16)
    positions = jnp.arange(seq_len, dtype=jnp.int32)
    inside = positions[None, :] < lengths[:, None]
    key_part = projected[:, :, 1]
    value_part = projected[:, :, 2]
    queries = projected[:, :, 0].reshape(prompts, seq_len, local_heads, DH)
    key_heads = key_part.reshape(prompts, seq_len, local_heads, DH)
    value_heads = value_part.reshape(prompts, seq_len, local_heads, DH)
    scores = jnp.einsum(
        "pqhd,pkhd->phqk", queries, key_heads, preferred_element_type=jnp.float32
    ) * (1.0 / math.sqrt(DH))
    scores = jnp.where(inside[:, None, None, :], scores, -1e30)
    row_peak = jnp.max(scores, axis=-1, keepdims=True)
    raised = jnp.exp(scores - row_peak)
    weights = (raised / jnp.sum(raised, axis=-1, keepdims=True)).astype(jnp.bfloat16)
    context = jnp.einsum(
        "phqk,pkhd->pqhd", weights, value_heads, preferred_element_type=jnp.float32
    )
    context = context.astype(jnp.bfloat16).reshape(prompts, heads_axis, row_count, block_width)
    key_cache = jnp.where(inside[:, :, None], key_part, jnp.zeros_like(key_part))
    value_cache = jnp.where(inside[:, :, None], value_part, jnp.zeros_like(value_part))
    attn_partial = jnp.einsum(
        "pjrd,ed->jpre", context, proj_weight_t, preferred_element_type=jnp.float32
    ).astype(jnp.bfloat16)
    attn_blocks = lax.all_to_all(attn_partial, "head", 0, 0, tiled=True)
    attn_rows = jnp.sum(attn_blocks.astype(jnp.float32), axis=0)
    token_rows = lax.dynamic_slice_in_dim(tokens, row_start, row_count, 1)
    normed_rows = layer_norm(
        token_rows.astype(jnp.float32) + attn_rows, norm_gain[0], norm_shift[0]
    ).astype(jnp.bfloat16)
    hidden = jax.nn.gelu(
        jnp.einsum("pld,df->plf", normed_rows, up_weight, preferred_element_type=jnp.float32),
        approximate=False,
    ).astype(jnp.bfloat16)
    hidden = hidden.reshape(prompts, row_count, heads_axis, hidden_block)
    down_blocks = down_weight_t.reshape(model_width, heads_axis, hidden_block)
    mlp_blocks = jnp.einsum(
        "plbf,ebf->plbe", hidden, down_blocks, preferred_element_type=jnp.float32
    ).astype(jnp.bfloat16)
    mlp_rows = jnp.sum(mlp_blocks.astype(jnp.float32), axis=2)
    finished = layer_norm(normed_rows.astype(jnp.float32) + mlp_rows, norm_gain[1], norm_shift[1])
    inside_rows = lax.dynamic_slice_in_dim(inside, row_start, row_count, 1)
    encoded = jnp.where(inside_rows[:, :, None], finished, 0.0).astype(jnp.bfloat16)
    return encoded, key_cache, value_cache


def shards(tokens, lengths, attn_in, attn_out, mlp_in, mlp_out, norm_gain, norm_shift):
    heads_axis = lax.axis_size("head")
    head_index = lax.axis_index("head")
    qkv_weight, proj_weight_t, up_weight, down_weight_t = regroup_weights(
        attn_in, attn_out, mlp_in, mlp_out, heads_axis, lax.axis_size("seq"))
    prompts = tokens.shape[0]
    chunk = max(1, prompts // CHUNKS)
    pieces = []
    for lower in range(0, prompts, chunk):
        pieces.append(encode_chunk(
            tokens[lower:lower + chunk], lengths[lower:lower + chunk], qkv_weight,
            proj_weight_t, up_weight, down_weight_t, norm_gain, norm_shift,
            heads_axis, head_index))
    return tuple(jnp.concatenate(parts, axis=0) for parts in zip(*pieces))


def solution(mesh):
    in_specs = (
        P("seq", None, None),
        P("seq"),
        P(("seq", "head"), None, None),
        P(None, ("seq", "head")),
        P(("seq", "head"), None),
        P(None, ("seq", "head")),
        P(),
        P(),
    )
    out_specs = (P("seq", "head", None), P("seq", None, "head"), P("seq", None, "head"))
    return jax.shard_map(shards, mesh=mesh, in_specs=in_specs, out_specs=out_specs, check_vma=False)
```

profile of v0, /device:TPU:1, one launch (start us, length us, event | category | flops | bytes accessed | tf_op | source)
XLA Modules:
  0.0 299.3 jit_solution(10767176931100129540)
XLA Ops:
  7.2 0.0 copy-start.3
  7.2 0.0 all-gather.5.cloned.1.call-start
  7.2 0.9 convert_bitcast_fusion.2
  8.1 0.9 convert_element_type.62
  9.0 0.9 copy_bitcast_fusion.1
  9.9 0.8 convert_bitcast_fusion.4
  10.7 0.1 broadcast_in_dim.36
  10.8 0.1 pad_maximum_fusion
  10.9 24.1 %all_to_all.25 = bf16[8,8,8704]{2,0,1:T(8,128)(2,1)S(1)} all-to-all(bf16[8,8,8704]{2,0,1:T(8,128)(2,1)S(1)} %pad_maximum_fusion), channel_id=1, replica_groups=mesh['seq'=16,'head'=8] {'head'}, dimensions={1} | all-to-all | bytes 2228224 | tf_op jit(solution)/shard_map/all_to_all | solution.py:33
  35.0 1.1 fusion.39
  36.1 0.0 all-gather.5.cloned.1.call-update
  36.2 1.1 broadcast_in_dim.37
  37.2 7.6 %all-to-all-start.1 = ((bf16[16,64,512]{2,1,0:T(8,128)(2,1)}), bf16[16,64,512]{2,1,0:T(8,128)(2,1)S(1)}, u32[]{:S(2)}, u32[]{:S(2)}) async-start(bf16[16,64,512]{2,1,0:T(8,128)(2,1)} %broadcast_in_dim.37), calls=%async_computation.1 | async-start | bytes 2097152 | tf_op jit(solution)/shard_map/all_to_all | solution.py:37
  44.8 0.0 all-gather.3.cloned.1.call-start
  44.8 0.0 copy-done.3
  44.9 0.1 iota_compare_fusion
  44.9 0.6 all-gather.3.cloned.1.call-update
  45.5 26.6 %all-to-all-done.1 = bf16[16,64,512]{2,1,0:T(8,128)(2,1)S(1)} async-done(((bf16[16,64,512]{2,1,0:T(8,128)(2,1)}), bf16[16,64,512]{2,1,0:T(8,128)(2,1)S(1)}, u32[]{:S(2)}, u32[]{:S(2)}) %all-to-all-start.1) | async-done | bytes 1048608 | tf_op jit(solution)/shard_map/all_to_all | solution.py:37
  72.1 0.0 copy-start
  72.1 0.1 slice.50
  72.2 1.2 copy.28
  73.4 0.0 copy-done
  73.4 7.3 %convert_bitcast_fusion.1 = bf16[8,512,3,128]{1,3,0,2:T(8,128)(2,1)S(1)} fusion(bf16[1024,3,128,1]{0,2,3,1:T(8,128)(2,1)} %bitcast.104, bf16[8,512,1024]{2,1,0:T(8,128)(2,1)} %param.8), kind=kOutput, calls=%fused_computation.40 | convolution fusion | flops 3222798336 | bytes 12320768 | tf_op jit(solution)/shard_map/pld,dte->plte/dot_general | solution.py:59
  80.6 1.8 fusion.38
  82.4 10.7 %fusion.42 = (f32[8,2,512]{2,1,0:T(2,128)S(1)}, f32[8,2,512,512]{2,3,1,0:T(8,128)}) fusion(pred[8,512]{1,0:T(8,128)(4,1)S(1)} %iota_compare_fusion, bf16[8,512,2,64]{1,3,2,0:T(8,128)(2,1)} %bitcast.103, bf16[8,512,2,64]{1,3,2,0:T(8,128)(2,1)} %bitcast.102), kind=kOutput, calls=%fused_computation.74 | convolution fusion | flops 553648640 | bytes 18911232 | tf_op jit(solution)/shard_map/sub | solution.py:74
  93.1 8.9 %fusion.33 = bf16[8,512,2,64]{1,3,2,0:T(8,128)(2,1)} fusion(bf16[8,512,2,64]{1,3,2,0:T(8,128)(2,1)} %bitcast.101, f32[8,2,512,512]{2,3,1,0:T(8,128)} %get-tuple-element.24, f32[8,2,512]{2,1,0:T(2,128)S(1)} %get-tuple-element.23), kind=kOutput, calls=%fused_computation.50 | convolution fusion | flops 545783808 | bytes 18907136 | tf_op jit(solution)/shard_map/phqk,pkhd->pqhd/dot_general | solution.py:76
  102.0 3.9 %reshape.108 = bf16[8,8,64,128]{2,1,3,0:T(8,128)(2,1)} reshape(bf16[8,512,2,64]{1,3,2,0:T(8,128)(2,1)} %fusion.33) | data formatting | bytes 2097152 | tf_op jit(solution)/shard_map/reshape | solution.py:79
  105.9 7.3 %convert_bitcast_fusion = bf16[8,8,64,1024]{3,2,0,1:T(8,128)(2,1)} fusion(bf16[8,8,64,128]{2,1,3,0:T(8,128)(2,1)} %reshape.108, bf16[1024,512]{1,0:T(8,128)(2,1)} %bitcast.100), kind=kOutput, calls=%fused_computation.32 | convolution fusion | flops 1077936128 | bytes 10747904 | tf_op jit(solution)/shard_map/pjrd,ed->jpre/dot_general | solution.py:82
  113.2 8.6 %copy.31 = bf16[8,8,64,1024]{3,2,1,0:T(8,128)(2,1)} copy(bf16[8,8,64,1024]{3,2,0,1:T(8,128)(2,1)} %convert_bitcast_fusion) | data formatting | bytes 16777216 | tf_op jit(solution)/shard_map/convert_element_type | solution.py:84
  121.7 0.0 copy-start.1
  121.7 0.0 copy-start.2
  121.7 5.3 %all-to-all-start.2 = ((bf16[8,8,64,1024]{3,2,1,0:T(8,128)(2,1)}), bf16[8,8,64,1024]{3,2,1,0:T(8,128)(2,1)}, u32[]{:S(2)}, u32[]{:S(2)}) async-start(bf16[8,8,64,1024]{3,2,1,0:T(8,128)(2,1)} %copy.31), calls=%async_computation.2 | async-start | bytes 16777216 | tf_op jit(solution)/shard_map/all_to_all | solution.py:85
  127.0 0.1 constant_dynamic-slice_fusion
  127.1 0.0 copy-done.1
  127.1 0.0 copy-done.2
  127.1 1.5 bitcast_select_fusion
  128.6 2.3 copy.34
  130.9 2.3 copy.35
  133.1 109.2 %all-to-all-done.2 = bf16[8,8,64,1024]{3,2,1,0:T(8,128)(2,1)} async-done(((bf16[8,8,64,1024]{3,2,1,0:T(8,128)(2,1)}), bf16[8,8,64,1024]{3,2,1,0:T(8,128)(2,1)}, u32[]{:S(2)}, u32[]{:S(2)}) %all-to-all-start.2) | async-done | bytes 8388640 | tf_op jit(solution)/shard_map/all_to_all | solution.py:85
  242.3 5.7 %convert_reduce_fusion.1 = f32[8,64,1024]{2,1,0:T(8,128)S(1)} fusion(bf16[8,8,64,1024]{3,2,1,0:T(8,128)(2,1)} %all-to-all-done.2), kind=kLoop, calls=%fused_computation.3 | loop fusion | flops 7864320 | bytes 10485760 | tf_op jit(solution)/shard_map/reduce_sum | solution.py:86
  248.0 1.5 fusion.35
  249.6 1.7 multiply_reduce_fusion.1
  251.3 1.8 add_convert_fusion
  253.1 0.0 all-gather.5.cloned.1.call-done
  253.1 23.8 %fusion.4 = bf16[8,64,4096]{2,1,0:T(8,128)(2,1)S(1)} fusion(bf16[8,64,1024]{2,1,0:T(8,128)(2,1)S(1)} %add_convert_fusion, bf16[1024,4096]{1,0:T(8,128)(2,1)} %all-gather.5.cloned.1.call-done), kind=kOutput, calls=%fused_computation.11 | convolution fusion | flops 4431282176 | bytes 13631488 | tf_op jit(solution)/shard_map/pld,df->plf/dot_general | solution.py:92
  276.9 2.5 copy.53
  279.5 0.0 all-gather.3.cloned.1.call-done
  279.5 9.2 %convert_reduce_fusion = f32[1024,8,64]{0,2,1:T(8,128)S(1)} fusion(bf16[8,512,512]{1,2,0:T(8,128)(2,1)} %bitcast.97, bf16[128,8,8,512]{3,2,1,0:T(8,128)(2,1)} %bitcast.109), kind=kOutput, calls=%fused_computation.2 | convolution fusion | flops 4307025920 | bytes 14680064
  288.7 0.3 fusion.34
  289.0 0.4 multiply_reduce_fusion
  289.4 3.1 %select_convert_fusion = bf16[8,64,1024]{2,1,0:T(8,128)(2,1)} fusion(f32[1024]{0:T(1024)S(1)} %bitcast.106, f32[1024]{0:T(1024)S(1)} %bitcast.105, f32[8,64]{1,0:T(8,128)S(1)} %add_rsqrt_fusion, f32[8,64]{1,0:T(8,128)S(1)} %broadcast_multiply_fusion, pred[8,64]{1,0:T(8,128)(4,1)S(1)} %constant_dynamic-slice_fusion, ...), kind=kLoop, calls=%fused_computation.43 | loop fusion | flops 4194304 | bytes 4207104 | tf_op jit(solution)/shard_map/convert_element_type | solution.py:103
  (8 shorter events, 0.1 us)
Async XLA Ops:
  7.2 37.7 %copy-start.3 = (s32[8]{0:T(128)S(1)}, s32[8]{0:T(128)}, u32[]{:S(2)}) copy-start(s32[8]{0:T(128)} %param.9) | copy-start | bytes 100
  7.2 245.9 %all-gather.5.cloned.1.call-start = ((), (), s32[]{:S(2)}) async-start(), calls=%async_computation.4 | async-start | bytes 8912896 | tf_op jit(solution)/shard_map/all_gather | solution.py:41
  37.2 34.9 %all-to-all-start.1 = ((bf16[16,64,512]{2,1,0:T(8,128)(2,1)}), bf16[16,64,512]{2,1,0:T(8,128)(2,1)S(1)}, u32[]{:S(2)}, u32[]{:S(2)}) async-start(bf16[16,64,512]{2,1,0:T(8,128)(2,1)} %broadcast_in_dim.37), calls=%async_computation.1 | async-start | bytes 2097152 | tf_op jit(solution)/shard_map/all_to_all | solution.py:37
  44.8 234.7 %all-gather.3.cloned.1.call-start = ((), (), s32[]{:S(2)}) async-start(), calls=%async_computation.3 | async-start | bytes 8912896 | tf_op jit(solution)/shard_map/all_gather | solution.py:43
  72.1 1.3 copy-start
  121.7 5.4 %copy-start.1 = (f32[2,1024]{1,0:T(2,128)S(1)}, f32[2,1024]{1,0:T(2,128)}, u32[]{:S(2)}) copy-start(f32[2,1024]{1,0:T(2,128)} %param.14) | copy-start | bytes 24580
  121.7 5.4 %copy-start.2 = (f32[2,1024]{1,0:T(2,128)S(1)}, f32[2,1024]{1,0:T(2,128)}, u32[]{:S(2)}) copy-start(f32[2,1024]{1,0:T(2,128)} %param.15) | copy-start | bytes 24580
  121.7 120.6 %all-to-all-start.2 = ((bf16[8,8,64,1024]{3,2,1,0:T(8,128)(2,1)}), bf16[8,8,64,1024]{3,2,1,0:T(8,128)(2,1)}, u32[]{:S(2)}, u32[]{:S(2)}) async-start(bf16[8,8,64,1024]{3,2,1,0:T(8,128)(2,1)} %copy.31), calls=%async_computation.2 | async-start | bytes 16777216 | tf_op jit(solution)/shard_map/all_to_all | solution.py:85
Sparse Core Ops, SparseCore 0:
  36.3 63.4 all-gather.4
  101.5 139.7 all-gather.2
where the time goes:
time: 300 us; the launch traced here: 299 us
  waiting for transfers between devices  136 us (45%)
  matrix products  67.2 us (22%)
  local copies, waits for them, and re-layouts  24.9 us (8%)
  blocking collectives  24.1 us (8%)
  other arithmetic  19.6 us (7%)
  between operations  14.2 us (5%)
  starting transfers between devices  12.9 us (4%)
    all_to_all x1, waiting for transfers between devices, encode_chunk(): attn_blocks = lax.all_to_all(attn_partial, 'head', 0, 0, tiled=True)  109 us
    all_to_all x1, waiting for transfers between devices, regroup_weights(): attn_whole = lax.all_to_all(attn_part, 'seq', 0, 0, tiled=True)  26.6 us
    all_to_all x1, blocking collectives, regroup_weights(): packed = lax.all_to_all(packed, 'head', 1, 0, tiled=True)  24.1 us
    dot_general x1, matrix products, encode_chunk(): jnp.einsum('pld,df->plf', normed_rows, up_weight, preferred_element_type=...  23.8 us
    sub x1, matrix products, encode_chunk(): raised = jnp.exp(scores - row_peak)  10.7 us
    unnamed x1, matrix products  9.22 us
    dot_general x1, matrix products, encode_chunk(): jnp.einsum('phqk,pkhd->pqhd', weights, value_heads, preferred_element_typ...  8.85 us
    convert_element_type x1, local copies, waits for them, and re-layouts, encode_chunk(): attn_partial = jnp.einsum('pjrd,ed->jpre', context, proj_weight_t, prefer...  8.57 us
  transfers between devices with their start and end apart: 4, of which 2 were waited for; matrix products, arithmetic and copies ran while one was open for 31% of the time, Pallas kernels for 0%

commit v1 on v0

--- a/solution.py
+++ b/solution.py
@@ -25,23 +25,23 @@
     block_width = model_width // heads_axis
     in_piece = attn_in.astype(jnp.bfloat16).reshape(rows, 3, heads_axis, block_width)
     in_piece = jnp.transpose(in_piece, (0, 2, 1, 3)).reshape(rows, heads_axis, 3 * block_width)
-    out_piece = attn_out.astype(jnp.bfloat16).T.reshape(rows, heads_axis, block_width)
-    mlp_rows = jnp.concatenate(
-        [mlp_in.astype(jnp.bfloat16), mlp_out.astype(jnp.bfloat16).T], axis=1)
-    mlp_piece = jnp.broadcast_to(mlp_rows[:, None], (rows, heads_axis, 2 * hidden_width))
-    packed = jnp.concatenate([in_piece, out_piece, mlp_piece], axis=2)
+    whole_rows = jnp.concatenate(
+        [attn_out.astype(jnp.bfloat16).T, mlp_in.astype(jnp.bfloat16),
+         mlp_out.astype(jnp.bfloat16).T], axis=1)
+    whole_piece = jnp.broadcast_to(whole_rows[:, None], (rows, heads_axis, whole_rows.shape[1]))
+    packed = jnp.concatenate([in_piece, whole_piece], axis=2)
     packed = lax.all_to_all(packed, "head", 1, 0, tiled=True)
     packed = packed.reshape(rows * heads_axis, packed.shape[2])
-    attn_part = packed[:, :4 * block_width]
-    attn_part = jnp.broadcast_to(attn_part[None], (seq_axis,) + attn_part.shape)
-    attn_whole = lax.all_to_all(attn_part, "seq", 0, 0, tiled=True)
-    attn_whole = attn_whole.reshape(-1, 4 * block_width)
-    qkv_weight = attn_whole[:, :3 * block_width].reshape(-1, 3, block_width)
-    proj_weight_t = attn_whole[:, 3 * block_width:]
-    up_weight = lax.all_gather(
-        packed[:, 4 * block_width:4 * block_width + hidden_width], "seq", axis=0, tiled=True)
-    down_weight_t = lax.all_gather(
-        packed[:, 4 * block_width + hidden_width:], "seq", axis=0, tiled=True)
+    in_part = packed[:, :3 * block_width]
+    in_part = jnp.broadcast_to(in_part[None], (seq_axis,) + in_part.shape)
+    qkv_weight = lax.all_to_all(in_part, "seq", 0, 0, tiled=True)
+    qkv_weight = qkv_weight.reshape(-1, 3, block_width)
+    edges = [3 * block_width, 3 * block_width + model_width,
+             3 * block_width + model_width + hidden_width,
+             3 * block_width + model_width + 2 * hidden_width]
+    proj_weight_t, up_weight, down_weight_t = [
+        lax.all_gather(packed[:, lower:upper], "seq", axis=0, tiled=True)
+        for lower, upper in zip(edges[:-1], edges[1:])]
     return qkv_weight, proj_weight_t, up_weight, down_weight_t
 
 
@@ -79,10 +79,12 @@
     context = context.astype(jnp.bfloat16).reshape(prompts, heads_axis, row_count, block_width)
     key_cache = jnp.where(inside[:, :, None], key_part, jnp.zeros_like(key_part))
     value_cache = jnp.where(inside[:, :, None], value_part, jnp.zeros_like(value_part))
-    attn_partial = jnp.einsum(
-        "pjrd,ed->jpre", context, proj_weight_t, preferred_element_type=jnp.float32
+    context_blocks = jnp.transpose(context, (1, 0, 2, 3))
+    context_blocks = lax.all_to_all(context_blocks, "head", 0, 0, tiled=True)
+    proj_blocks = proj_weight_t.reshape(model_width, heads_axis, block_width)
+    attn_blocks = jnp.einsum(
+        "sprf,esf->spre", context_blocks, proj_blocks, preferred_element_type=jnp.float32
     ).astype(jnp.bfloat16)
-    attn_blocks = lax.all_to_all(attn_partial, "head", 0, 0, tiled=True)
     attn_rows = jnp.sum(attn_blocks.astype(jnp.float32), axis=0)
     token_rows = lax.dynamic_slice_in_dim(tokens, row_start, row_count, 1)
     normed_rows = layer_norm(

time: 300 us -> 217 us (0.72)
  waiting for transfers between devices: 136 us -> 63.8 us
  other arithmetic: 19.6 us -> 14 us
  matrix products: 67.2 us -> 63.8 us
    all_to_all x2, waiting for transfers between devices: 136 us -> 25.5 us  [the longest x1 16.7 us: regroup_weights(): qkv_weight = lax.all_to_all(in_part, 'seq', 0, 0, tiled=True)]
    all_gather x2 -> x3, waiting for transfers between devices: 0.02 us -> 37.7 us  [regroup_weights(): lax.all_gather(packed[:, lower:upper], 'seq', axis=0, tiled=True)]
    convert_element_type x1 -> x0, local copies, waits for them, and re-layouts: 8.57 us -> none  [encode_chunk(): attn_partial = jnp.einsum('pjrd,ed->jpre', context, proj_weight_t, prefer...]
    reduce_sum x1 -> x0, other arithmetic: 5.69 us -> none  [encode_chunk(): attn_rows = jnp.sum(attn_blocks.astype(jnp.float32), axis=0)]
    dot_general x1, matrix products: 7.29 us -> 3.68 us  [encode_chunk(): jnp.einsum('sprf,esf->spre', context_blocks, proj_blocks, preferred_eleme...]
    reshape x1 -> x2, local copies, waits for them, and re-layouts: 3.88 us -> 7.36 us  [encode_chunk(): context.astype(jnp.bfloat16)]
  transfers between devices with their start and end apart: 4 -> 5, of which waited for: 2 -> 4; matrix products, arithmetic and copies ran while one was open for 31% -> 39% of each run, Pallas kernels for 0% -> 0%
where the time goes in v1:
time: 217 us; the launch traced here: 216 us
  waiting for transfers between devices  63.8 us (29%)
  matrix products  63.8 us (29%)
  blocking collectives  24.8 us (11%)
  local copies, waits for them, and re-layouts  23.1 us (11%)
  other arithmetic  14 us (6%)
  between operations  13.9 us (6%)
  starting transfers between devices  12.3 us (6%)
    all_gather x3, waiting for transfers between devices, regroup_weights(): lax.all_gather(packed[:, lower:upper], 'seq', axis=0, tiled=True)  37.7 us
    all_to_all x1, blocking collectives, regroup_weights(): packed = lax.all_to_all(packed, 'head', 1, 0, tiled=True)  24.8 us
    dot_general x1, matrix products, encode_chunk(): jnp.einsum('pld,df->plf', normed_rows, up_weight, preferred_element_type=...  23.8 us
    all_to_all x1, waiting for transfers between devices, regroup_weights(): qkv_weight = lax.all_to_all(in_part, 'seq', 0, 0, tiled=True)  16.7 us
    sub x1, matrix products, encode_chunk(): raised = jnp.exp(scores - row_peak)  10.7 us
    unnamed x1, matrix products  9.22 us
    dot_general x1, matrix products, encode_chunk(): jnp.einsum('phqk,pkhd->pqhd', weights, value_heads, preferred_element_typ...  9.02 us
    all_to_all x1, waiting for transfers between devices, encode_chunk(): context_blocks = lax.all_to_all(context_blocks, 'head', 0, 0, tiled=True)  8.79 us
  transfers between devices with their start and end apart: 5, of which 4 were waited for; matrix products, arithmetic and copies ran while one was open for 39% of the time, Pallas kernels for 0%

profile of v1, /device:TPU:1, one launch (start us, length us, event | category | flops | bytes accessed | tf_op | source)
XLA Modules:
  0.0 215.7 jit_solution(6838226630606293750)
XLA Ops:
  7.2 0.0 copy-start.2
  7.2 0.0 all-gather.4.cloned.1.call-start
  7.2 0.9 convert_bitcast_fusion.1
  8.1 0.9 convert_element_type.59
  9.0 0.8 convert_bitcast_fusion.3
  9.8 0.9 copy_bitcast_fusion.1
  10.7 0.1 broadcast_in_dim.36
  10.8 0.1 pad_maximum_fusion
  10.9 24.8 %all_to_all.25 = bf16[8,8,9600]{2,0,1:T(8,128)(2,1)S(1)} all-to-all(bf16[8,8,9600]{2,0,1:T(8,128)(2,1)S(1)} %pad_maximum_fusion), channel_id=1, replica_groups=mesh['seq'=16,'head'=8] {'head'}, dimensions={1} | all-to-all | bytes 2457600 | tf_op jit(solution)/shard_map/all_to_all | solution.py:33
  35.7 0.6 slice.48
  36.4 0.0 all-gather.4.cloned.1.call-update
  36.4 0.0 all-gather.8.cloned.1.call-start
  36.4 1.1 fusion.39
  37.6 0.0 all-gather.8.cloned.1.call-update
  37.6 0.0 all-gather.6.cloned.1.call-start
  37.6 0.7 all-gather.6.cloned.1.call-update
  38.3 1.0 broadcast_in_dim.37
  39.3 7.7 %all-to-all-start.1 = ((bf16[16,64,384]{2,1,0:T(8,128)(2,1)}), bf16[16,64,384]{2,1,0:T(8,128)(2,1)S(1)}, u32[]{:S(2)}, u32[]{:S(2)}) async-start(bf16[16,64,384]{2,1,0:T(8,128)(2,1)} %broadcast_in_dim.37), calls=%async_computation.1 | async-start | bytes 1572864 | tf_op jit(solution)/shard_map/all_to_all | solution.py:37
  47.1 0.0 copy-done.2
  47.1 0.1 iota_compare_fusion
  47.1 16.7 %all-to-all-done.1 = bf16[16,64,384]{2,1,0:T(8,128)(2,1)S(1)} async-done(((bf16[16,64,384]{2,1,0:T(8,128)(2,1)}), bf16[16,64,384]{2,1,0:T(8,128)(2,1)S(1)}, u32[]{:S(2)}, u32[]{:S(2)}) %all-to-all-start.1) | async-done | bytes 786464 | tf_op jit(solution)/shard_map/all_to_all | solution.py:37
  63.8 1.1 reshape.102
  64.9 7.3 %convert_bitcast_fusion = bf16[8,512,3,128]{1,3,0,2:T(8,128)(2,1)S(1)} fusion(bf16[8,512,1024]{2,1,0:T(8,128)(2,1)} %param.8, bf16[1024,3,128,1]{2,1,0,3:T(4,128)(2,1)} %bitcast.95), kind=kOutput, calls=%fused_computation.39 | convolution fusion | flops 3222798336 | bytes 12320768 | tf_op jit(solution)/shard_map/pld,dte->plte/dot_general | solution.py:59
  72.2 1.8 fusion.38
  74.0 10.7 %fusion.42 = (f32[8,2,512]{2,1,0:T(2,128)S(1)}, f32[8,2,512,512]{2,3,1,0:T(8,128)}) fusion(pred[8,512]{1,0:T(8,128)(4,1)S(1)} %iota_compare_fusion, bf16[8,512,2,64]{1,3,2,0:T(8,128)(2,1)} %bitcast.98, bf16[8,512,2,64]{1,3,2,0:T(8,128)(2,1)} %bitcast.97), kind=kOutput, calls=%fused_computation.72 | convolution fusion | flops 553648640 | bytes 18911232 | tf_op jit(solution)/shard_map/sub | solution.py:74
  84.7 9.0 %fusion.32 = bf16[8,512,2,64]{1,3,2,0:T(8,128)(2,1)} fusion(bf16[8,512,2,64]{1,3,2,0:T(8,128)(2,1)} %bitcast.96, f32[8,2,512,512]{2,3,1,0:T(8,128)} %get-tuple-element.21, f32[8,2,512]{2,1,0:T(2,128)S(1)} %get-tuple-element.20), kind=kOutput, calls=%fused_computation.48 | convolution fusion | flops 545783808 | bytes 18907136 | tf_op jit(solution)/shard_map/phqk,pkhd->pqhd/dot_general | solution.py:76
  93.7 0.0 copy-start
  93.7 0.0 copy-start.1
  93.7 4.0 %reshape.103 = bf16[8,8,64,128]{2,1,3,0:T(8,128)(2,1)} reshape(bf16[8,512,2,64]{1,3,2,0:T(8,128)(2,1)} %fusion.32) | data formatting | bytes 2097152 | tf_op jit(solution)/shard_map/reshape | solution.py:79
  97.7 3.4 %copy.22 = bf16[8,8,64,128]{3,2,0,1:T(8,128)(2,1)} copy(bf16[8,8,64,128]{2,1,3,0:T(8,128)(2,1)} %reshape.103) | data formatting | bytes 2097152 | tf_op jit(solution)/shard_map/reshape | solution.py:79
  101.1 4.4 %all-to-all-start.2 = ((bf16[8,8,64,128]{3,2,1,0:T(8,128)(2,1)}), bf16[8,8,64,128]{3,2,1,0:T(8,128)(2,1)}, u32[]{:S(2)}, u32[]{:S(2)}) async-start(bf16[8,8,64,128]{3,2,1,0:T(8,128)(2,1)} %bitcast.91), calls=%async_computation.2 | async-start | bytes 2097152 | tf_op jit(solution)/shard_map/all_to_all | solution.py:83
  105.5 0.1 constant_dynamic-slice_fusion
  105.6 0.0 copy-done
  105.6 0.0 copy-done.1
  105.6 1.5 bitcast_select_fusion
  107.1 2.3 %copy.27 = bf16[8,512,128]{2,1,0:T(8,128)(2,1)} copy(bf16[8,512,128]{1,2,0:T(8,128)(2,1)} %get-tuple-element.10) | data formatting | bytes 2097152
  109.3 2.3 %copy.28 = bf16[8,512,128]{2,1,0:T(8,128)(2,1)} copy(bf16[8,512,128]{1,2,0:T(8,128)(2,1)} %get-tuple-element.9) | data formatting | bytes 2097152
  111.6 0.0 all-gather.4.cloned.1.call-done
  111.6 2.9 %copy.23 = bf16[1024,1024]{0,1:T(8,128)(2,1)S(1)} copy(bf16[1024,1024]{1,0:T(8,128)(2,1)} %all-gather.4.cloned.1.call-done) | data formatting | bytes 4194304 | tf_op jit(solution)/shard_map/all_gather | solution.py:43
  114.5 8.8 %all-to-all-done.2 = bf16[8,8,64,128]{3,2,1,0:T(8,128)(2,1)} async-done(((bf16[8,8,64,128]{3,2,1,0:T(8,128)(2,1)}), bf16[8,8,64,128]{3,2,1,0:T(8,128)(2,1)}, u32[]{:S(2)}, u32[]{:S(2)}) %all-to-all-start.2) | async-done | bytes 1048608 | tf_op jit(solution)/shard_map/all_to_all | solution.py:83
  123.3 3.7 %convert_reduce_fusion.1 = f32[8,64,1024]{2,1,0:T(8,128)S(1)} fusion(bf16[8,8,64,128]{3,2,1,0:T(8,128)(2,1)} %all-to-all-done.2, bf16[1024,8,128,1]{0,2,3,1:T(8,128)(2,1)S(1)} %bitcast.94), kind=kOutput, calls=%fused_computation.3 | convolution fusion | flops 1085800448 | bytes 5242880 | tf_op jit(solution)/shard_map/sprf,esf->spre/dot_general | solution.py:85
  127.0 1.6 fusion.35
  128.6 1.7 multiply_reduce_fusion.1
  130.3 1.8 add_convert_fusion
  132.1 9.2 %all-gather.8.cloned.1.call-done = bf16[1024,4096]{1,0:T(8,128)(2,1)} async-done(((bf16[64,4096]{1,0:T(8,128)(2,1)}), bf16[1024,4096]{1,0:T(8,128)(2,1)}) %all-gather.8.cloned.1.call-update) | async-done | bytes 8388624 | tf_op jit(solution)/shard_map/all_gather | solution.py:43
  141.4 23.8 %fusion.4 = bf16[8,64,4096]{2,1,0:T(8,128)(2,1)S(1)} fusion(bf16[8,64,1024]{2,1,0:T(8,128)(2,1)S(1)} %add_convert_fusion, bf16[1024,4096]{1,0:T(8,128)(2,1)} %all-gather.8.cloned.1.call-done), kind=kOutput, calls=%fused_computation.11 | convolution fusion | flops 4431282176 | bytes 13631488 | tf_op jit(solution)/shard_map/pld,df->plf/dot_general | solution.py:94
  165.2 2.5 %copy.50 = bf16[8,8,8,8,512]{4,3,1,0,2:T(8,128)(2,1)} copy(bf16[8,8,8,8,512]{4,3,2,1,0:T(8,128)(2,1)S(1)} %bitcast.93) | data formatting | bytes 8388608 | tf_op jit(solution)/shard_map/reshape | solution.py:97
  167.7 28.4 %all-gather.6.cloned.1.call-done = bf16[1024,4096]{1,0:T(8,128)(2,1)} async-done(((bf16[64,4096]{1,0:T(8,128)(2,1)}), bf16[1024,4096]{1,0:T(8,128)(2,1)}) %all-gather.6.cloned.1.call-update) | async-done | bytes 8388624 | tf_op jit(solution)/shard_map/all_gather | solution.py:43
  196.1 9.2 %convert_reduce_fusion = f32[1024,8,64]{0,2,1:T(8,128)S(1)} fusion(bf16[8,512,512]{1,2,0:T(8,128)(2,1)} %bitcast.92, bf16[128,8,8,512]{3,2,1,0:T(8,128)(2,1)} %bitcast.103), kind=kOutput, calls=%fused_computation.2 | convolution fusion | flops 4307025920 | bytes 14680064
  205.4 0.3 fusion.33
  205.7 0.4 multiply_reduce_fusion
  206.1 3.1 %select_convert_fusion = bf16[8,64,1024]{2,1,0:T(8,128)(2,1)} fusion(f32[1024]{0:T(1024)S(1)} %bitcast.100, f32[1024]{0:T(1024)S(1)} %bitcast.99, f32[8,64]{1,0:T(8,128)S(1)} %add_rsqrt_fusion, f32[8,64]{1,0:T(8,128)S(1)} %broadcast_multiply_fusion, pred[8,64]{1,0:T(8,128)(4,1)S(1)} %constant_dynamic-slice_fusion, f32[1024,8,64]{0,2,1:T(8,128)S(1)} %convert_reduce_fusion, ...), kind=kLoop, calls=%fused_computation.41 | loop fusion | flops 4194304 | bytes 4207104 | tf_op jit(solution)/shard_map/convert_element_type | solution.py:105
  (8 shorter events, 0.1 us)
Async XLA Ops:
  7.2 39.9 %copy-start.2 = (s32[8]{0:T(128)S(1)}, s32[8]{0:T(128)}, u32[]{:S(2)}) copy-start(s32[8]{0:T(128)} %param.9) | copy-start | bytes 100
  7.2 104.4 %all-gather.4.cloned.1.call-start = ((), (), s32[]{:S(2)}) async-start(), calls=%async_computation.3 | async-start | bytes 2228224 | tf_op jit(solution)/shard_map/all_gather | solution.py:43
  36.4 105.0 %all-gather.8.cloned.1.call-start = ((), (), s32[]{:S(2)}) async-start(), calls=%async_computation.5 | async-start | bytes 8912896 | tf_op jit(solution)/shard_map/all_gather | solution.py:43
  37.6 158.5 %all-gather.6.cloned.1.call-start = ((), (), s32[]{:S(2)}) async-start(), calls=%async_computation.4 | async-start | bytes 8912896 | tf_op jit(solution)/shard_map/all_gather | solution.py:43
  39.3 24.5 %all-to-all-start.1 = ((bf16[16,64,384]{2,1,0:T(8,128)(2,1)}), bf16[16,64,384]{2,1,0:T(8,128)(2,1)S(1)}, u32[]{:S(2)}, u32[]{:S(2)}) async-start(bf16[16,64,384]{2,1,0:T(8,128)(2,1)} %broadcast_in_dim.37), calls=%async_computation.1 | async-start | bytes 1572864 | tf_op jit(solution)/shard_map/all_to_all | solution.py:37
  93.7 11.9 %copy-start = (f32[2,1024]{1,0:T(2,128)S(1)}, f32[2,1024]{1,0:T(2,128)}, u32[]{:S(2)}) copy-start(f32[2,1024]{1,0:T(2,128)} %param.14) | copy-start | bytes 24580
  93.7 11.9 %copy-start.1 = (f32[2,1024]{1,0:T(2,128)S(1)}, f32[2,1024]{1,0:T(2,128)}, u32[]{:S(2)}) copy-start(f32[2,1024]{1,0:T(2,128)} %param.15) | copy-start | bytes 24580
  101.1 22.2 %all-to-all-start.2 = ((bf16[8,8,64,128]{3,2,1,0:T(8,128)(2,1)}), bf16[8,8,64,128]{3,2,1,0:T(8,128)(2,1)}, u32[]{:S(2)}, u32[]{:S(2)}) async-start(bf16[8,8,64,128]{3,2,1,0:T(8,128)(2,1)} %bitcast.91), calls=%async_computation.2 | async-start | bytes 2097152 | tf_op jit(solution)/shard_map/all_to_all | solution.py:83
Sparse Core Ops, SparseCore 0:
  36.5 40.5 all-gather.3
  78.8 62.4 all-gather.7
  143.1 53.0 all-gather.5

commit v2 on v1

--- a/solution.py
+++ b/solution.py
@@ -32,16 +32,16 @@
     packed = jnp.concatenate([in_piece, whole_piece], axis=2)
     packed = lax.all_to_all(packed, "head", 1, 0, tiled=True)
     packed = packed.reshape(rows * heads_axis, packed.shape[2])
-    in_part = packed[:, :3 * block_width]
-    in_part = jnp.broadcast_to(in_part[None], (seq_axis,) + in_part.shape)
-    qkv_weight = lax.all_to_all(in_part, "seq", 0, 0, tiled=True)
-    qkv_weight = qkv_weight.reshape(-1, 3, block_width)
-    edges = [3 * block_width, 3 * block_width + model_width,
-             3 * block_width + model_width + hidden_width,
-             3 * block_width + model_width + 2 * hidden_width]
-    proj_weight_t, up_weight, down_weight_t = [
-        lax.all_gather(packed[:, lower:upper], "seq", axis=0, tiled=True)
-        for lower, upper in zip(edges[:-1], edges[1:])]
+    attn_width = 3 * block_width + model_width
+    attn_part = packed[:, :attn_width]
+    attn_part = jnp.broadcast_to(attn_part[None], (seq_axis,) + attn_part.shape)
+    attn_whole = lax.all_to_all(attn_part, "seq", 0, 0, tiled=True)
+    attn_whole = attn_whole.reshape(-1, attn_width)
+    qkv_weight = attn_whole[:, :3 * block_width].reshape(-1, 3, block_width)
+    proj_weight_t = attn_whole[:, 3 * block_width:]
+    up_weight, down_weight_t = [
+        lax.all_gather(packed[:, lower:lower + hidden_width], "seq", axis=0, tiled=True)
+        for lower in (attn_width, attn_width + hidden_width)]
     return qkv_weight, proj_weight_t, up_weight, down_weight_t
 
 

time: 217 us -> 227 us (1.046)
  local copies, waits for them, and re-layouts: 23.1 us -> 27.9 us
  waiting for transfers between devices: 63.8 us -> 67.4 us
    all_to_all x1, waiting for transfers between devices: 16.7 us -> 61.2 us  [regroup_weights(): attn_whole = lax.all_to_all(attn_part, 'seq', 0, 0, tiled=True)]
    all_gather x3 -> x2, waiting for transfers between devices: 37.7 us -> 0.02 us  [regroup_weights(): lax.all_gather(packed[:, lower:lower + hidden_width], 'seq', axis=0, tile...]
    slice x3 -> x6, local copies, waits for them, and re-layouts: 1.77 us -> 9.98 us  [the longest x2 5.55 us: regroup_weights(): proj_weight_t = attn_whole[:, 3 * block_width:]]
    all_to_all x1, waiting for transfers between devices: 8.79 us -> 5.45 us  [encode_chunk(): context_blocks = lax.all_to_all(context_blocks, 'head', 0, 0, tiled=True)]
    all_gather x1 -> x0, local copies, waits for them, and re-layouts: 2.85 us -> none  [regroup_weights(): lax.all_gather(packed[:, lower:upper], 'seq', axis=0, tiled=True)]
  transfers between devices with their start and end apart: 5 -> 4, of which waited for: 4 -> 2; matrix products, arithmetic and copies ran while one was open for 39% -> 39% of each run, Pallas kernels for 0% -> 0%
where the time goes in v2:
time: 227 us; the launch traced here: 225 us
  waiting for transfers between devices  67.4 us (30%)
  matrix products  64.4 us (28%)
  local copies, waits for them, and re-layouts  27.9 us (12%)
  blocking collectives  24.8 us (11%)
  between operations  14.2 us (6%)
  other arithmetic  14.1 us (6%)
  starting transfers between devices  12.2 us (5%)
    all_to_all x1, waiting for transfers between devices, regroup_weights(): attn_whole = lax.all_to_all(attn_part, 'seq', 0, 0, tiled=True)  61.2 us
    all_to_all x1, blocking collectives, regroup_weights(): packed = lax.all_to_all(packed, 'head', 1, 0, tiled=True)  24.8 us
    dot_general x1, matrix products, encode_chunk(): jnp.einsum('pld,df->plf', normed_rows, up_weight, preferred_element_type=...  23.9 us
    sub x1, matrix products, encode_chunk(): raised = jnp.exp(scores - row_peak)  10.7 us
    unnamed x1, matrix products  9.22 us
    dot_general x1, matrix products, encode_chunk(): jnp.einsum('phqk,pkhd->pqhd', weights, value_heads, preferred_element_typ...  8.84 us
    all_to_all x1, starting transfers between devices, regroup_weights(): attn_whole = lax.all_to_all(attn_part, 'seq', 0, 0, tiled=True)  7.74 us
    reshape x2, local copies, waits for them, and re-layouts, encode_chunk(): context.astype(jnp.bfloat16)  7.31 us
  transfers between devices with their start and end apart: 4, of which 2 were waited for; matrix products, arithmetic and copies ran while one was open for 39% of the time, Pallas kernels for 0%

profile of v2, /device:TPU:1, one launch (start us, length us, event | category | flops | bytes accessed | tf_op | source)
XLA Modules:
  0.0 225.1 jit_solution(6334391488074036303)
XLA Ops:
  7.2 0.0 all-gather.5.cloned.1.call-start
  7.2 0.9 convert_bitcast_fusion.1
  8.1 0.9 convert_element_type.59
  9.0 0.8 convert_bitcast_fusion.3
  9.8 0.9 copy_bitcast_fusion.1
  10.7 0.1 broadcast_in_dim.36
  10.8 0.0 copy-start.3
  10.8 0.1 pad_maximum_fusion
  10.9 24.8 %all_to_all.25 = bf16[8,8,9600]{2,0,1:T(8,128)(2,1)S(1)} all-to-all(bf16[8,8,9600]{2,0,1:T(8,128)(2,1)S(1)} %pad_maximum_fusion), channel_id=1, replica_groups=mesh['seq'=16,'head'=8] {'head'}, dimensions={1} | all-to-all | bytes 2457600 | tf_op jit(solution)/shard_map/all_to_all | solution.py:33
  35.7 1.2 fusion.38
  36.9 0.0 all-gather.5.cloned.1.call-update
  36.9 0.0 all-gather.3.cloned.1.call-start
  37.0 0.7 all-gather.3.cloned.1.call-update
  37.7 1.9 broadcast_in_dim.37
  39.6 7.7 %all-to-all-start.1 = ((bf16[16,64,1408]{2,1,0:T(8,128)(2,1)}), bf16[16,64,1408]{2,1,0:T(8,128)(2,1)S(1)}, u32[]{:S(2)}, u32[]{:S(2)}) async-start(bf16[16,64,1408]{2,1,0:T(8,128)(2,1)} %broadcast_in_dim.37), calls=%async_computation.1 | async-start | bytes 5767168 | tf_op jit(solution)/shard_map/all_to_all | solution.py:38
  47.3 0.0 copy-done.3
  47.3 0.1 iota_compare_fusion
  47.4 61.2 %all-to-all-done.1 = bf16[16,64,1408]{2,1,0:T(8,128)(2,1)S(1)} async-done(((bf16[16,64,1408]{2,1,0:T(8,128)(2,1)}), bf16[16,64,1408]{2,1,0:T(8,128)(2,1)S(1)}, u32[]{:S(2)}, u32[]{:S(2)}) %all-to-all-start.1) | async-done | bytes 2883616 | tf_op jit(solution)/shard_map/all_to_all | solution.py:38
  108.6 1.0 slice.49
  109.5 2.3 %copy.20 = bf16[1024,384]{0,1:T(8,128)(2,1)} copy(bf16[1024,384]{1,0:T(8,128)(2,1)} %slice.49) | data formatting | bytes 1572864 | tf_op jit(solution)/shard_map/slice | solution.py:40
  111.8 7.3 %convert_bitcast_fusion = bf16[8,512,3,128]{1,3,0,2:T(8,128)(2,1)S(1)} fusion(bf16[1024,3,128,1]{0,2,3,1:T(8,128)(2,1)} %bitcast.105, bf16[8,512,1024]{2,1,0:T(8,128)(2,1)} %param.8), kind=kOutput, calls=%fused_computation.39 | convolution fusion | flops 3222798336 | bytes 12320768 | tf_op jit(solution)/shard_map/pld,dte->plte/dot_general | solution.py:59
  119.1 0.0 copy-start
  119.1 1.6 copy-done
  120.7 1.8 fusion.37
  122.5 10.7 %fusion.41 = (f32[8,2,512]{2,1,0:T(2,128)S(1)}, f32[8,2,512,512]{2,3,1,0:T(8,128)}) fusion(pred[8,512]{1,0:T(8,128)(4,1)S(1)} %iota_compare_fusion, bf16[8,512,2,64]{1,3,2,0:T(8,128)(2,1)} %bitcast.104, bf16[8,512,2,64]{1,3,2,0:T(8,128)(2,1)} %bitcast.103), kind=kOutput, calls=%fused_computation.71 | convolution fusion | flops 553648640 | bytes 18911232 | tf_op jit(solution)/shard_map/sub | solution.py:74
  133.2 8.8 %fusion.32 = bf16[8,512,2,64]{1,3,2,0:T(8,128)(2,1)} fusion(bf16[8,512,2,64]{1,3,2,0:T(8,128)(2,1)} %bitcast.102, f32[8,2,512,512]{2,3,1,0:T(8,128)} %get-tuple-element.21, f32[8,2,512]{2,1,0:T(2,128)S(1)} %get-tuple-element.20), kind=kOutput, calls=%fused_computation.48 | convolution fusion | flops 545783808 | bytes 18907136 | tf_op jit(solution)/shard_map/phqk,pkhd->pqhd/dot_general | solution.py:76
  142.1 0.0 copy-start.1
  142.1 0.0 copy-start.2
  142.1 4.0 %reshape.107 = bf16[8,8,64,128]{2,1,3,0:T(8,128)(2,1)} reshape(bf16[8,512,2,64]{1,3,2,0:T(8,128)(2,1)} %fusion.32) | data formatting | bytes 2097152 | tf_op jit(solution)/shard_map/reshape | solution.py:79
  146.0 3.4 %copy.22 = bf16[8,8,64,128]{3,2,0,1:T(8,128)(2,1)} copy(bf16[8,8,64,128]{2,1,3,0:T(8,128)(2,1)} %reshape.107) | data formatting | bytes 2097152 | tf_op jit(solution)/shard_map/reshape | solution.py:79
  149.4 4.4 %all-to-all-start.2 = ((bf16[8,8,64,128]{3,2,1,0:T(8,128)(2,1)}), bf16[8,8,64,128]{3,2,1,0:T(8,128)(2,1)}, u32[]{:S(2)}, u32[]{:S(2)}) async-start(bf16[8,8,64,128]{3,2,1,0:T(8,128)(2,1)} %bitcast.98), calls=%async_computation.2 | async-start | bytes 2097152 | tf_op jit(solution)/shard_map/all_to_all | solution.py:83
  153.8 0.1 constant_dynamic-slice_fusion
  153.9 0.0 copy-done.1
  153.9 0.0 copy-done.2
  153.9 1.6 slice.53
  155.5 4.0 %copy.23 = bf16[1024,1024]{0,1:T(8,128)(2,1)} copy(bf16[1024,1024]{1,0:T(8,128)(2,1)} %slice.53) | data formatting | bytes 4194304 | tf_op jit(solution)/shard_map/slice | solution.py:41
  159.5 1.7 bitcast_select_fusion
  161.2 1.3 copy.27
  162.5 1.3 copy.28
  163.8 5.5 %all-to-all-done.2 = bf16[8,8,64,128]{3,2,1,0:T(8,128)(2,1)} async-done(((bf16[8,8,64,128]{3,2,1,0:T(8,128)(2,1)}), bf16[8,8,64,128]{3,2,1,0:T(8,128)(2,1)}, u32[]{:S(2)}, u32[]{:S(2)}) %all-to-all-start.2) | async-done | bytes 1048608 | tf_op jit(solution)/shard_map/all_to_all | solution.py:83
  169.3 4.5 %convert_reduce_fusion.1 = f32[8,64,1024]{2,1,0:T(8,128)S(1)} fusion(bf16[8,8,64,128]{3,2,1,0:T(8,128)(2,1)} %all-to-all-done.2, bf16[1024,8,128,1]{0,2,3,1:T(8,128)(2,1)} %bitcast.101), kind=kOutput, calls=%fused_computation.3 | convolution fusion | flops 1085800448 | bytes 5242880 | tf_op jit(solution)/shard_map/sprf,esf->spre/dot_general | solution.py:85
  173.7 1.5 fusion.34
  175.3 1.7 multiply_reduce_fusion.1
  177.0 1.7 add_convert_fusion
  178.7 0.0 all-gather.5.cloned.1.call-done
  178.8 23.9 %fusion.4 = bf16[8,64,4096]{2,1,0:T(8,128)(2,1)S(1)} fusion(bf16[8,64,1024]{2,1,0:T(8,128)(2,1)S(1)} %add_convert_fusion, bf16[1024,4096]{1,0:T(8,128)(2,1)} %all-gather.5.cloned.1.call-done), kind=kOutput, calls=%fused_computation.11 | convolution fusion | flops 4431282176 | bytes 13631488 | tf_op jit(solution)/shard_map/pld,df->plf/dot_general | solution.py:94
  202.7 2.5 %copy.46 = bf16[8,8,8,8,512]{4,3,1,0,2:T(8,128)(2,1)} copy(bf16[8,8,8,8,512]{4,3,2,1,0:T(8,128)(2,1)S(1)} %bitcast.100) | data formatting | bytes 8388608 | tf_op jit(solution)/shard_map/reshape | solution.py:97
  205.2 0.0 all-gather.3.cloned.1.call-done
  205.2 9.2 %convert_reduce_fusion = f32[1024,8,64]{0,2,1:T(8,128)S(1)} fusion(bf16[8,512,512]{1,2,0:T(8,128)(2,1)} %bitcast.99, bf16[128,8,8,512]{3,2,1,0:T(8,128)(2,1)} %bitcast.110), kind=kOutput, calls=%fused_computation.2 | convolution fusion | flops 4307025920 | bytes 14680064
  214.4 0.3 fusion.33
  214.7 0.4 multiply_reduce_fusion
  215.2 3.1 %select_convert_fusion = bf16[8,64,1024]{2,1,0:T(8,128)(2,1)} fusion(f32[1024]{0:T(1024)S(1)} %bitcast.107, f32[1024]{0:T(1024)S(1)} %bitcast.106, f32[8,64]{1,0:T(8,128)S(1)} %add_rsqrt_fusion, f32[8,64]{1,0:T(8,128)S(1)} %broadcast_multiply_fusion, pred[8,64]{1,0:T(8,128)(4,1)S(1)} %constant_dynamic-slice_fusion, ...), kind=kLoop, calls=%fused_computation.41 | loop fusion | flops 4194304 | bytes 4207104 | tf_op jit(solution)/shard_map/convert_element_type | solution.py:105
  (8 shorter events, 0.1 us)
Async XLA Ops:
  7.2 171.6 %all-gather.5.cloned.1.call-start = ((), (), s32[]{:S(2)}) async-start(), calls=%async_computation.4 | async-start | bytes 8912896 | tf_op jit(solution)/shard_map/all_gather | solution.py:43
  10.8 36.5 %copy-start.3 = (s32[8]{0:T(128)S(1)}, s32[8]{0:T(128)}, u32[]{:S(2)}) copy-start(s32[8]{0:T(128)} %param.9) | copy-start | bytes 100
  36.9 168.3 %all-gather.3.cloned.1.call-start = ((), (), s32[]{:S(2)}) async-start(), calls=%async_computation.3 | async-start | bytes 8912896 | tf_op jit(solution)/shard_map/all_gather | solution.py:43
  39.6 69.0 %all-to-all-start.1 = ((bf16[16,64,1408]{2,1,0:T(8,128)(2,1)}), bf16[16,64,1408]{2,1,0:T(8,128)(2,1)S(1)}, u32[]{:S(2)}, u32[]{:S(2)}) async-start(bf16[16,64,1408]{2,1,0:T(8,128)(2,1)} %broadcast_in_dim.37), calls=%async_computation.1 | async-start | bytes 5767168 | tf_op jit(solution)/shard_map/all_to_all | solution.py:38
  119.1 1.6 copy-start
  142.1 11.8 %copy-start.1 = (f32[2,1024]{1,0:T(2,128)S(1)}, f32[2,1024]{1,0:T(2,128)}, u32[]{:S(2)}) copy-start(f32[2,1024]{1,0:T(2,128)} %param.14) | copy-start | bytes 24580
  142.1 11.8 %copy-start.2 = (f32[2,1024]{1,0:T(2,128)S(1)}, f32[2,1024]{1,0:T(2,128)}, u32[]{:S(2)}) copy-start(f32[2,1024]{1,0:T(2,128)} %param.15) | copy-start | bytes 24580
  149.4 19.9 %all-to-all-start.2 = ((bf16[8,8,64,128]{3,2,1,0:T(8,128)(2,1)}), bf16[8,8,64,128]{3,2,1,0:T(8,128)(2,1)}, u32[]{:S(2)}, u32[]{:S(2)}) async-start(bf16[8,8,64,128]{3,2,1,0:T(8,128)(2,1)} %bitcast.98), calls=%async_computation.2 | async-start | bytes 2097152 | tf_op jit(solution)/shard_map/all_to_all | solution.py:83
Sparse Core Ops, SparseCore 0:
  37.0 83.7 all-gather.4
  122.5 65.2 all-gather.2

commit v3 on v1

--- a/solution.py
+++ b/solution.py
@@ -25,9 +25,10 @@
     block_width = model_width // heads_axis
     in_piece = attn_in.astype(jnp.bfloat16).reshape(rows, 3, heads_axis, block_width)
     in_piece = jnp.transpose(in_piece, (0, 2, 1, 3)).reshape(rows, heads_axis, 3 * block_width)
+    down_rows = mlp_out.astype(jnp.bfloat16).T
+    half = hidden_width // 2
     whole_rows = jnp.concatenate(
-        [attn_out.astype(jnp.bfloat16).T, mlp_in.astype(jnp.bfloat16),
-         mlp_out.astype(jnp.bfloat16).T], axis=1)
+        [attn_out.astype(jnp.bfloat16).T, mlp_in.astype(jnp.bfloat16), down_rows[:, :half]], axis=1)
     whole_piece = jnp.broadcast_to(whole_rows[:, None], (rows, heads_axis, whole_rows.shape[1]))
     packed = jnp.concatenate([in_piece, whole_piece], axis=2)
     packed = lax.all_to_all(packed, "head", 1, 0, tiled=True)
@@ -38,11 +39,24 @@
     qkv_weight = qkv_weight.reshape(-1, 3, block_width)
     edges = [3 * block_width, 3 * block_width + model_width,
              3 * block_width + model_width + hidden_width,
-             3 * block_width + model_width + 2 * hidden_width]
-    proj_weight_t, up_weight, down_weight_t = [
+             3 * block_width + model_width + hidden_width + half]
+    proj_weight_t, up_weight = [
         lax.all_gather(packed[:, lower:upper], "seq", axis=0, tiled=True)
-        for lower, upper in zip(edges[:-1], edges[1:])]
-    return qkv_weight, proj_weight_t, up_weight, down_weight_t
+        for lower, upper in zip(edges[:-2], edges[1:-1])]
+    low_rows, up_weight = lax.optimization_barrier((packed[:, edges[2]:edges[3]], up_weight))
+    down_low = lax.all_gather(low_rows, "seq", axis=0, tiled=True)
+    down_high = lax.all_gather(down_rows[:, half:], "seq", axis=0, tiled=True)
+    return qkv_weight, proj_weight_t, up_weight, (down_low, down_high)
+
+
+def spread_down(down_low, down_high, heads_axis):
+    rows = down_high.shape[0]
+    down_high = jnp.broadcast_to(down_high[None], (heads_axis,) + down_high.shape)
+    down_high = lax.all_to_all(down_high, "head", 0, 0, tiled=True)
+    seq_axis = lax.axis_size("seq")
+    down_high = down_high.reshape(heads_axis, seq_axis, rows // seq_axis, -1)
+    down_high = jnp.transpose(down_high, (1, 0, 2, 3)).reshape(heads_axis * rows, -1)
+    return jnp.concatenate([down_low, down_high], axis=1)
 
 
 def encode_chunk(tokens, lengths, qkv_weight, proj_weight_t, up_weight, down_weight_t,
@@ -59,6 +73,8 @@
     projected = jnp.einsum(
         "pld,dte->plte", tokens, qkv_weight, preferred_element_type=jnp.float32
     ).astype(jnp.bfloat16)
+    down_high, projected = lax.optimization_barrier((down_weight_t[1], projected))
+    down_weight_t = spread_down(down_weight_t[0], down_high, heads_axis)
     positions = jnp.arange(seq_len, dtype=jnp.int32)
     inside = positions[None, :] < lengths[:, None]
     key_part = projected[:, :, 1]

time: 217 us -> 287 us (1.32)
  blocking collectives: 24.8 us -> 83.9 us
  local copies, waits for them, and re-layouts: 23.1 us -> 58.4 us
  waiting for transfers between devices: 63.8 us -> 40.5 us
    all_gather x0 -> x1, blocking collectives: none -> 40.8 us  [regroup_weights(): down_high = lax.all_gather(down_rows[:, half:], 'seq', axis=0, tiled=True)]
    all_gather x3 -> x2, waiting for transfers between devices: 37.7 us -> 0.01 us  [regroup_weights(): lax.all_gather(packed[:, lower:upper], 'seq', axis=0, tiled=True)]
    all_to_all x1, waiting for transfers between devices: 8.79 us -> 40.5 us  [spread_down(): down_high = lax.all_to_all(down_high, 'head', 0, 0, tiled=True)]
    all_to_all x0 -> x1, blocking collectives: none -> 21.1 us  [encode_chunk(): context_blocks = lax.all_to_all(context_blocks, 'head', 0, 0, tiled=True)]
    concatenate x0 -> x3, local copies, waits for them, and re-layouts: none -> 19.1 us  [spread_down(): return jnp.concatenate([down_low, down_high], axis=1)]
    all_to_all x1, waiting for transfers between devices: 16.7 us -> 0.01 us  [regroup_weights(): qkv_weight = lax.all_to_all(in_part, 'seq', 0, 0, tiled=True)]
    all_gather x0 -> x1, local copies, waits for them, and re-layouts: none -> 6.42 us  [regroup_weights(): down_low = lax.all_gather(low_rows, 'seq', axis=0, tiled=True)]
    transpose x0 -> x1, local copies, waits for them, and re-layouts: none -> 4.79 us  [spread_down(): jnp.transpose(down_high, (1, 0, 2, 3)).reshape(heads_axis * rows, -1)]
  transfers between devices with their start and end apart: 5 -> 5, of which waited for: 4 -> 1; matrix products, arithmetic and copies ran while one was open for 39% -> 37% of each run, Pallas kernels for 0% -> 0%
where the time goes in v3:
time: 287 us; the launch traced here: 285 us
  blocking collectives  83.9 us (29%)
  matrix products  61.3 us (21%)
  local copies, waits for them, and re-layouts  58.4 us (20%)
  waiting for transfers between devices  40.5 us (14%)
  other arithmetic  14 us (5%)
  between operations  14 us (5%)
  starting transfers between devices  12.6 us (4%)
    all_gather x1, blocking collectives, regroup_weights(): down_high = lax.all_gather(down_rows[:, half:], 'seq', axis=0, tiled=True)  40.8 us
    all_to_all x1, waiting for transfers between devices, spread_down(): down_high = lax.all_to_all(down_high, 'head', 0, 0, tiled=True)  40.5 us
    dot_general x1, matrix products, encode_chunk(): jnp.einsum('pld,df->plf', normed_rows, up_weight, preferred_element_type=...  23.6 us
    all_to_all x1, blocking collectives, regroup_weights(): packed = lax.all_to_all(packed, 'head', 1, 0, tiled=True)  22 us
    all_to_all x1, blocking collectives, encode_chunk(): context_blocks = lax.all_to_all(context_blocks, 'head', 0, 0, tiled=True)  21.1 us
    concatenate x3, local copies, waits for them, and re-layouts, spread_down(): return jnp.concatenate([down_low, down_high], axis=1)  19.1 us
    sub x1, matrix products, encode_chunk(): raised = jnp.exp(scores - row_peak)  10.7 us
    dot_general x1, matrix products, encode_chunk(): jnp.einsum('phqk,pkhd->pqhd', weights, value_heads, preferred_element_typ...  8.76 us
  transfers between devices with their start and end apart: 5, of which 1 were waited for; matrix products, arithmetic and copies ran while one was open for 37% of the time, Pallas kernels for 0%

profile of v3, /device:TPU:1, one launch (start us, length us, event | category | flops | bytes accessed | tf_op | source)
XLA Modules:
  0.0 284.7 jit_solution(11838374127737146019)
XLA Ops:
  7.2 0.0 copy-start.4
  7.2 0.0 all-gather.6.cloned.1.call-start
  7.2 0.9 convert_bitcast_fusion.1
  8.1 0.9 convert_element_type.60
  9.1 0.8 convert_bitcast_fusion.3
  9.8 0.9 convert_bitcast_fusion.2
  10.8 0.1 broadcast_in_dim.38
  10.8 0.1 pad_maximum_fusion
  10.9 22.0 %all_to_all.30 = bf16[8,8,7552]{2,0,1:T(8,128)(2,1)S(1)} all-to-all(bf16[8,8,7552]{2,0,1:T(8,128)(2,1)S(1)} %pad_maximum_fusion), channel_id=1, replica_groups=mesh['seq'=16,'head'=8] {'head'}, dimensions={1} | all-to-all | bytes 1933312 | tf_op jit(solution)/shard_map/all_to_all | solution.py:34
  32.9 0.0 copy-start
  32.9 0.9 slice.57
  33.8 0.0 all-gather.6.cloned.1.call-update
  33.8 1.0 broadcast_in_dim.39
  34.8 7.8 %all-to-all-start.1 = ((bf16[16,64,384]{2,1,0:T(8,128)(2,1)}), bf16[16,64,384]{2,1,0:T(8,128)(2,1)S(1)}, u32[]{:S(2)}, u32[]{:S(2)}) async-start(bf16[16,64,384]{2,1,0:T(8,128)(2,1)} %broadcast_in_dim.39), calls=%async_computation.1 | async-start | bytes 1572864 | tf_op jit(solution)/shard_map/all_to_all | solution.py:38
  42.6 0.0 all-gather.4.cloned.1.call-start
  42.6 0.0 copy-done.4
  42.6 0.1 iota_compare_fusion
  42.7 40.8 %all_gather.12 = bf16[128,2048]{1,0:T(8,128)(2,1)} all-gather(bf16[8,2048]{1,0:T(8,128)(2,1)S(1)} %get-tuple-element.26), channel_id=1, replica_groups=mesh['seq'=16,'head'=8] {'seq'}, dimensions={0}, use_global_device_ids=true | all-gather | bytes 557056 | tf_op jit(solution)/shard_map/all_gather | solution.py:48
  83.5 0.7 slice.55
  84.1 0.0 all-gather.4.cloned.1.call-update
  84.1 0.0 all-to-all-done.1
  84.2 1.1 reshape.108
  85.2 0.0 copy-done
  85.3 7.4 %convert_bitcast_fusion = bf16[8,512,3,128]{1,3,0,2:T(8,128)(2,1)S(1)} fusion(bf16[8,512,1024]{2,1,0:T(8,128)(2,1)} %param.8, bf16[1024,3,128,1]{2,1,0,3:T(4,128)(2,1)} %bitcast.102), kind=kOutput, calls=%fused_computation.40 | convolution fusion | flops 3222798336 | bytes 12320768 | tf_op jit(solution)/shard_map/pld,dte->plte/dot_general | solution.py:73
  92.6 1.8 fusion.40
  94.4 10.7 %fusion.44 = (f32[8,2,512]{2,1,0:T(2,128)S(1)}, f32[8,2,512,512]{2,3,1,0:T(8,128)}) fusion(pred[8,512]{1,0:T(8,128)(4,1)S(1)} %iota_compare_fusion, bf16[8,512,2,64]{1,3,2,0:T(8,128)(2,1)} %bitcast.105, bf16[8,512,2,64]{1,3,2,0:T(8,128)(2,1)} %bitcast.104), kind=kOutput, calls=%fused_computation.75 | convolution fusion | flops 553648640 | bytes 18911232 | tf_op jit(solution)/shard_map/sub | solution.py:90
  105.1 8.8 %fusion.33 = bf16[8,512,2,64]{1,3,2,0:T(8,128)(2,1)} fusion(bf16[8,512,2,64]{1,3,2,0:T(8,128)(2,1)} %bitcast.103, f32[8,2,512,512]{2,3,1,0:T(8,128)} %get-tuple-element.32, f32[8,2,512]{2,1,0:T(2,128)S(1)} %get-tuple-element.31), kind=kOutput, calls=%fused_computation.49 | convolution fusion | flops 545783808 | bytes 18907136 | tf_op jit(solution)/shard_map/phqk,pkhd->pqhd/dot_general | solution.py:92
  113.9 3.9 %reshape.109 = bf16[8,8,64,128]{2,1,3,0:T(8,128)(2,1)} reshape(bf16[8,512,2,64]{1,3,2,0:T(8,128)(2,1)} %fusion.33) | data formatting | bytes 2097152 | tf_op jit(solution)/shard_map/reshape | solution.py:95
  117.8 3.3 %copy.35 = bf16[8,8,64,128]{3,2,0,1:T(8,128)(2,1)} copy(bf16[8,8,64,128]{2,1,3,0:T(8,128)(2,1)} %reshape.109) | data formatting | bytes 2097152 | tf_op jit(solution)/shard_map/reshape | solution.py:95
  121.2 0.0 copy-start.2
  121.2 0.0 copy-start.3
  121.2 21.1 %all_to_all.31 = bf16[8,8,64,128]{3,2,1,0:T(8,128)(2,1)} all-to-all(bf16[8,8,64,128]{3,2,1,0:T(8,128)(2,1)} %bitcast.94), channel_id=1, replica_groups=mesh['seq'=16,'head'=8] {'head'}, dimensions={0} | all-to-all | bytes 2097152 | tf_op jit(solution)/shard_map/all_to_all | solution.py:99
  142.3 3.5 %broadcast_in_dim.70 = bf16[8,128,2048]{2,1,0:T(8,128)(2,1)} broadcast(bf16[128,2048]{1,0:T(8,128)(2,1)} %all_gather.12), dimensions={1,2} | broadcast | bytes 4718592 | tf_op jit(solution)/shard_map/broadcast_in_dim | solution.py:54
  145.8 4.5 %all-to-all-start.3 = ((bf16[8,128,2048]{2,1,0:T(8,128)(2,1)}), bf16[8,128,2048]{2,1,0:T(8,128)(2,1)}, u32[]{:S(2)}, u32[]{:S(2)}) async-start(bf16[8,128,2048]{2,1,0:T(8,128)(2,1)} %broadcast_in_dim.70), calls=%async_computation.3 | async-start | bytes 8388608 | tf_op jit(solution)/shard_map/all_to_all | solution.py:55
  150.4 0.2 all-gather.8.cloned.1.call-start
  150.6 0.1 constant_dynamic-slice_fusion
  150.7 1.7 slice.56
  152.4 0.0 all-gather.6.cloned.1.call-done
  152.4 0.0 all-gather.8.cloned.1.call-update
  152.4 0.0 copy-done.2
  152.4 0.0 copy-done.3
  152.4 1.5 bitcast_select_fusion
  153.9 0.0 copy-start.1
  153.9 2.3 copy.43
  156.3 2.3 copy.44
  158.5 0.0 all-gather.4.cloned.1.call-done
  158.5 2.9 %copy.36 = bf16[1024,1024]{0,1:T(8,128)(2,1)S(1)} copy(bf16[1024,1024]{1,0:T(8,128)(2,1)} %all-gather.4.cloned.1.call-done) | data formatting | bytes 4194304 | tf_op jit(solution)/shard_map/all_gather | solution.py:44
  161.4 0.0 copy-done.1
  161.4 2.3 convert_reduce_fusion.1
  163.7 1.5 fusion.36
  165.3 1.7 multiply_reduce_fusion.1
  167.0 1.7 add_convert_fusion
  168.7 40.5 %all-to-all-done.3 = bf16[8,128,2048]{2,1,0:T(8,128)(2,1)} async-done(((bf16[8,128,2048]{2,1,0:T(8,128)(2,1)}), bf16[8,128,2048]{2,1,0:T(8,128)(2,1)}, u32[]{:S(2)}, u32[]{:S(2)}) %all-to-all-start.3) | async-done | bytes 4194336 | tf_op jit(solution)/shard_map/all_to_all | solution.py:55
  209.2 4.8 %copy.39 = bf16[16,8,8,2048]{3,2,1,0:T(8,128)(2,1)} copy(bf16[16,8,8,2048]{3,2,0,1:T(8,128)(2,1)} %bitcast.23) | data formatting | bytes 8388608 | tf_op jit(solution)/shard_map/transpose | solution.py:58
  214.0 7.9 %concatenate.17 = bf16[1024,4,512]{2,1,0:T(4,128)(2,1)} reshape(bf16[16,8,8,2048]{3,2,1,0:T(8,128)(2,1)} %copy.39) | data formatting | bytes 8388608 | tf_op jit(solution)/shard_map/concatenate | solution.py:59
  221.9 5.0 %copy.41 = bf16[1024,4,512]{2,0,1:T(8,128)(2,1)} copy(bf16[1024,4,512]{2,1,0:T(4,128)(2,1)} %concatenate.17) | data formatting | bytes 8388608 | tf_op jit(solution)/shard_map/concatenate | solution.py:59
  226.8 23.6 %fusion.4 = bf16[8,64,4096]{2,1,0:T(8,128)(2,1)S(1)} fusion(bf16[8,64,1024]{2,1,0:T(8,128)(2,1)S(1)} %add_convert_fusion, bf16[1024,4096]{1,0:T(8,128)(2,1)} %all-gather.6.cloned.1.call-done), kind=kOutput, calls=%fused_computation.11 | convolution fusion | flops 4431282176 | bytes 13631488 | tf_op jit(solution)/shard_map/pld,df->plf/dot_general | solution.py:110
  250.4 2.6 copy.60
  253.0 6.4 %copy.38 = bf16[1024,2048]{0,1:T(8,128)(2,1)} copy(bf16[1024,2048]{1,0:T(8,128)(2,1)} %all-gather.8.cloned.1.call-done) | data formatting | bytes 8388608 | tf_op jit(solution)/shard_map/all_gather | solution.py:47
  259.5 6.2 %copy.40 = bf16[1024,4,512]{2,0,1:T(8,128)(2,1)} copy(bf16[1024,4,512]{0,2,1:T(8,128)(2,1)} %bitcast.93) | data formatting | bytes 8388608 | tf_op jit(solution)/shard_map/concatenate | solution.py:59
  265.7 8.6 %convert_reduce_fusion = f32[1024,8,64]{0,2,1:T(8,128)S(1)} fusion(bf16[8,512,512]{1,2,0:T(8,128)(2,1)} %bitcast.95, bf16[1024,4,512]{2,0,1:T(8,128)(2,1)} %copy.41, bf16[1024,4,512]{2,0,1:T(8,128)(2,1)} %copy.40), kind=kOutput, calls=%fused_computation.2 | convolution fusion | flops 4311220224 | bytes 14680064
  274.2 0.3 fusion.34
  274.6 0.5 multiply_reduce_fusion
  275.1 3.1 %select_convert_fusion = bf16[8,64,1024]{2,1,0:T(8,128)(2,1)} fusion(f32[1024]{0:T(1024)S(1)} %bitcast.107, f32[1024]{0:T(1024)S(1)} %bitcast.106, f32[8,64]{1,0:T(8,128)S(1)} %add_rsqrt_fusion, f32[8,64]{1,0:T(8,128)S(1)} %broadcast_multiply_fusion, pred[8,64]{1,0:T(8,128)(4,1)S(1)} %constant_dynamic-slice_fusion, ...), kind=kLoop, calls=%fused_computation.42 | loop fusion | flops 4194304 | bytes 4207104 | tf_op jit(solution)/shard_map/convert_element_type | solution.py:121
  (12 shorter events, 0.1 us)
Async XLA Ops:
  7.2 35.5 %copy-start.4 = (s32[8]{0:T(128)S(1)}, s32[8]{0:T(128)}, u32[]{:S(2)}) copy-start(s32[8]{0:T(128)} %param.9) | copy-start | bytes 100
  7.2 145.2 %all-gather.6.cloned.1.call-start = ((), (), s32[]{:S(2)}) async-start(), calls=%async_computation.5 | async-start | bytes 8912896 | tf_op jit(solution)/shard_map/all_gather | solution.py:44
  32.9 52.4 %copy-start = (bf16[8,8,7552]{2,0,1:T(8,128)(2,1)}, bf16[8,8,7552]{2,0,1:T(8,128)(2,1)S(1)}, u32[]{:S(2)}) copy-start(bf16[8,8,7552]{2,0,1:T(8,128)(2,1)S(1)} %all_to_all.30) | copy-start | bytes 2899972
  34.8 49.4 %all-to-all-start.1 = ((bf16[16,64,384]{2,1,0:T(8,128)(2,1)}), bf16[16,64,384]{2,1,0:T(8,128)(2,1)S(1)}, u32[]{:S(2)}, u32[]{:S(2)}) async-start(bf16[16,64,384]{2,1,0:T(8,128)(2,1)} %broadcast_in_dim.39), calls=%async_computation.1 | async-start | bytes 1572864 | tf_op jit(solution)/shard_map/all_to_all | solution.py:38
  42.6 115.9 %all-gather.4.cloned.1.call-start = ((), (), s32[]{:S(2)}) async-start(), calls=%async_computation.4 | async-start | bytes 2228224 | tf_op jit(solution)/shard_map/all_gather | solution.py:44
  121.2 31.2 %copy-start.2 = (f32[2,1024]{1,0:T(2,128)S(1)}, f32[2,1024]{1,0:T(2,128)}, u32[]{:S(2)}) copy-start(f32[2,1024]{1,0:T(2,128)} %param.14) | copy-start | bytes 24580
  121.2 31.2 %copy-start.3 = (f32[2,1024]{1,0:T(2,128)S(1)}, f32[2,1024]{1,0:T(2,128)}, u32[]{:S(2)}) copy-start(f32[2,1024]{1,0:T(2,128)} %param.15) | copy-start | bytes 24580
  145.8 63.4 %all-to-all-start.3 = ((bf16[8,128,2048]{2,1,0:T(8,128)(2,1)}), bf16[8,128,2048]{2,1,0:T(8,128)(2,1)}, u32[]{:S(2)}, u32[]{:S(2)}) async-start(bf16[8,128,2048]{2,1,0:T(8,128)(2,1)} %broadcast_in_dim.70), calls=%async_computation.3 | async-start | bytes 8388608 | tf_op jit(solution)/shard_map/all_to_all | solution.py:55
  150.4 102.7 %all-gather.8.cloned.1.call-start = ((), (), s32[]{:S(2)}) async-start(), calls=%async_computation.6 | async-start | bytes 4456448 | tf_op jit(solution)/shard_map/all_gather | solution.py:47
  153.9 7.5 %copy-start.1 = (bf16[8,8,64,128]{3,2,1,0:T(8,128)(2,1)S(1)}, bf16[8,8,64,128]{3,2,1,0:T(8,128)(2,1)}, u32[]{:S(2)}) copy-start(bf16[8,8,64,128]{3,2,1,0:T(8,128)(2,1)} %all_to_all.31) | copy-start | bytes 3145732
Sparse Core Ops, SparseCore 0:
  33.9 65.8 all-gather.5
  101.5 39.4 all-gather.3
  152.9 67.9 all-gather.7

commit v4 on v1

--- a/solution.py
+++ b/solution.py
@@ -36,12 +36,11 @@
     in_part = jnp.broadcast_to(in_part[None], (seq_axis,) + in_part.shape)
     qkv_weight = lax.all_to_all(in_part, "seq", 0, 0, tiled=True)
     qkv_weight = qkv_weight.reshape(-1, 3, block_width)
-    edges = [3 * block_width, 3 * block_width + model_width,
-             3 * block_width + model_width + hidden_width,
-             3 * block_width + model_width + 2 * hidden_width]
-    proj_weight_t, up_weight, down_weight_t = [
-        lax.all_gather(packed[:, lower:upper], "seq", axis=0, tiled=True)
-        for lower, upper in zip(edges[:-1], edges[1:])]
+    early_end = 3 * block_width + model_width + hidden_width
+    early = lax.all_gather(packed[:, 3 * block_width:early_end], "seq", axis=0, tiled=True)
+    proj_weight_t = early[:, :model_width]
+    up_weight = early[:, model_width:]
+    down_weight_t = lax.all_gather(packed[:, early_end:], "seq", axis=0, tiled=True)
     return qkv_weight, proj_weight_t, up_weight, down_weight_t
 
 

time: 217 us -> 184 us (0.85)
  waiting for transfers between devices: 63.8 us -> 27.9 us
    all_gather x3 -> x2, waiting for transfers between devices: 37.7 us -> 1.52 us  [the longest x1 1.52 us: regroup_weights(): lax.all_gather(packed[:, early_end:], 'seq', axis=0, tiled=True)]
    all_to_all x1, waiting for transfers between devices: 16.7 us -> 21.3 us  [regroup_weights(): qkv_weight = lax.all_to_all(in_part, 'seq', 0, 0, tiled=True)]
    slice x2 -> x4, local copies, waits for them, and re-layouts: 1.77 us -> 6.05 us  [the longest x2 4.34 us: regroup_weights(): proj_weight_t = early[:, :model_width]]
    all_to_all x1, waiting for transfers between devices: 8.79 us -> 5.07 us  [encode_chunk(): context_blocks = lax.all_to_all(context_blocks, 'head', 0, 0, tiled=True)]
    all_gather x1 -> x0, local copies, waits for them, and re-layouts: 2.85 us -> none  [regroup_weights(): lax.all_gather(packed[:, lower:upper], 'seq', axis=0, tiled=True)]
  transfers between devices with their start and end apart: 5 -> 4, of which waited for: 4 -> 3; matrix products, arithmetic and copies ran while one was open for 39% -> 47% of each run, Pallas kernels for 0% -> 0%
where the time goes in v4:
time: 184 us; the launch traced here: 182 us
  matrix products  64.7 us (35%)
  waiting for transfers between devices  27.9 us (15%)
  blocking collectives  24.8 us (13%)
  local copies, waits for them, and re-layouts  24.4 us (13%)
  between operations  14.2 us (8%)
  other arithmetic  14 us (8%)
  starting transfers between devices  12.2 us (7%)
    all_to_all x1, blocking collectives, regroup_weights(): packed = lax.all_to_all(packed, 'head', 1, 0, tiled=True)  24.8 us
    dot_general x1, matrix products, encode_chunk(): jnp.einsum('pld,df->plf', normed_rows, up_weight, preferred_element_type=...  23.8 us
    all_to_all x1, waiting for transfers between devices, regroup_weights(): qkv_weight = lax.all_to_all(in_part, 'seq', 0, 0, tiled=True)  21.3 us
    sub x1, matrix products, encode_chunk(): raised = jnp.exp(scores - row_peak)  10.8 us
    unnamed x1, matrix products  9.23 us
    dot_general x1, matrix products, encode_chunk(): jnp.einsum('phqk,pkhd->pqhd', weights, value_heads, preferred_element_typ...  9.01 us
    all_to_all x1, starting transfers between devices, regroup_weights(): qkv_weight = lax.all_to_all(in_part, 'seq', 0, 0, tiled=True)  7.74 us
    dot_general x1, matrix products, encode_chunk(): jnp.einsum('pld,dte->plte', tokens, qkv_weight, preferred_element_type=jn...  7.39 us
  transfers between devices with their start and end apart: 4, of which 3 were waited for; matrix products, arithmetic and copies ran while one was open for 47% of the time, Pallas kernels for 0%

profile of v4, /device:TPU:1, one launch (start us, length us, event | category | flops | bytes accessed | tf_op | source)
XLA Modules:
  0.0 182.3 jit_solution(12231516812554814228)
XLA Ops:
  7.2 0.0 copy-start.2
  7.2 0.0 all-gather.3.cloned.1.call-start
  7.2 0.9 convert_bitcast_fusion.1
  8.1 0.9 convert_element_type.59
  9.0 0.8 convert_bitcast_fusion.3
  9.8 0.9 copy_bitcast_fusion.1
  10.7 0.1 broadcast_in_dim.36
  10.8 0.1 pad_maximum_fusion
  10.9 24.8 %all_to_all.25 = bf16[8,8,9600]{2,0,1:T(8,128)(2,1)S(1)} all-to-all(bf16[8,8,9600]{2,0,1:T(8,128)(2,1)S(1)} %pad_maximum_fusion), channel_id=1, replica_groups=mesh['seq'=16,'head'=8] {'head'}, dimensions={1} | all-to-all | bytes 2457600 | tf_op jit(solution)/shard_map/all_to_all | solution.py:33
  35.7 0.9 slice.52
  36.6 0.0 all-gather.3.cloned.1.call-update
  36.6 0.0 all-gather.5.cloned.1.call-start
  36.7 0.8 slice.54
  37.5 0.0 all-gather.5.cloned.1.call-update
  37.6 1.0 broadcast_in_dim.37
  38.5 7.7 %all-to-all-start.1 = ((bf16[16,64,384]{2,1,0:T(8,128)(2,1)}), bf16[16,64,384]{2,1,0:T(8,128)(2,1)S(1)}, u32[]{:S(2)}, u32[]{:S(2)}) async-start(bf16[16,64,384]{2,1,0:T(8,128)(2,1)} %broadcast_in_dim.37), calls=%async_computation.1 | async-start | bytes 1572864 | tf_op jit(solution)/shard_map/all_to_all | solution.py:37
  46.3 0.0 copy-done.2
  46.3 0.1 iota_compare_fusion
  46.4 21.3 %all-to-all-done.1 = bf16[16,64,384]{2,1,0:T(8,128)(2,1)S(1)} async-done(((bf16[16,64,384]{2,1,0:T(8,128)(2,1)}), bf16[16,64,384]{2,1,0:T(8,128)(2,1)S(1)}, u32[]{:S(2)}, u32[]{:S(2)}) %all-to-all-start.1) | async-done | bytes 786464 | tf_op jit(solution)/shard_map/all_to_all | solution.py:37
  67.6 1.1 reshape.102
  68.7 7.4 %convert_bitcast_fusion = bf16[8,512,3,128]{1,3,0,2:T(8,128)(2,1)S(1)} fusion(bf16[8,512,1024]{2,1,0:T(8,128)(2,1)} %param.8, bf16[1024,3,128,1]{2,1,0,3:T(4,128)(2,1)} %bitcast.95), kind=kOutput, calls=%fused_computation.39 | convolution fusion | flops 3222798336 | bytes 12320768 | tf_op jit(solution)/shard_map/pld,dte->plte/dot_general | solution.py:58
  76.1 1.8 fusion.37
  77.9 10.8 %fusion.40 = (f32[8,2,512]{2,1,0:T(2,128)S(1)}, f32[8,2,512,512]{2,3,1,0:T(8,128)}) fusion(pred[8,512]{1,0:T(8,128)(4,1)S(1)} %iota_compare_fusion, bf16[8,512,2,64]{1,3,2,0:T(8,128)(2,1)} %bitcast.98, bf16[8,512,2,64]{1,3,2,0:T(8,128)(2,1)} %bitcast.97), kind=kOutput, calls=%fused_computation.71 | convolution fusion | flops 553648640 | bytes 18911232 | tf_op jit(solution)/shard_map/sub | solution.py:73
  88.7 9.0 %fusion.31 = bf16[8,512,2,64]{1,3,2,0:T(8,128)(2,1)} fusion(bf16[8,512,2,64]{1,3,2,0:T(8,128)(2,1)} %bitcast.96, f32[8,2,512,512]{2,3,1,0:T(8,128)} %get-tuple-element.19, f32[8,2,512]{2,1,0:T(2,128)S(1)} %get-tuple-element.18), kind=kOutput, calls=%fused_computation.48 | convolution fusion | flops 545783808 | bytes 18907136 | tf_op jit(solution)/shard_map/phqk,pkhd->pqhd/dot_general | solution.py:75
  97.7 0.0 copy-start
  97.7 0.0 copy-start.1
  97.7 4.0 %reshape.103 = bf16[8,8,64,128]{2,1,3,0:T(8,128)(2,1)} reshape(bf16[8,512,2,64]{1,3,2,0:T(8,128)(2,1)} %fusion.31) | data formatting | bytes 2097152 | tf_op jit(solution)/shard_map/reshape | solution.py:78
  101.7 3.3 %copy.22 = bf16[8,8,64,128]{3,2,0,1:T(8,128)(2,1)} copy(bf16[8,8,64,128]{2,1,3,0:T(8,128)(2,1)} %reshape.103) | data formatting | bytes 2097152 | tf_op jit(solution)/shard_map/reshape | solution.py:78
  105.0 4.4 %all-to-all-start.2 = ((bf16[8,8,64,128]{3,2,1,0:T(8,128)(2,1)}), bf16[8,8,64,128]{3,2,1,0:T(8,128)(2,1)}, u32[]{:S(2)}, u32[]{:S(2)}) async-start(bf16[8,8,64,128]{3,2,1,0:T(8,128)(2,1)} %bitcast.91), calls=%async_computation.2 | async-start | bytes 2097152 | tf_op jit(solution)/shard_map/all_to_all | solution.py:82
  109.4 0.1 constant_dynamic-slice_fusion
  109.5 0.0 copy-done
  109.5 0.0 copy-done.1
  109.6 1.5 bitcast_select_fusion
  111.0 2.3 %copy.27 = bf16[8,512,128]{2,1,0:T(8,128)(2,1)} copy(bf16[8,512,128]{1,2,0:T(8,128)(2,1)} %get-tuple-element.10) | data formatting | bytes 2097152
  113.3 2.3 %copy.28 = bf16[8,512,128]{2,1,0:T(8,128)(2,1)} copy(bf16[8,512,128]{1,2,0:T(8,128)(2,1)} %get-tuple-element.9) | data formatting | bytes 2097152
  115.5 0.0 all-gather.3.cloned.1.call-done
  115.5 1.8 slice.53
  117.3 2.6 %copy.23 = bf16[1024,1024]{0,1:T(8,128)(2,1)} copy(bf16[1024,1024]{1,0:T(8,128)(2,1)S(1)} %slice.53) | data formatting | bytes 4194304 | tf_op jit(solution)/shard_map/slice | solution.py:41
  119.9 5.1 %all-to-all-done.2 = bf16[8,8,64,128]{3,2,1,0:T(8,128)(2,1)} async-done(((bf16[8,8,64,128]{3,2,1,0:T(8,128)(2,1)}), bf16[8,8,64,128]{3,2,1,0:T(8,128)(2,1)}, u32[]{:S(2)}, u32[]{:S(2)}) %all-to-all-start.2) | async-done | bytes 1048608 | tf_op jit(solution)/shard_map/all_to_all | solution.py:82
  125.0 4.4 %convert_reduce_fusion.1 = f32[8,64,1024]{2,1,0:T(8,128)S(1)} fusion(bf16[8,8,64,128]{3,2,1,0:T(8,128)(2,1)} %all-to-all-done.2, bf16[1024,8,128,1]{0,2,3,1:T(8,128)(2,1)} %bitcast.94), kind=kOutput, calls=%fused_computation.3 | convolution fusion | flops 1085800448 | bytes 5242880 | tf_op jit(solution)/shard_map/sprf,esf->spre/dot_general | solution.py:84
  129.4 1.5 fusion.34
  131.0 1.7 multiply_reduce_fusion.1
  132.7 1.8 add_convert_fusion
  134.5 23.8 %fusion.4 = bf16[8,64,4096]{2,1,0:T(8,128)(2,1)S(1)} fusion(bf16[8,64,1024]{2,1,0:T(8,128)(2,1)S(1)} %add_convert_fusion, bf16[1024,5120]{1,0:T(8,128)(2,1)} %all-gather.3.cloned.1.call-done), kind=kOutput, calls=%fused_computation.11 | convolution fusion | flops 4431282176 | bytes 13631488 | tf_op jit(solution)/shard_map/pld,df->plf/dot_general | solution.py:93
  158.3 2.5 %copy.50 = bf16[8,8,8,8,512]{4,3,1,0,2:T(8,128)(2,1)} copy(bf16[8,8,8,8,512]{4,3,2,1,0:T(8,128)(2,1)S(1)} %bitcast.93) | data formatting | bytes 8388608 | tf_op jit(solution)/shard_map/reshape | solution.py:96
  160.9 1.5 all-gather.5.cloned.1.call-done
  162.4 9.2 %convert_reduce_fusion = f32[1024,8,64]{0,2,1:T(8,128)S(1)} fusion(bf16[8,512,512]{1,2,0:T(8,128)(2,1)} %bitcast.92, bf16[128,8,8,512]{3,2,1,0:T(8,128)(2,1)} %bitcast.103), kind=kOutput, calls=%fused_computation.2 | convolution fusion | flops 4307025920 | bytes 14680064
  171.6 0.3 fusion.32
  171.9 0.4 multiply_reduce_fusion
  172.4 3.1 %select_convert_fusion = bf16[8,64,1024]{2,1,0:T(8,128)(2,1)} fusion(f32[1024]{0:T(1024)S(1)} %bitcast.100, f32[1024]{0:T(1024)S(1)} %bitcast.99, f32[8,64]{1,0:T(8,128)S(1)} %add_rsqrt_fusion, f32[8,64]{1,0:T(8,128)S(1)} %broadcast_multiply_fusion, pred[8,64]{1,0:T(8,128)(4,1)S(1)} %constant_dynamic-slice_fusion, f32[1024,8,64]{0,2,1:T(8,128)S(1)} %convert_reduce_fusion, ...), kind=kLoop, calls=%fused_computation.41 | loop fusion | flops 4194304 | bytes 4207104 | tf_op jit(solution)/shard_map/convert_element_type | solution.py:104
  (8 shorter events, 0.1 us)
Async XLA Ops:
  7.2 39.1 %copy-start.2 = (s32[8]{0:T(128)S(1)}, s32[8]{0:T(128)}, u32[]{:S(2)}) copy-start(s32[8]{0:T(128)} %param.9) | copy-start | bytes 100
  7.2 108.4 %all-gather.3.cloned.1.call-start = ((), (), s32[]{:S(2)}) async-start(), calls=%async_computation.3 | async-start | bytes 11141120 | tf_op jit(solution)/shard_map/all_gather | solution.py:40
  36.6 125.8 %all-gather.5.cloned.1.call-start = ((), (), s32[]{:S(2)}) async-start(), calls=%async_computation.4 | async-start | bytes 8912896 | tf_op jit(solution)/shard_map/all_gather | solution.py:43
  38.5 29.1 %all-to-all-start.1 = ((bf16[16,64,384]{2,1,0:T(8,128)(2,1)}), bf16[16,64,384]{2,1,0:T(8,128)(2,1)S(1)}, u32[]{:S(2)}, u32[]{:S(2)}) async-start(bf16[16,64,384]{2,1,0:T(8,128)(2,1)} %broadcast_in_dim.37), calls=%async_computation.1 | async-start | bytes 1572864 | tf_op jit(solution)/shard_map/all_to_all | solution.py:37
  97.7 11.8 %copy-start = (f32[2,1024]{1,0:T(2,128)S(1)}, f32[2,1024]{1,0:T(2,128)}, u32[]{:S(2)}) copy-start(f32[2,1024]{1,0:T(2,128)} %param.14) | copy-start | bytes 24580
  97.7 11.8 %copy-start.1 = (f32[2,1024]{1,0:T(2,128)S(1)}, f32[2,1024]{1,0:T(2,128)}, u32[]{:S(2)}) copy-start(f32[2,1024]{1,0:T(2,128)} %param.15) | copy-start | bytes 24580
  105.0 20.0 %all-to-all-start.2 = ((bf16[8,8,64,128]{3,2,1,0:T(8,128)(2,1)}), bf16[8,8,64,128]{3,2,1,0:T(8,128)(2,1)}, u32[]{:S(2)}, u32[]{:S(2)}) async-start(bf16[8,8,64,128]{3,2,1,0:T(8,128)(2,1)} %bitcast.91), calls=%async_computation.2 | async-start | bytes 2097152 | tf_op jit(solution)/shard_map/all_to_all | solution.py:82
Sparse Core Ops, SparseCore 0:
  36.8 71.0 all-gather.2
  109.6 52.7 all-gather.4

commit v5 on v4

--- a/solution.py
+++ b/solution.py
@@ -72,13 +72,14 @@
     row_peak = jnp.max(scores, axis=-1, keepdims=True)
     raised = jnp.exp(scores - row_peak)
     weights = (raised / jnp.sum(raised, axis=-1, keepdims=True)).astype(jnp.bfloat16)
+    weights = weights.reshape(prompts, local_heads, heads_axis, row_count, seq_len)
     context = jnp.einsum(
-        "phqk,pkhd->pqhd", weights, value_heads, preferred_element_type=jnp.float32
+        "phjrk,pkhd->jprhd", weights, value_heads, preferred_element_type=jnp.float32
     )
-    context = context.astype(jnp.bfloat16).reshape(prompts, heads_axis, row_count, block_width)
+    context_blocks = context.astype(jnp.bfloat16).reshape(
+        heads_axis, prompts, row_count, block_width)
     key_cache = jnp.where(inside[:, :, None], key_part, jnp.zeros_like(key_part))
     value_cache = jnp.where(inside[:, :, None], value_part, jnp.zeros_like(value_part))
-    context_blocks = jnp.transpose(context, (1, 0, 2, 3))
     context_blocks = lax.all_to_all(context_blocks, "head", 0, 0, tiled=True)
     proj_blocks = proj_weight_t.reshape(model_width, heads_axis, block_width)
     attn_blocks = jnp.einsum(

time: 184 us -> 190 us (1.033)
  other arithmetic: 14 us -> 21.1 us
  matrix products: 64.7 us -> 60.4 us
  local copies, waits for them, and re-layouts: 24.4 us -> 28.1 us
    convert_element_type x0 -> x1, other arithmetic: none -> 7.04 us  [encode_chunk(): (raised / jnp.sum(raised, axis=-1, keepdims=True)).astype(jnp.bfloat16)]
    convert_element_type x0 -> x1, local copies, waits for them, and re-layouts: none -> 6.19 us  [encode_chunk(): context.astype(jnp.bfloat16)]
    dot_general x1, matrix products: 9.01 us -> 5.44 us  [encode_chunk(): jnp.einsum('phjrk,pkhd->jprhd', weights, value_heads, preferred_element_t...]
    reshape x2 -> x1, local copies, waits for them, and re-layouts: 7.3 us -> 4.74 us  [encode_chunk(): context.astype(jnp.bfloat16)]
    unnamed x8 -> x10, local copies, waits for them, and re-layouts: 4.53 us -> 4.54 us
  transfers between devices with their start and end apart: 4 -> 4, of which waited for: 3 -> 3; matrix products, arithmetic and copies ran while one was open for 47% -> 49% of each run, Pallas kernels for 0% -> 0%
where the time goes in v5:
time: 190 us; the launch traced here: 188 us
  matrix products  60.4 us (32%)
  local copies, waits for them, and re-layouts  28.1 us (15%)
  waiting for transfers between devices  27.6 us (15%)
  blocking collectives  24.8 us (13%)
  other arithmetic  21.1 us (11%)
  between operations  14.2 us (7%)
  starting transfers between devices  12.2 us (6%)
    all_to_all x1, blocking collectives, regroup_weights(): packed = lax.all_to_all(packed, 'head', 1, 0, tiled=True)  24.8 us
    dot_general x1, matrix products, encode_chunk(): jnp.einsum('pld,df->plf', normed_rows, up_weight, preferred_element_type=...  23.8 us
    all_to_all x1, waiting for transfers between devices, regroup_weights(): qkv_weight = lax.all_to_all(in_part, 'seq', 0, 0, tiled=True)  21.3 us
    sub x1, matrix products, encode_chunk(): raised = jnp.exp(scores - row_peak)  10 us
    unnamed x1, matrix products  9.22 us
    all_to_all x1, starting transfers between devices, regroup_weights(): qkv_weight = lax.all_to_all(in_part, 'seq', 0, 0, tiled=True)  7.74 us
    dot_general x1, matrix products, encode_chunk(): jnp.einsum('pld,dte->plte', tokens, qkv_weight, preferred_element_type=jn...  7.39 us
    convert_element_type x1, other arithmetic, encode_chunk(): (raised / jnp.sum(raised, axis=-1, keepdims=True)).astype(jnp.bfloat16)  7.04 us
  transfers between devices with their start and end apart: 4, of which 3 were waited for; matrix products, arithmetic and copies ran while one was open for 49% of the time, Pallas kernels for 0%

profile of v5, /device:TPU:1, one launch (start us, length us, event | category | flops | bytes accessed | tf_op | source)
XLA Modules:
  0.0 188.4 jit_solution(13749165994424334949)
XLA Ops:
  7.2 0.0 copy-start.3
  7.2 0.0 all-gather.3.cloned.1.call-start
  7.2 0.9 convert_bitcast_fusion.2
  8.1 0.9 convert_element_type.59
  9.0 0.8 convert_bitcast_fusion.4
  9.8 0.9 copy_bitcast_fusion.1
  10.7 0.1 broadcast_in_dim.36
  10.8 0.1 pad_maximum_fusion
  10.9 24.8 %all_to_all.25 = bf16[8,8,9600]{2,0,1:T(8,128)(2,1)S(1)} all-to-all(bf16[8,8,9600]{2,0,1:T(8,128)(2,1)S(1)} %pad_maximum_fusion), channel_id=1, replica_groups=mesh['seq'=16,'head'=8] {'head'}, dimensions={1} | all-to-all | bytes 2457600 | tf_op jit(solution)/shard_map/all_to_all | solution.py:33
  35.7 0.9 slice.52
  36.6 0.0 all-gather.3.cloned.1.call-update
  36.6 0.0 all-gather.5.cloned.1.call-start
  36.7 0.8 slice.54
  37.5 0.0 all-gather.5.cloned.1.call-update
  37.6 1.0 broadcast_in_dim.37
  38.5 7.7 %all-to-all-start.1 = ((bf16[16,64,384]{2,1,0:T(8,128)(2,1)}), bf16[16,64,384]{2,1,0:T(8,128)(2,1)S(1)}, u32[]{:S(2)}, u32[]{:S(2)}) async-start(bf16[16,64,384]{2,1,0:T(8,128)(2,1)} %broadcast_in_dim.37), calls=%async_computation.1 | async-start | bytes 1572864 | tf_op jit(solution)/shard_map/all_to_all | solution.py:37
  46.3 0.0 copy-done.3
  46.3 0.1 iota_compare_fusion
  46.4 21.3 %all-to-all-done.1 = bf16[16,64,384]{2,1,0:T(8,128)(2,1)S(1)} async-done(((bf16[16,64,384]{2,1,0:T(8,128)(2,1)}), bf16[16,64,384]{2,1,0:T(8,128)(2,1)S(1)}, u32[]{:S(2)}, u32[]{:S(2)}) %all-to-all-start.1) | async-done | bytes 786464 | tf_op jit(solution)/shard_map/all_to_all | solution.py:37
  67.6 1.1 reshape.105
  68.7 7.4 %convert_bitcast_fusion = bf16[8,512,3,128]{1,3,0,2:T(8,128)(2,1)S(1)} fusion(bf16[8,512,1024]{2,1,0:T(8,128)(2,1)} %param.8, bf16[1024,3,128,1]{2,1,0,3:T(4,128)(2,1)} %bitcast.97), kind=kOutput, calls=%fused_computation.38 | convolution fusion | flops 3222798336 | bytes 12320768 | tf_op jit(solution)/shard_map/pld,dte->plte/dot_general | solution.py:58
  76.1 1.8 fusion.34
  77.9 10.0 %fusion.37 = (f32[8,2,512]{2,1,0:T(2,128)S(1)}, f32[8,2,512,512]{3,2,1,0:T(8,128)}) fusion(pred[8,512]{1,0:T(8,128)(4,1)S(1)} %iota_compare_fusion, bf16[8,512,2,64]{1,3,2,0:T(8,128)(2,1)} %bitcast.99, bf16[8,512,2,64]{1,3,2,0:T(8,128)(2,1)} %bitcast.98), kind=kOutput, calls=%fused_computation.69 | convolution fusion | flops 553648640 | bytes 18911232 | tf_op jit(solution)/shard_map/sub | solution.py:73
  87.9 0.0 copy-start
  87.9 7.0 %divide_convert_fusion = bf16[8,2,512,512]{3,2,1,0:T(8,128)(2,1)S(1)} fusion(f32[8,2,512,512]{3,2,1,0:T(8,128)} %get-tuple-element.19, f32[8,2,512]{2,1,0:T(2,128)S(1)} %get-tuple-element.18), kind=kLoop, calls=%fused_computation.4 | loop fusion | flops 8388608 | bytes 25198592 | tf_op jit(solution)/shard_map/convert_element_type | solution.py:74
  95.0 0.0 copy-done
  95.0 0.0 copy-start.1
  95.0 0.0 copy-start.2
  95.0 5.4 %convert_bitcast_fusion.1 = bf16[8,8,64,2,64]{2,4,0,3,1:T(8,128)(2,1)} fusion(bf16[8,512,2,64,1]{1,3,4,2,0:T(8,128)(2,1)S(1)} %bitcast.95, bf16[8,2,8,64,512]{4,3,2,1,0:T(8,128)(2,1)S(1)} %bitcast.89), kind=kOutput, calls=%fused_computation.44 | convolution fusion | flops 537395200 | bytes 10485760 | tf_op jit(solution)/shard_map/phjrk,pkhd->jprhd/dot_general | solution.py:76
  100.5 6.2 %copy.19 = bf16[8,8,64,2,64]{4,3,2,1,0:T(2,128)(2,1)} copy(bf16[8,8,64,2,64]{2,4,0,3,1:T(8,128)(2,1)} %convert_bitcast_fusion.1) | data formatting | bytes 2097152 | tf_op jit(solution)/shard_map/convert_element_type | solution.py:79
  106.7 4.7 %reshape.107 = bf16[8,8,64,128]{3,2,1,0:T(8,128)(2,1)} reshape(bf16[8,8,64,2,64]{4,3,2,1,0:T(2,128)(2,1)} %copy.19) | data formatting | bytes 2097152 | tf_op jit(solution)/shard_map/reshape | solution.py:79
  111.4 4.4 %all-to-all-start.2 = ((bf16[8,8,64,128]{3,2,1,0:T(8,128)(2,1)}), bf16[8,8,64,128]{3,2,1,0:T(8,128)(2,1)}, u32[]{:S(2)}, u32[]{:S(2)}) async-start(bf16[8,8,64,128]{3,2,1,0:T(8,128)(2,1)} %reshape.107), calls=%async_computation.2 | async-start | bytes 2097152 | tf_op jit(solution)/shard_map/all_to_all | solution.py:83
  115.8 0.1 constant_dynamic-slice_fusion
  115.9 0.0 copy-done.1
  115.9 0.0 copy-done.2
  116.0 1.5 bitcast_select_fusion
  117.4 2.3 %copy.24 = bf16[8,512,128]{2,1,0:T(8,128)(2,1)} copy(bf16[8,512,128]{1,2,0:T(8,128)(2,1)} %get-tuple-element.10) | data formatting | bytes 2097152
  119.7 2.3 %copy.25 = bf16[8,512,128]{2,1,0:T(8,128)(2,1)} copy(bf16[8,512,128]{1,2,0:T(8,128)(2,1)} %get-tuple-element.9) | data formatting | bytes 2097152
  121.9 0.0 all-gather.3.cloned.1.call-done
  121.9 1.8 slice.53
  123.7 2.6 %copy.20 = bf16[1024,1024]{0,1:T(8,128)(2,1)} copy(bf16[1024,1024]{1,0:T(8,128)(2,1)S(1)} %slice.53) | data formatting | bytes 4194304 | tf_op jit(solution)/shard_map/slice | solution.py:41
  126.3 5.9 %all-to-all-done.2 = bf16[8,8,64,128]{3,2,1,0:T(8,128)(2,1)} async-done(((bf16[8,8,64,128]{3,2,1,0:T(8,128)(2,1)}), bf16[8,8,64,128]{3,2,1,0:T(8,128)(2,1)}, u32[]{:S(2)}, u32[]{:S(2)}) %all-to-all-start.2) | async-done | bytes 1048608 | tf_op jit(solution)/shard_map/all_to_all | solution.py:83
  132.1 4.5 %convert_reduce_fusion.1 = f32[8,64,1024]{2,1,0:T(8,128)S(1)} fusion(bf16[8,8,64,128]{3,2,1,0:T(8,128)(2,1)} %all-to-all-done.2, bf16[1024,8,128,1]{0,2,3,1:T(8,128)(2,1)} %bitcast.96), kind=kOutput, calls=%fused_computation.3 | convolution fusion | flops 1085800448 | bytes 5242880 | tf_op jit(solution)/shard_map/sprf,esf->spre/dot_general | solution.py:85
  136.6 1.6 fusion.31
  138.2 1.8 multiply_reduce_fusion.1
  139.9 1.8 add_convert_fusion
  141.7 23.8 %fusion.4 = bf16[8,64,4096]{2,1,0:T(8,128)(2,1)S(1)} fusion(bf16[8,64,1024]{2,1,0:T(8,128)(2,1)S(1)} %add_convert_fusion, bf16[1024,5120]{1,0:T(8,128)(2,1)} %all-gather.3.cloned.1.call-done), kind=kOutput, calls=%fused_computation.11 | convolution fusion | flops 4431282176 | bytes 13631488 | tf_op jit(solution)/shard_map/pld,df->plf/dot_general | solution.py:94
  165.6 2.5 %copy.47 = bf16[8,8,8,8,512]{4,3,1,0,2:T(8,128)(2,1)} copy(bf16[8,8,8,8,512]{4,3,2,1,0:T(8,128)(2,1)S(1)} %bitcast.94) | data formatting | bytes 8388608 | tf_op jit(solution)/shard_map/reshape | solution.py:97
  168.1 0.4 all-gather.5.cloned.1.call-done
  168.5 9.2 %convert_reduce_fusion = f32[1024,8,64]{0,2,1:T(8,128)S(1)} fusion(bf16[8,512,512]{1,2,0:T(8,128)(2,1)} %bitcast.93, bf16[128,8,8,512]{3,2,1,0:T(8,128)(2,1)} %bitcast.104), kind=kOutput, calls=%fused_computation.2 | convolution fusion | flops 4307025920 | bytes 14680064
  177.7 0.3 fusion.29
  178.0 0.4 multiply_reduce_fusion
  178.5 3.1 %select_convert_fusion = bf16[8,64,1024]{2,1,0:T(8,128)(2,1)} fusion(f32[1024]{0:T(1024)S(1)} %bitcast.101, f32[1024]{0:T(1024)S(1)} %bitcast.100, f32[8,64]{1,0:T(8,128)S(1)} %add_rsqrt_fusion, f32[8,64]{1,0:T(8,128)S(1)} %broadcast_multiply_fusion, pred[8,64]{1,0:T(8,128)(4,1)S(1)} %constant_dynamic-slice_fusion, ...), kind=kLoop, calls=%fused_computation.40 | loop fusion | flops 4194304 | bytes 4207104 | tf_op jit(solution)/shard_map/convert_element_type | solution.py:105
  (8 shorter events, 0.1 us)
Async XLA Ops:
  7.2 39.1 %copy-start.3 = (s32[8]{0:T(128)S(1)}, s32[8]{0:T(128)}, u32[]{:S(2)}) copy-start(s32[8]{0:T(128)} %param.9) | copy-start | bytes 100
  7.2 114.8 %all-gather.3.cloned.1.call-start = ((), (), s32[]{:S(2)}) async-start(), calls=%async_computation.3 | async-start | bytes 11141120 | tf_op jit(solution)/shard_map/all_gather | solution.py:40
  36.6 131.8 %all-gather.5.cloned.1.call-start = ((), (), s32[]{:S(2)}) async-start(), calls=%async_computation.4 | async-start | bytes 8912896 | tf_op jit(solution)/shard_map/all_gather | solution.py:43
  38.5 29.1 %all-to-all-start.1 = ((bf16[16,64,384]{2,1,0:T(8,128)(2,1)}), bf16[16,64,384]{2,1,0:T(8,128)(2,1)S(1)}, u32[]{:S(2)}, u32[]{:S(2)}) async-start(bf16[16,64,384]{2,1,0:T(8,128)(2,1)} %broadcast_in_dim.37), calls=%async_computation.1 | async-start | bytes 1572864 | tf_op jit(solution)/shard_map/all_to_all | solution.py:37
  87.9 7.1 %copy-start = (bf16[8,512,1,128]{1,3,0,2:T(8,128)(2,1)S(1)}, bf16[8,512,1,128]{1,3,0,2:T(8,128)(2,1)}, u32[]{:S(2)}) copy-start(bf16[8,512,1,128]{1,3,0,2:T(8,128)(2,1)} %get-tuple-element.13) | copy-start | bytes 3145732
  95.0 20.9 %copy-start.1 = (f32[2,1024]{1,0:T(2,128)S(1)}, f32[2,1024]{1,0:T(2,128)}, u32[]{:S(2)}) copy-start(f32[2,1024]{1,0:T(2,128)} %param.14) | copy-start | bytes 24580
  95.0 20.9 %copy-start.2 = (f32[2,1024]{1,0:T(2,128)S(1)}, f32[2,1024]{1,0:T(2,128)}, u32[]{:S(2)}) copy-start(f32[2,1024]{1,0:T(2,128)} %param.15) | copy-start | bytes 24580
  111.4 20.7 %all-to-all-start.2 = ((bf16[8,8,64,128]{3,2,1,0:T(8,128)(2,1)}), bf16[8,8,64,128]{3,2,1,0:T(8,128)(2,1)}, u32[]{:S(2)}, u32[]{:S(2)}) async-start(bf16[8,8,64,128]{3,2,1,0:T(8,128)(2,1)} %reshape.107), calls=%async_computation.2 | async-start | bytes 2097152 | tf_op jit(solution)/shard_map/all_to_all | solution.py:83
Sparse Core Ops, SparseCore 0:
  36.8 71.0 all-gather.2
  109.6 58.8 all-gather.4

commit v6 on v4

--- a/solution.py
+++ b/solution.py
@@ -29,15 +29,17 @@
         [attn_out.astype(jnp.bfloat16).T, mlp_in.astype(jnp.bfloat16),
          mlp_out.astype(jnp.bfloat16).T], axis=1)
     whole_piece = jnp.broadcast_to(whole_rows[:, None], (rows, heads_axis, whole_rows.shape[1]))
-    packed = jnp.concatenate([in_piece, whole_piece], axis=2)
-    packed = lax.all_to_all(packed, "head", 1, 0, tiled=True)
-    packed = packed.reshape(rows * heads_axis, packed.shape[2])
-    in_part = packed[:, :3 * block_width]
+    whole_piece = lax.all_to_all(whole_piece, "head", 1, 0, tiled=True)
+    whole_piece = whole_piece.reshape(rows * heads_axis, whole_piece.shape[2])
+    in_piece, whole_piece = lax.optimization_barrier((in_piece, whole_piece))
+    in_part = lax.all_to_all(in_piece, "head", 1, 0, tiled=True)
+    in_part = in_part.reshape(rows * heads_axis, 3 * block_width)
     in_part = jnp.broadcast_to(in_part[None], (seq_axis,) + in_part.shape)
     qkv_weight = lax.all_to_all(in_part, "seq", 0, 0, tiled=True)
     qkv_weight = qkv_weight.reshape(-1, 3, block_width)
-    early_end = 3 * block_width + model_width + hidden_width
-    early = lax.all_gather(packed[:, 3 * block_width:early_end], "seq", axis=0, tiled=True)
+    packed = whole_piece
+    early_end = model_width + hidden_width
+    early = lax.all_gather(packed[:, :early_end], "seq", axis=0, tiled=True)
     proj_weight_t = early[:, :model_width]
     up_weight = early[:, model_width:]
     down_weight_t = lax.all_gather(packed[:, early_end:], "seq", axis=0, tiled=True)

time: 184 us -> 194 us (1.054)
  waiting for transfers between devices: 27.9 us -> 44.8 us
  blocking collectives: 24.8 us -> 10.3 us
  starting transfers between devices: 12.2 us -> 19.8 us
    all_to_all x0 -> x1, waiting for transfers between devices: none -> 16.3 us  [regroup_weights(): whole_piece = lax.all_to_all(whole_piece, 'head', 1, 0, tiled=True)]
    all_to_all x1, blocking collectives: 24.8 us -> 10.3 us  [regroup_weights(): in_part = lax.all_to_all(in_piece, 'head', 1, 0, tiled=True)]
    all_to_all x0 -> x1, starting transfers between devices: none -> 7.48 us  [regroup_weights(): whole_piece = lax.all_to_all(whole_piece, 'head', 1, 0, tiled=True)]
  transfers between devices with their start and end apart: 4 -> 5, of which waited for: 3 -> 3; matrix products, arithmetic and copies ran while one was open for 47% -> 45% of each run, Pallas kernels for 0% -> 0%
where the time goes in v6:
time: 194 us; the launch traced here: 193 us
  matrix products  64.5 us (33%)
  waiting for transfers between devices  44.8 us (23%)
  local copies, waits for them, and re-layouts  25.4 us (13%)
  starting transfers between devices  19.8 us (10%)
  between operations  14.2 us (7%)
  other arithmetic  13.9 us (7%)
  blocking collectives  10.3 us (5%)
    dot_general x1, matrix products, encode_chunk(): jnp.einsum('pld,df->plf', normed_rows, up_weight, preferred_element_type=...  23.8 us
    all_to_all x1, waiting for transfers between devices, regroup_weights(): qkv_weight = lax.all_to_all(in_part, 'seq', 0, 0, tiled=True)  21.5 us
    all_to_all x1, waiting for transfers between devices, regroup_weights(): whole_piece = lax.all_to_all(whole_piece, 'head', 1, 0, tiled=True)  16.3 us
    sub x1, matrix products, encode_chunk(): raised = jnp.exp(scores - row_peak)  10.7 us
    all_to_all x1, blocking collectives, regroup_weights(): in_part = lax.all_to_all(in_piece, 'head', 1, 0, tiled=True)  10.3 us
    unnamed x1, matrix products  9.23 us
    dot_general x1, matrix products, encode_chunk(): jnp.einsum('phqk,pkhd->pqhd', weights, value_heads, preferred_element_typ...  8.86 us
    all_to_all x1, starting transfers between devices, regroup_weights(): qkv_weight = lax.all_to_all(in_part, 'seq', 0, 0, tiled=True)  7.77 us
  transfers between devices with their start and end apart: 5, of which 3 were waited for; matrix products, arithmetic and copies ran while one was open for 45% of the time, Pallas kernels for 0%

profile of v6, /device:TPU:1, one launch (start us, length us, event | category | flops | bytes accessed | tf_op | source)
XLA Modules:
  0.0 192.9 jit_solution(6044843027836089347)
XLA Ops:
  7.2 0.0 copy-start.2
  7.2 0.9 convert_bitcast_fusion.1
  8.1 0.9 convert_element_type.59
  9.0 0.8 convert_bitcast_fusion.3
  9.8 1.1 broadcast_in_dim.61
  10.9 7.5 %all-to-all-start = ((bf16[8,8,9216]{2,0,1:T(8,128)(2,1)}), bf16[8,8,9216]{2,0,1:T(8,128)(2,1)S(1)}, u32[]{:S(2)}, u32[]{:S(2)}) async-start(bf16[8,8,9216]{2,0,1:T(8,128)(2,1)} %broadcast_in_dim.61), calls=%async_computation | async-start | bytes 2359296 | tf_op jit(solution)/shard_map/all_to_all | solution.py:32
  18.3 0.0 all-gather.3.cloned.1.call-start
  18.4 0.9 convert_bitcast_fusion.2
  19.3 16.3 %all-to-all-done = bf16[8,8,9216]{2,0,1:T(8,128)(2,1)S(1)} async-done(((bf16[8,8,9216]{2,0,1:T(8,128)(2,1)}), bf16[8,8,9216]{2,0,1:T(8,128)(2,1)S(1)}, u32[]{:S(2)}, u32[]{:S(2)}) %all-to-all-start) | async-done | bytes 1179680 | tf_op jit(solution)/shard_map/all_to_all | solution.py:32
  35.6 0.9 slice.36
  36.5 0.0 all-gather.3.cloned.1.call-update
  36.5 0.0 all-gather.5.cloned.1.call-start
  36.6 0.8 slice.40
  37.4 0.0 all-gather.5.cloned.1.call-update
  37.4 10.3 %all_to_all.40 = bf16[8,8,384]{2,0,1:T(8,128)(2,1)S(1)} all-to-all(bf16[8,8,384]{2,0,1:T(8,128)(2,1)S(1)} %copy.40), channel_id=1, replica_groups=mesh['seq'=16,'head'=8] {'head'}, dimensions={1} | all-to-all | bytes 98304 | tf_op jit(solution)/shard_map/all_to_all | solution.py:35
  47.7 1.0 broadcast_in_dim.63
  48.7 7.8 %all-to-all-start.2 = ((bf16[16,64,384]{2,1,0:T(8,128)(2,1)}), bf16[16,64,384]{2,1,0:T(8,128)(2,1)S(1)}, u32[]{:S(2)}, u32[]{:S(2)}) async-start(bf16[16,64,384]{2,1,0:T(8,128)(2,1)} %broadcast_in_dim.63), calls=%async_computation.2 | async-start | bytes 1572864 | tf_op jit(solution)/shard_map/all_to_all | solution.py:38
  56.5 0.0 copy-done.2
  56.5 0.1 iota_compare_fusion
  56.6 21.5 %all-to-all-done.2 = bf16[16,64,384]{2,1,0:T(8,128)(2,1)S(1)} async-done(((bf16[16,64,384]{2,1,0:T(8,128)(2,1)}), bf16[16,64,384]{2,1,0:T(8,128)(2,1)S(1)}, u32[]{:S(2)}, u32[]{:S(2)}) %all-to-all-start.2) | async-done | bytes 786464 | tf_op jit(solution)/shard_map/all_to_all | solution.py:38
  78.1 1.1 reshape.103
  79.2 7.4 %convert_bitcast_fusion = bf16[8,512,3,128]{1,3,0,2:T(8,128)(2,1)S(1)} fusion(bf16[8,512,1024]{2,1,0:T(8,128)(2,1)} %param.8, bf16[1024,3,128,1]{2,1,0,3:T(4,128)(2,1)} %bitcast.106), kind=kOutput, calls=%fused_computation.39 | convolution fusion | flops 3222798336 | bytes 12320768 | tf_op jit(solution)/shard_map/pld,dte->plte/dot_general | solution.py:60
  86.6 1.8 fusion.37
  88.3 10.7 %fusion.40 = (f32[8,2,512]{2,1,0:T(2,128)S(1)}, f32[8,2,512,512]{2,3,1,0:T(8,128)}) fusion(pred[8,512]{1,0:T(8,128)(4,1)S(1)} %iota_compare_fusion, bf16[8,512,2,64]{1,3,2,0:T(8,128)(2,1)} %bitcast.109, bf16[8,512,2,64]{1,3,2,0:T(8,128)(2,1)} %bitcast.108), kind=kOutput, calls=%fused_computation.71 | convolution fusion | flops 553648640 | bytes 18911232 | tf_op jit(solution)/shard_map/sub | solution.py:75
  99.1 8.9 %fusion.31 = bf16[8,512,2,64]{1,3,2,0:T(8,128)(2,1)} fusion(bf16[8,512,2,64]{1,3,2,0:T(8,128)(2,1)} %bitcast.107, f32[8,2,512,512]{2,3,1,0:T(8,128)} %get-tuple-element.29, f32[8,2,512]{2,1,0:T(2,128)S(1)} %get-tuple-element.28), kind=kOutput, calls=%fused_computation.48 | convolution fusion | flops 545783808 | bytes 18907136 | tf_op jit(solution)/shard_map/phqk,pkhd->pqhd/dot_general | solution.py:77
  107.9 0.0 copy-start
  107.9 0.0 copy-start.1
  107.9 4.0 %reshape.104 = bf16[8,8,64,128]{2,1,3,0:T(8,128)(2,1)} reshape(bf16[8,512,2,64]{1,3,2,0:T(8,128)(2,1)} %fusion.31) | data formatting | bytes 2097152 | tf_op jit(solution)/shard_map/reshape | solution.py:80
  111.9 3.3 %copy.43 = bf16[8,8,64,128]{3,2,0,1:T(8,128)(2,1)} copy(bf16[8,8,64,128]{2,1,3,0:T(8,128)(2,1)} %reshape.104) | data formatting | bytes 2097152 | tf_op jit(solution)/shard_map/reshape | solution.py:80
  115.2 4.4 %all-to-all-start.3 = ((bf16[8,8,64,128]{3,2,1,0:T(8,128)(2,1)}), bf16[8,8,64,128]{3,2,1,0:T(8,128)(2,1)}, u32[]{:S(2)}, u32[]{:S(2)}) async-start(bf16[8,8,64,128]{3,2,1,0:T(8,128)(2,1)} %bitcast.102), calls=%async_computation.3 | async-start | bytes 2097152 | tf_op jit(solution)/shard_map/all_to_all | solution.py:84
  119.7 0.1 constant_dynamic-slice_fusion
  119.7 0.0 copy-done
  119.8 0.0 copy-done.1
  119.8 1.5 bitcast_select_fusion
  121.3 2.3 %copy.48 = bf16[8,512,128]{2,1,0:T(8,128)(2,1)} copy(bf16[8,512,128]{1,2,0:T(8,128)(2,1)} %get-tuple-element.20) | data formatting | bytes 2097152
  123.5 2.3 %copy.49 = bf16[8,512,128]{2,1,0:T(8,128)(2,1)} copy(bf16[8,512,128]{1,2,0:T(8,128)(2,1)} %get-tuple-element.19) | data formatting | bytes 2097152
  125.8 0.0 all-gather.3.cloned.1.call-done
  125.8 1.8 slice.47
  127.5 2.6 %copy.44 = bf16[1024,1024]{0,1:T(8,128)(2,1)} copy(bf16[1024,1024]{1,0:T(8,128)(2,1)S(1)} %slice.47) | data formatting | bytes 4194304 | tf_op jit(solution)/shard_map/slice | solution.py:43
  130.1 7.0 %all-to-all-done.3 = bf16[8,8,64,128]{3,2,1,0:T(8,128)(2,1)} async-done(((bf16[8,8,64,128]{3,2,1,0:T(8,128)(2,1)}), bf16[8,8,64,128]{3,2,1,0:T(8,128)(2,1)}, u32[]{:S(2)}, u32[]{:S(2)}) %all-to-all-start.3) | async-done | bytes 1048608 | tf_op jit(solution)/shard_map/all_to_all | solution.py:84
  137.1 4.4 %convert_reduce_fusion.1 = f32[8,64,1024]{2,1,0:T(8,128)S(1)} fusion(bf16[8,8,64,128]{3,2,1,0:T(8,128)(2,1)} %all-to-all-done.3, bf16[1024,8,128,1]{0,2,3,1:T(8,128)(2,1)} %bitcast.105), kind=kOutput, calls=%fused_computation.3 | convolution fusion | flops 1085800448 | bytes 5242880 | tf_op jit(solution)/shard_map/sprf,esf->spre/dot_general | solution.py:86
  141.5 1.5 fusion.34
  143.1 1.7 multiply_reduce_fusion.1
  144.8 1.8 add_convert_fusion
  146.6 23.8 %fusion.4 = bf16[8,64,4096]{2,1,0:T(8,128)(2,1)S(1)} fusion(bf16[8,64,1024]{2,1,0:T(8,128)(2,1)S(1)} %add_convert_fusion, bf16[1024,5120]{1,0:T(8,128)(2,1)} %all-gather.3.cloned.1.call-done), kind=kOutput, calls=%fused_computation.11 | convolution fusion | flops 4431282176 | bytes 13631488 | tf_op jit(solution)/shard_map/pld,df->plf/dot_general | solution.py:95
  170.5 2.5 %copy.74 = bf16[8,8,8,8,512]{4,3,1,0,2:T(8,128)(2,1)} copy(bf16[8,8,8,8,512]{4,3,2,1,0:T(8,128)(2,1)S(1)} %bitcast.104) | data formatting | bytes 8388608 | tf_op jit(solution)/shard_map/reshape | solution.py:98
  173.0 0.0 all-gather.5.cloned.1.call-done
  173.0 9.2 %convert_reduce_fusion = f32[1024,8,64]{0,2,1:T(8,128)S(1)} fusion(bf16[8,512,512]{1,2,0:T(8,128)(2,1)} %bitcast.103, bf16[128,8,8,512]{3,2,1,0:T(8,128)(2,1)} %bitcast.115), kind=kOutput, calls=%fused_computation.2 | convolution fusion | flops 4307025920 | bytes 14680064
  182.2 0.3 fusion.32
  182.5 0.4 multiply_reduce_fusion
  183.0 3.1 %select_convert_fusion = bf16[8,64,1024]{2,1,0:T(8,128)(2,1)} fusion(f32[1024]{0:T(1024)S(1)} %bitcast.112, f32[1024]{0:T(1024)S(1)} %bitcast.111, f32[8,64]{1,0:T(8,128)S(1)} %add_rsqrt_fusion, f32[8,64]{1,0:T(8,128)S(1)} %broadcast_multiply_fusion, pred[8,64]{1,0:T(8,128)(4,1)S(1)} %constant_dynamic-slice_fusion, ...), kind=kLoop, calls=%fused_computation.41 | loop fusion | flops 4194304 | bytes 4207104 | tf_op jit(solution)/shard_map/convert_element_type | solution.py:106
  (9 shorter events, 0.1 us)
Async XLA Ops:
  7.2 49.3 %copy-start.2 = (s32[8]{0:T(128)S(1)}, s32[8]{0:T(128)}, u32[]{:S(2)}) copy-start(s32[8]{0:T(128)} %param.9) | copy-start | bytes 100
  10.9 24.7 %all-to-all-start = ((bf16[8,8,9216]{2,0,1:T(8,128)(2,1)}), bf16[8,8,9216]{2,0,1:T(8,128)(2,1)S(1)}, u32[]{:S(2)}, u32[]{:S(2)}) async-start(bf16[8,8,9216]{2,0,1:T(8,128)(2,1)} %broadcast_in_dim.61), calls=%async_computation | async-start | bytes 2359296 | tf_op jit(solution)/shard_map/all_to_all | solution.py:32
  18.3 107.4 %all-gather.3.cloned.1.call-start = ((), (), s32[]{:S(2)}) async-start(), calls=%async_computation.4 | async-start | bytes 11141120 | tf_op jit(solution)/shard_map/all_gather | solution.py:42
  36.5 136.5 %all-gather.5.cloned.1.call-start = ((), (), s32[]{:S(2)}) async-start(), calls=%async_computation.5 | async-start | bytes 8912896 | tf_op jit(solution)/shard_map/all_gather | solution.py:45
  48.7 29.4 %all-to-all-start.2 = ((bf16[16,64,384]{2,1,0:T(8,128)(2,1)}), bf16[16,64,384]{2,1,0:T(8,128)(2,1)S(1)}, u32[]{:S(2)}, u32[]{:S(2)}) async-start(bf16[16,64,384]{2,1,0:T(8,128)(2,1)} %broadcast_in_dim.63), calls=%async_computation.2 | async-start | bytes 1572864 | tf_op jit(solution)/shard_map/all_to_all | solution.py:38
  107.9 11.8 %copy-start = (f32[2,1024]{1,0:T(2,128)S(1)}, f32[2,1024]{1,0:T(2,128)}, u32[]{:S(2)}) copy-start(f32[2,1024]{1,0:T(2,128)} %param.14) | copy-start | bytes 24580
  107.9 11.8 %copy-start.1 = (f32[2,1024]{1,0:T(2,128)S(1)}, f32[2,1024]{1,0:T(2,128)}, u32[]{:S(2)}) copy-start(f32[2,1024]{1,0:T(2,128)} %param.15) | copy-start | bytes 24580
  115.2 21.9 %all-to-all-start.3 = ((bf16[8,8,64,128]{3,2,1,0:T(8,128)(2,1)}), bf16[8,8,64,128]{3,2,1,0:T(8,128)(2,1)}, u32[]{:S(2)}, u32[]{:S(2)}) async-start(bf16[8,8,64,128]{3,2,1,0:T(8,128)(2,1)} %bitcast.102), calls=%async_computation.3 | async-start | bytes 2097152 | tf_op jit(solution)/shard_map/all_to_all | solution.py:84
Sparse Core Ops, SparseCore 0:
  36.6 70.7 all-gather.2
  109.1 62.4 all-gather.4

commit v7 on v4

--- a/solution.py
+++ b/solution.py
@@ -1,8 +1,12 @@
 import math
+
+import functools
 
 import jax
 import jax.numpy as jnp
 from jax import lax
+from jax.experimental import pallas as pl
+from jax.experimental.pallas import tpu as pltpu
 from jax.sharding import PartitionSpec as P
 
 DH = 64
@@ -16,6 +20,49 @@
     center = values - jnp.mean(values, axis=-1, keepdims=True)
     spread = jnp.mean(center * center, axis=-1, keepdims=True)
     return center * lax.rsqrt(spread + EPSILON) * gain + shift
+
+
+def exchange_kernel(n, x_ref, y_ref, send_sems, recv_sems, local_sem):
+    me = lax.axis_index("head")
+    s = lax.axis_index("seq")
+    mesh_ids = pl.DeviceIdType.MESH
+    barrier = pltpu.get_barrier_semaphore()
+    for j in range(1, n):
+        pl.semaphore_signal(barrier, inc=1, device_id=(s, lax.rem(me + j, n)),
+                            device_id_type=mesh_ids)
+    pl.semaphore_wait(barrier, n - 1)
+    local = pltpu.make_async_copy(x_ref.at[me], y_ref.at[me], local_sem)
+    local.start()
+    copies = []
+    for j in range(1, n):
+        peer = lax.rem(me + j, n)
+        copy = pltpu.make_async_remote_copy(
+            src_ref=x_ref.at[peer], dst_ref=y_ref.at[me],
+            send_sem=send_sems.at[j], recv_sem=recv_sems.at[j],
+            device_id=(s, peer), device_id_type=mesh_ids)
+        copy.start()
+        copies.append(copy)
+    local.wait()
+    for j in range(1, n):
+        origin = lax.rem(me + n - j, n)
+        copies[j - 1].wait_send()
+        incoming = pltpu.make_async_remote_copy(
+            src_ref=x_ref.at[origin], dst_ref=y_ref.at[origin],
+            send_sem=send_sems.at[j], recv_sem=recv_sems.at[j],
+            device_id=(s, origin), device_id_type=mesh_ids)
+        incoming.wait_recv()
+
+
+def exchange(x, n):
+    return pl.pallas_call(
+        functools.partial(exchange_kernel, n),
+        out_shape=jax.ShapeDtypeStruct(x.shape, x.dtype),
+        in_specs=[pl.BlockSpec(memory_space=pl.ANY)],
+        out_specs=pl.BlockSpec(memory_space=pl.ANY),
+        scratch_shapes=[pltpu.SemaphoreType.DMA((n,)), pltpu.SemaphoreType.DMA((n,)),
+                        pltpu.SemaphoreType.DMA(())],
+        compiler_params=pltpu.CompilerParams(collective_id=0, has_side_effects=True),
+    )(x)
 
 
 def regroup_weights(attn_in, attn_out, mlp_in, mlp_out, heads_axis, seq_axis):
@@ -79,7 +126,7 @@
     key_cache = jnp.where(inside[:, :, None], key_part, jnp.zeros_like(key_part))
     value_cache = jnp.where(inside[:, :, None], value_part, jnp.zeros_like(value_part))
     context_blocks = jnp.transpose(context, (1, 0, 2, 3))
-    context_blocks = lax.all_to_all(context_blocks, "head", 0, 0, tiled=True)
+    context_blocks = exchange(context_blocks, heads_axis)
     proj_blocks = proj_weight_t.reshape(model_width, heads_axis, block_width)
     attn_blocks = jnp.einsum(
         "sprf,esf->spre", context_blocks, proj_blocks, preferred_element_type=jnp.float32

time: 184 us -> 189 us (1.027)
  Pallas kernels: 0 us -> 15.8 us
  waiting for transfers between devices: 27.9 us -> 21.2 us
  starting transfers between devices: 12.2 us -> 7.82 us
    pallas_call x0 -> x1, Pallas kernels: none -> 15.8 us  [exchange(): pl.pallas_call(functools.partial(exchange_kernel, n), out_shape=jax.Shape...]
    all_to_all x1 -> x0, waiting for transfers between devices: 5.07 us -> none  [encode_chunk(): context_blocks = lax.all_to_all(context_blocks, 'head', 0, 0, tiled=True)]
    all_to_all x1 -> x0, starting transfers between devices: 4.43 us -> none  [encode_chunk(): context_blocks = lax.all_to_all(context_blocks, 'head', 0, 0, tiled=True)]
    unnamed x8 -> x10, local copies, waits for them, and re-layouts: 4.53 us -> 4.63 us
  transfers between devices with their start and end apart: 4 -> 3, of which waited for: 3 -> 1; matrix products, arithmetic and copies ran while one was open for 47% -> 46% of each run, Pallas kernels for 0% -> 8%
where the time goes in v7:
time: 189 us; the launch traced here: 187 us
  matrix products  64.4 us (34%)
  blocking collectives  24.8 us (13%)
  local copies, waits for them, and re-layouts  24.5 us (13%)
  waiting for transfers between devices  21.2 us (11%)
  Pallas kernels  15.8 us (8%)
  between operations  14.2 us (8%)
  other arithmetic  13.9 us (7%)
  starting transfers between devices  7.82 us (4%)
    all_to_all x1, blocking collectives, regroup_weights(): packed = lax.all_to_all(packed, 'head', 1, 0, tiled=True)  24.8 us
    dot_general x1, matrix products, encode_chunk(): jnp.einsum('pld,df->plf', normed_rows, up_weight, preferred_element_type=...  23.9 us
    all_to_all x1, waiting for transfers between devices, regroup_weights(): qkv_weight = lax.all_to_all(in_part, 'seq', 0, 0, tiled=True)  21.2 us
    pallas_call x1, Pallas kernels, exchange(): pl.pallas_call(functools.partial(exchange_kernel, n), out_shape=jax.Shape...  15.8 us
    sub x1, matrix products, encode_chunk(): raised = jnp.exp(scores - row_peak)  10.8 us
    unnamed x1, matrix products  9.23 us
    dot_general x1, matrix products, encode_chunk(): jnp.einsum('phqk,pkhd->pqhd', weights, value_heads, preferred_element_typ...  9.01 us
    all_to_all x1, starting transfers between devices, regroup_weights(): qkv_weight = lax.all_to_all(in_part, 'seq', 0, 0, tiled=True)  7.74 us
  transfers between devices with their start and end apart: 3, of which 1 were waited for; matrix products, arithmetic and copies ran while one was open for 46% of the time, Pallas kernels for 8%

profile of v7, /device:TPU:1, one launch (start us, length us, event | category | flops | bytes accessed | tf_op | source)
XLA Modules:
  0.0 186.7 jit_solution(12048936543387745400)
XLA Ops:
  7.2 0.0 copy-start.3
  7.2 0.0 copy-start.1
  7.2 0.0 copy-start.2
  7.2 0.0 all-gather.3.cloned.1.call-start
  7.2 0.9 convert_bitcast_fusion.1
  8.2 0.9 convert_element_type.59
  9.1 0.8 convert_bitcast_fusion.3
  9.8 0.9 copy_bitcast_fusion.1
  10.7 0.1 broadcast_in_dim.36
  10.8 0.1 pad_maximum_fusion
  10.9 24.8 %all_to_all.20 = bf16[8,8,9600]{2,0,1:T(8,128)(2,1)S(1)} all-to-all(bf16[8,8,9600]{2,0,1:T(8,128)(2,1)S(1)} %pad_maximum_fusion), channel_id=1, replica_groups=mesh['seq'=16,'head'=8] {'head'}, dimensions={1} | all-to-all | bytes 2457600 | tf_op jit(solution)/shard_map/all_to_all | solution.py:80
  35.7 0.9 slice.52
  36.6 0.0 all-gather.3.cloned.1.call-update
  36.7 0.0 all-gather.5.cloned.1.call-start
  36.7 0.8 slice.54
  37.5 0.0 all-gather.5.cloned.1.call-update
  37.6 1.0 broadcast_in_dim.37
  38.6 7.7 %all-to-all-start.1 = ((bf16[16,64,384]{2,1,0:T(8,128)(2,1)}), bf16[16,64,384]{2,1,0:T(8,128)(2,1)S(1)}, u32[]{:S(2)}, u32[]{:S(2)}) async-start(bf16[16,64,384]{2,1,0:T(8,128)(2,1)} %broadcast_in_dim.37), calls=%async_computation.1 | async-start | bytes 1572864 | tf_op jit(solution)/shard_map/all_to_all | solution.py:84
  46.3 0.0 copy-done.3
  46.3 0.1 iota_compare_fusion
  46.4 0.1 constant_dynamic-slice_fusion
  46.5 0.0 copy-done.1
  46.5 0.0 copy-done.2
  46.5 21.2 %all-to-all-done.1 = bf16[16,64,384]{2,1,0:T(8,128)(2,1)S(1)} async-done(((bf16[16,64,384]{2,1,0:T(8,128)(2,1)}), bf16[16,64,384]{2,1,0:T(8,128)(2,1)S(1)}, u32[]{:S(2)}, u32[]{:S(2)}) %all-to-all-start.1) | async-done | bytes 786464 | tf_op jit(solution)/shard_map/all_to_all | solution.py:84
  67.7 1.1 reshape.102
  68.7 7.4 %convert_bitcast_fusion = bf16[8,512,3,128]{1,3,0,2:T(8,128)(2,1)S(1)} fusion(bf16[8,512,1024]{2,1,0:T(8,128)(2,1)} %param.8, bf16[1024,3,128,1]{2,1,0,3:T(4,128)(2,1)} %bitcast.95), kind=kOutput, calls=%fused_computation.39 | convolution fusion | flops 3222798336 | bytes 12320768 | tf_op jit(solution)/shard_map/pld,dte->plte/dot_general | solution.py:105
  76.1 1.8 fusion.37
  77.9 10.8 %fusion.40 = (f32[8,2,512]{2,1,0:T(2,128)S(1)}, f32[8,2,512,512]{2,3,1,0:T(8,128)}) fusion(pred[8,512]{1,0:T(8,128)(4,1)S(1)} %iota_compare_fusion, bf16[8,512,2,64]{1,3,2,0:T(8,128)(2,1)} %bitcast.98, bf16[8,512,2,64]{1,3,2,0:T(8,128)(2,1)} %bitcast.97), kind=kOutput, calls=%fused_computation.71 | convolution fusion | flops 553648640 | bytes 18911232 | tf_op jit(solution)/shard_map/sub | solution.py:120
  88.7 9.0 %fusion.31 = bf16[8,512,2,64]{1,3,2,0:T(8,128)(2,1)} fusion(bf16[8,512,2,64]{1,3,2,0:T(8,128)(2,1)} %bitcast.96, f32[8,2,512,512]{2,3,1,0:T(8,128)} %get-tuple-element.19, f32[8,2,512]{2,1,0:T(2,128)S(1)} %get-tuple-element.18), kind=kOutput, calls=%fused_computation.48 | convolution fusion | flops 545783808 | bytes 18907136 | tf_op jit(solution)/shard_map/phqk,pkhd->pqhd/dot_general | solution.py:122
  97.7 3.9 %reshape.103 = bf16[8,8,64,128]{2,1,3,0:T(8,128)(2,1)} reshape(bf16[8,512,2,64]{1,3,2,0:T(8,128)(2,1)} %fusion.31) | data formatting | bytes 2097152 | tf_op jit(solution)/shard_map/reshape | solution.py:125
  101.7 3.3 %copy.21 = bf16[8,8,64,128]{3,2,0,1:T(8,128)(2,1)} copy(bf16[8,8,64,128]{2,1,3,0:T(8,128)(2,1)} %reshape.103) | data formatting | bytes 2097152 | tf_op jit(solution)/shard_map/reshape | solution.py:125
  105.0 15.8 %shard_map.103 = bf16[8,8,64,128]{3,2,1,0:T(8,128)(2,1)} custom-call(bf16[8,8,64,128]{3,2,1,0:T(8,128)(2,1)} %bitcast.91), custom_call_target="tpu_custom_call" | custom-call | tf_op jit(solution)/shard_map/pallas_call | solution.py:57
  120.8 1.5 bitcast_select_fusion
  122.3 0.0 copy-start
  122.3 2.4 %copy.26 = bf16[8,512,128]{2,1,0:T(8,128)(2,1)} copy(bf16[8,512,128]{1,2,0:T(8,128)(2,1)} %get-tuple-element.10) | data formatting | bytes 2097152
  124.6 2.3 %copy.27 = bf16[8,512,128]{2,1,0:T(8,128)(2,1)} copy(bf16[8,512,128]{1,2,0:T(8,128)(2,1)} %get-tuple-element.9) | data formatting | bytes 2097152
  126.9 0.0 all-gather.3.cloned.1.call-done
  126.9 1.8 slice.53
  128.7 2.6 %copy.22 = bf16[1024,1024]{0,1:T(8,128)(2,1)} copy(bf16[1024,1024]{1,0:T(8,128)(2,1)S(1)} %slice.53) | data formatting | bytes 4194304 | tf_op jit(solution)/shard_map/slice | solution.py:88
  131.2 0.0 copy-done
  131.2 4.1 %convert_reduce_fusion.1 = f32[8,64,1024]{2,1,0:T(8,128)S(1)} fusion(bf16[8,8,64,128]{3,2,1,0:T(8,128)(2,1)S(1)} %copy-done, bf16[1024,8,128,1]{0,2,3,1:T(8,128)(2,1)} %bitcast.94), kind=kOutput, calls=%fused_computation.3 | convolution fusion | flops 1085800448 | bytes 5242880 | tf_op jit(solution)/shard_map/sprf,esf->spre/dot_general | solution.py:131
  135.3 1.6 fusion.34
  136.9 1.7 multiply_reduce_fusion.1
  138.6 1.7 add_convert_fusion
  140.4 23.9 %fusion.4 = bf16[8,64,4096]{2,1,0:T(8,128)(2,1)S(1)} fusion(bf16[8,64,1024]{2,1,0:T(8,128)(2,1)S(1)} %add_convert_fusion, bf16[1024,5120]{1,0:T(8,128)(2,1)} %all-gather.3.cloned.1.call-done), kind=kOutput, calls=%fused_computation.11 | convolution fusion | flops 4431282176 | bytes 13631488 | tf_op jit(solution)/shard_map/pld,df->plf/dot_general | solution.py:140
  164.2 2.5 %copy.49 = bf16[8,8,8,8,512]{4,3,1,0,2:T(8,128)(2,1)} copy(bf16[8,8,8,8,512]{4,3,2,1,0:T(8,128)(2,1)S(1)} %bitcast.93) | data formatting | bytes 8388608 | tf_op jit(solution)/shard_map/reshape | solution.py:143
  166.8 0.0 all-gather.5.cloned.1.call-done
  166.8 9.2 %convert_reduce_fusion = f32[1024,8,64]{0,2,1:T(8,128)S(1)} fusion(bf16[8,512,512]{1,2,0:T(8,128)(2,1)} %bitcast.92, bf16[128,8,8,512]{3,2,1,0:T(8,128)(2,1)} %bitcast.103), kind=kOutput, calls=%fused_computation.2 | convolution fusion | flops 4307025920 | bytes 14680064
  176.0 0.3 fusion.32
  176.3 0.4 multiply_reduce_fusion
  176.8 3.1 %select_convert_fusion = bf16[8,64,1024]{2,1,0:T(8,128)(2,1)} fusion(f32[1024]{0:T(1024)S(1)} %bitcast.100, f32[1024]{0:T(1024)S(1)} %bitcast.99, f32[8,64]{1,0:T(8,128)S(1)} %add_rsqrt_fusion, f32[8,64]{1,0:T(8,128)S(1)} %broadcast_multiply_fusion, pred[8,64]{1,0:T(8,128)(4,1)S(1)} %constant_dynamic-slice_fusion, f32[1024,8,64]{0,2,1:T(8,128)S(1)} %convert_reduce_fusion, ...), kind=kLoop, calls=%fused_computation.41 | loop fusion | flops 4194304 | bytes 4207104 | tf_op jit(solution)/shard_map/convert_element_type | solution.py:151
  (8 shorter events, 0.1 us)
Async XLA Ops:
  7.2 39.1 %copy-start.3 = (s32[8]{0:T(128)S(1)}, s32[8]{0:T(128)}, u32[]{:S(2)}) copy-start(s32[8]{0:T(128)} %param.9) | copy-start | bytes 100
  7.2 39.3 %copy-start.1 = (f32[2,1024]{1,0:T(2,128)S(1)}, f32[2,1024]{1,0:T(2,128)}, u32[]{:S(2)}) copy-start(f32[2,1024]{1,0:T(2,128)} %param.14) | copy-start | bytes 24580
  7.2 39.3 %copy-start.2 = (f32[2,1024]{1,0:T(2,128)S(1)}, f32[2,1024]{1,0:T(2,128)}, u32[]{:S(2)}) copy-start(f32[2,1024]{1,0:T(2,128)} %param.15) | copy-start | bytes 24580
  7.2 119.7 %all-gather.3.cloned.1.call-start = ((), (), s32[]{:S(2)}) async-start(), calls=%async_computation.2 | async-start | bytes 11141120 | tf_op jit(solution)/shard_map/all_gather | solution.py:87
  36.7 130.1 %all-gather.5.cloned.1.call-start = ((), (), s32[]{:S(2)}) async-start(), calls=%async_computation.3 | async-start | bytes 8912896 | tf_op jit(solution)/shard_map/all_gather | solution.py:90
  38.6 29.1 %all-to-all-start.1 = ((bf16[16,64,384]{2,1,0:T(8,128)(2,1)}), bf16[16,64,384]{2,1,0:T(8,128)(2,1)S(1)}, u32[]{:S(2)}, u32[]{:S(2)}) async-start(bf16[16,64,384]{2,1,0:T(8,128)(2,1)} %broadcast_in_dim.37), calls=%async_computation.1 | async-start | bytes 1572864 | tf_op jit(solution)/shard_map/all_to_all | solution.py:84
  122.3 9.0 %copy-start = (bf16[8,8,64,128]{3,2,1,0:T(8,128)(2,1)S(1)}, bf16[8,8,64,128]{3,2,1,0:T(8,128)(2,1)}, u32[]{:S(2)}) copy-start(bf16[8,8,64,128]{3,2,1,0:T(8,128)(2,1)} %shard_map.103) | copy-start | bytes 3145732
Sparse Core Ops, SparseCore 0:
  36.8 71.3 all-gather.2
  109.9 51.8 all-gather.4

commit v8 on v4

--- a/solution.py
+++ b/solution.py
@@ -40,7 +40,10 @@
     early = lax.all_gather(packed[:, 3 * block_width:early_end], "seq", axis=0, tiled=True)
     proj_weight_t = early[:, :model_width]
     up_weight = early[:, model_width:]
-    down_weight_t = lax.all_gather(packed[:, early_end:], "seq", axis=0, tiled=True)
+    half = hidden_width // 2
+    down_weight_t = tuple(
+        lax.all_gather(packed[:, lower:lower + half], "seq", axis=0, tiled=True)
+        for lower in (early_end, early_end + half))
     return qkv_weight, proj_weight_t, up_weight, down_weight_t
 
 
@@ -93,12 +96,19 @@
         jnp.einsum("pld,df->plf", normed_rows, up_weight, preferred_element_type=jnp.float32),
         approximate=False,
     ).astype(jnp.bfloat16)
-    hidden = hidden.reshape(prompts, row_count, heads_axis, hidden_block)
-    down_blocks = down_weight_t.reshape(model_width, heads_axis, hidden_block)
-    mlp_blocks = jnp.einsum(
-        "plbf,ebf->plbe", hidden, down_blocks, preferred_element_type=jnp.float32
-    ).astype(jnp.bfloat16)
-    mlp_rows = jnp.sum(mlp_blocks.astype(jnp.float32), axis=2)
+    half_blocks = heads_axis // 2
+    hidden = hidden.reshape(prompts, row_count, 2, half_blocks, hidden_block)
+    mlp_rows = None
+    for part, down_half in enumerate(down_weight_t):
+        if mlp_rows is not None:
+            mlp_rows, down_half = lax.optimization_barrier((mlp_rows, down_half))
+        half_blocks_out = jnp.einsum(
+            "plbf,ebf->plbe", hidden[:, :, part],
+            down_half.reshape(model_width, half_blocks, hidden_block),
+            preferred_element_type=jnp.float32,
+        ).astype(jnp.bfloat16)
+        half_rows = jnp.sum(half_blocks_out.astype(jnp.float32), axis=2)
+        mlp_rows = half_rows if mlp_rows is None else mlp_rows + half_rows
     finished = layer_norm(normed_rows.astype(jnp.float32) + mlp_rows, norm_gain[1], norm_shift[1])
     inside_rows = lax.dynamic_slice_in_dim(inside, row_start, row_count, 1)
     encoded = jnp.where(inside_rows[:, :, None], finished, 0.0).astype(jnp.bfloat16)

time: 184 us -> 203 us (1.10)
  local copies, waits for them, and re-layouts: 24.4 us -> 35.6 us
  waiting for transfers between devices: 27.9 us -> 34.3 us
  matrix products: 64.7 us -> 68 us
    all_gather x1 -> x2, waiting for transfers between devices: 1.52 us -> 8.24 us  [regroup_weights(): lax.all_gather(packed[:, lower:lower + half], 'seq', axis=0, tiled=True)]
    reshape x1, local copies, waits for them, and re-layouts: 2.54 us -> 7.92 us  [encode_chunk(): hidden = hidden.reshape(prompts, row_count, 2, half_blocks, hidden_block)]
    slice x3 -> x4, local copies, waits for them, and re-layouts: 0.83 us -> 4.17 us  [the longest x1 3.28 us: encode_chunk(): hidden[:, :, part]]
    unnamed x1 -> x2, matrix products: 9.23 us -> 11.7 us
    unnamed x8 -> x12, local copies, waits for them, and re-layouts: 4.53 us -> 6.81 us
  transfers between devices with their start and end apart: 4 -> 5, of which waited for: 3 -> 3; matrix products, arithmetic and copies ran while one was open for 47% -> 51% of each run, Pallas kernels for 0% -> 0%
where the time goes in v8:
time: 203 us; the launch traced here: 202 us
  matrix products  68 us (33%)
  local copies, waits for them, and re-layouts  35.6 us (18%)
  waiting for transfers between devices  34.3 us (17%)
  blocking collectives  24.8 us (12%)
  between operations  13.9 us (7%)
  other arithmetic  13.5 us (7%)
  starting transfers between devices  12.3 us (6%)
    all_to_all x1, blocking collectives, regroup_weights(): packed = lax.all_to_all(packed, 'head', 1, 0, tiled=True)  24.8 us
    dot_general x1, matrix products, encode_chunk(): jnp.einsum('pld,df->plf', normed_rows, up_weight, preferred_element_type=...  24.6 us
    all_to_all x1, waiting for transfers between devices, regroup_weights(): qkv_weight = lax.all_to_all(in_part, 'seq', 0, 0, tiled=True)  21.2 us
    unnamed x2, matrix products  11.7 us
    sub x1, matrix products, encode_chunk(): raised = jnp.exp(scores - row_peak)  10.8 us
    dot_general x1, matrix products, encode_chunk(): jnp.einsum('phqk,pkhd->pqhd', weights, value_heads, preferred_element_typ...  9.02 us
    all_gather x2, waiting for transfers between devices, regroup_weights(): lax.all_gather(packed[:, lower:lower + half], 'seq', axis=0, tiled=True)  8.24 us
    reshape x1, local copies, waits for them, and re-layouts, encode_chunk(): hidden = hidden.reshape(prompts, row_count, 2, half_blocks, hidden_block)  7.92 us
  transfers between devices with their start and end apart: 5, of which 3 were waited for; matrix products, arithmetic and copies ran while one was open for 51% of the time, Pallas kernels for 0%

profile of v8, /device:TPU:1, one launch (start us, length us, event | category | flops | bytes accessed | tf_op | source)
XLA Modules:
  0.0 202.4 jit_solution(2688375529795258058)
XLA Ops:
  7.2 0.0 copy-start.3
  7.2 0.0 all-gather.4.cloned.1.call-start
  7.2 0.9 convert_bitcast_fusion.1
  8.1 0.9 convert_element_type.67
  9.0 0.8 convert_bitcast_fusion.3
  9.8 0.9 copy_bitcast_fusion
  10.7 0.1 broadcast_in_dim.36
  10.8 0.1 pad_maximum_fusion
  10.9 24.8 %all_to_all.25 = bf16[8,8,9600]{2,0,1:T(8,128)(2,1)S(1)} all-to-all(bf16[8,8,9600]{2,0,1:T(8,128)(2,1)S(1)} %pad_maximum_fusion), channel_id=1, replica_groups=mesh['seq'=16,'head'=8] {'head'}, dimensions={1} | all-to-all | bytes 2457600 | tf_op jit(solution)/shard_map/all_to_all | solution.py:33
  35.7 0.9 slice.64
  36.6 0.0 all-gather.4.cloned.1.call-update
  36.6 0.0 all-gather.6.cloned.1.call-start
  36.7 0.9 fusion.48
  37.6 0.0 all-gather.6.cloned.1.call-update
  37.6 1.0 broadcast_in_dim.37
  38.6 7.7 %all-to-all-start.1 = ((bf16[16,64,384]{2,1,0:T(8,128)(2,1)}), bf16[16,64,384]{2,1,0:T(8,128)(2,1)S(1)}, u32[]{:S(2)}, u32[]{:S(2)}) async-start(bf16[16,64,384]{2,1,0:T(8,128)(2,1)} %broadcast_in_dim.37), calls=%async_computation.1 | async-start | bytes 1572864 | tf_op jit(solution)/shard_map/all_to_all | solution.py:37
  46.3 0.0 copy-done.3
  46.3 0.1 iota_compare_fusion
  46.4 21.2 %all-to-all-done.1 = bf16[16,64,384]{2,1,0:T(8,128)(2,1)S(1)} async-done(((bf16[16,64,384]{2,1,0:T(8,128)(2,1)}), bf16[16,64,384]{2,1,0:T(8,128)(2,1)S(1)}, u32[]{:S(2)}, u32[]{:S(2)}) %all-to-all-start.1) | async-done | bytes 786464 | tf_op jit(solution)/shard_map/all_to_all | solution.py:37
  67.6 1.1 reshape.105
  68.7 7.4 %convert_bitcast_fusion = bf16[8,512,3,128]{1,3,0,2:T(8,128)(2,1)S(1)} fusion(bf16[8,512,1024]{2,1,0:T(8,128)(2,1)} %param.8, bf16[1024,3,128,1]{2,1,0,3:T(4,128)(2,1)} %bitcast.110), kind=kOutput, calls=%fused_computation.43 | convolution fusion | flops 3222798336 | bytes 12320768 | tf_op jit(solution)/shard_map/pld,dte->plte/dot_general | solution.py:61
  76.1 1.8 fusion.47
  77.9 10.8 %fusion.51 = (f32[8,2,512]{2,1,0:T(2,128)S(1)}, f32[8,2,512,512]{2,3,1,0:T(8,128)}) fusion(pred[8,512]{1,0:T(8,128)(4,1)S(1)} %iota_compare_fusion, bf16[8,512,2,64]{1,3,2,0:T(8,128)(2,1)} %bitcast.113, bf16[8,512,2,64]{1,3,2,0:T(8,128)(2,1)} %bitcast.112), kind=kOutput, calls=%fused_computation.78 | convolution fusion | flops 553648640 | bytes 18911232 | tf_op jit(solution)/shard_map/sub | solution.py:76
  88.7 9.0 %fusion.35 = bf16[8,512,2,64]{1,3,2,0:T(8,128)(2,1)} fusion(bf16[8,512,2,64]{1,3,2,0:T(8,128)(2,1)} %bitcast.111, f32[8,2,512,512]{2,3,1,0:T(8,128)} %get-tuple-element.29, f32[8,2,512]{2,1,0:T(2,128)S(1)} %get-tuple-element.28), kind=kOutput, calls=%fused_computation.53 | convolution fusion | flops 545783808 | bytes 18907136 | tf_op jit(solution)/shard_map/phqk,pkhd->pqhd/dot_general | solution.py:78
  97.7 0.0 copy-start.1
  97.7 0.0 copy-start.2
  97.7 4.0 %reshape.106 = bf16[8,8,64,128]{2,1,3,0:T(8,128)(2,1)} reshape(bf16[8,512,2,64]{1,3,2,0:T(8,128)(2,1)} %fusion.35) | data formatting | bytes 2097152 | tf_op jit(solution)/shard_map/reshape | solution.py:81
  101.7 3.3 %copy.24 = bf16[8,8,64,128]{3,2,0,1:T(8,128)(2,1)} copy(bf16[8,8,64,128]{2,1,3,0:T(8,128)(2,1)} %reshape.106) | data formatting | bytes 2097152 | tf_op jit(solution)/shard_map/reshape | solution.py:81
  105.0 4.2 %all-to-all-start.2 = ((bf16[8,8,64,128]{3,2,1,0:T(8,128)(2,1)}), bf16[8,8,64,128]{3,2,1,0:T(8,128)(2,1)}, u32[]{:S(2)}, u32[]{:S(2)}) async-start(bf16[8,8,64,128]{3,2,1,0:T(8,128)(2,1)} %bitcast.105), calls=%async_computation.2 | async-start | bytes 2097152 | tf_op jit(solution)/shard_map/all_to_all | solution.py:85
  109.2 0.2 all-gather.8.cloned.1.call-start
  109.5 0.1 constant_dynamic-slice_fusion
  109.6 0.0 copy-done.1
  109.6 0.0 copy-done.2
  109.6 0.4 all-gather.8.cloned.1.call-update
  110.0 1.5 bitcast_select_fusion
  111.4 2.3 %copy.31 = bf16[8,512,128]{2,1,0:T(8,128)(2,1)} copy(bf16[8,512,128]{1,2,0:T(8,128)(2,1)} %get-tuple-element.18) | data formatting | bytes 2097152
  113.7 2.3 %copy.32 = bf16[8,512,128]{2,1,0:T(8,128)(2,1)} copy(bf16[8,512,128]{1,2,0:T(8,128)(2,1)} %get-tuple-element.17) | data formatting | bytes 2097152
  116.0 0.0 all-gather.4.cloned.1.call-done
  116.0 1.9 slice.65
  117.9 2.6 %copy.25 = bf16[1024,1024]{0,1:T(8,128)(2,1)} copy(bf16[1024,1024]{1,0:T(8,128)(2,1)S(1)} %slice.65) | data formatting | bytes 4194304 | tf_op jit(solution)/shard_map/slice | solution.py:41
  120.5 4.4 %all-to-all-done.2 = bf16[8,8,64,128]{3,2,1,0:T(8,128)(2,1)} async-done(((bf16[8,8,64,128]{3,2,1,0:T(8,128)(2,1)}), bf16[8,8,64,128]{3,2,1,0:T(8,128)(2,1)}, u32[]{:S(2)}, u32[]{:S(2)}) %all-to-all-start.2) | async-done | bytes 1048608 | tf_op jit(solution)/shard_map/all_to_all | solution.py:85
  124.9 4.4 %convert_reduce_fusion = f32[8,64,1024]{2,1,0:T(8,128)S(1)} fusion(bf16[8,8,64,128]{3,2,1,0:T(8,128)(2,1)} %all-to-all-done.2, bf16[1024,8,128,1]{0,2,3,1:T(8,128)(2,1)} %bitcast.107), kind=kOutput, calls=%fused_computation.1 | convolution fusion | flops 1085800448 | bytes 5242880 | tf_op jit(solution)/shard_map/sprf,esf->spre/dot_general | solution.py:87
  129.3 1.6 fusion.41
  130.9 1.7 multiply_reduce_fusion.1
  132.7 1.7 add_convert_fusion
  134.4 24.6 %fusion.4 = bf16[8,64,4096]{2,1,0:T(8,128)(2,1)} fusion(bf16[8,64,1024]{2,1,0:T(8,128)(2,1)S(1)} %add_convert_fusion, bf16[1024,5120]{1,0:T(8,128)(2,1)} %all-gather.4.cloned.1.call-done), kind=kOutput, calls=%fused_computation.9 | convolution fusion | flops 4431282176 | bytes 13631488 | tf_op jit(solution)/shard_map/pld,df->plf/dot_general | solution.py:96
  159.1 7.9 %reshape.109 = bf16[8,64,2,4,512]{4,3,2,1,0:T(4,128)(2,1)} reshape(bf16[8,64,4096]{2,1,0:T(8,128)(2,1)} %fusion.4) | data formatting | bytes 8388608 | tf_op jit(solution)/shard_map/reshape | solution.py:100
  167.0 3.3 %fusion.46 = (bf16[8,64,1,4,512]{4,3,2,1,0:T(4,128)(2,1)S(1)}, bf16[8,64,1,4,512]{4,3,2,1,0:T(4,128)(2,1)S(1)}) fusion(bf16[8,64,2,4,512]{4,3,2,1,0:T(4,128)(2,1)} %reshape.109), kind=kLoop, calls=%fused_computation.73 | loop fusion | bytes 8388608 | tf_op jit(solution)/shard_map/slice | solution.py:106
  170.3 1.8 copy.40
  172.1 0.0 all-gather.6.cloned.1.call-done
  172.1 6.8 %convert_reduce_fusion.2 = f32[1024,8,64]{0,2,1:T(8,128)} fusion(bf16[4,512,512]{1,2,0:T(8,128)(2,1)} %bitcast.108, bf16[128,4,8,512]{3,2,1,0:T(8,128)(2,1)} %bitcast.118), kind=kOutput, calls=%fused_computation.17 | convolution fusion | flops 2153250816 | bytes 8388608
  178.9 8.2 %all-gather.8.cloned.1.call-done = bf16[1024,2048]{1,0:T(8,128)(2,1)} async-done(((bf16[64,2048]{1,0:T(8,128)(2,1)}), bf16[1024,2048]{1,0:T(8,128)(2,1)}) %all-gather.8.cloned.1.call-update) | async-done | bytes 4194320 | tf_op jit(solution)/shard_map/all_gather | solution.py:45
  187.1 0.5 copy.41
  187.6 0.0 copy-start
  187.6 4.9 %convert_reduce_fusion.1 = f32[1024,8,64]{0,2,1:T(8,128)S(1)} fusion(bf16[4,512,512]{1,2,0:T(8,128)(2,1)S(1)} %bitcast.109, bf16[128,4,8,512]{3,2,1,0:T(8,128)(2,1)} %bitcast.119), kind=kOutput, calls=%fused_computation.16 | convolution fusion | flops 2153250816 | bytes 8388608
  192.5 0.0 copy-done
  192.5 0.4 fusion.44
  193.0 0.3 multiply_reduce_fusion
  193.3 2.6 %select_convert_fusion = bf16[8,64,1024]{2,1,0:T(8,128)(2,1)} fusion(f32[8,64,1024]{2,1,0:T(8,128)S(1)} %get-tuple-element.14, f32[1024]{0:T(1024)S(1)} %bitcast.115, f32[1024]{0:T(1024)S(1)} %bitcast.114, f32[8,64]{1,0:T(8,128)S(1)} %add_rsqrt_fusion, f32[8,64]{1,0:T(8,128)S(1)} %broadcast_multiply_fusion, pred[8,64]{1,0:T(8,128)(4,1)S(1)} %constant_dynamic-slice_fusion), kind=kLoop, calls=%fused_computation.46 | loop fusion | flops 3145728 | bytes 3158528 | tf_op jit(solution)/shard_map/convert_element_type | solution.py:114
  (8 shorter events, 0.1 us)
Async XLA Ops:
  7.2 39.2 %copy-start.3 = (s32[8]{0:T(128)S(1)}, s32[8]{0:T(128)}, u32[]{:S(2)}) copy-start(s32[8]{0:T(128)} %param.9) | copy-start | bytes 100
  7.2 108.8 %all-gather.4.cloned.1.call-start = ((), (), s32[]{:S(2)}) async-start(), calls=%async_computation.3 | async-start | bytes 11141120 | tf_op jit(solution)/shard_map/all_gather | solution.py:40
  36.6 135.5 %all-gather.6.cloned.1.call-start = ((), (), s32[]{:S(2)}) async-start(), calls=%async_computation.4 | async-start | bytes 4456448 | tf_op jit(solution)/shard_map/all_gather | solution.py:45
  38.6 29.0 %all-to-all-start.1 = ((bf16[16,64,384]{2,1,0:T(8,128)(2,1)}), bf16[16,64,384]{2,1,0:T(8,128)(2,1)S(1)}, u32[]{:S(2)}, u32[]{:S(2)}) async-start(bf16[16,64,384]{2,1,0:T(8,128)(2,1)} %broadcast_in_dim.37), calls=%async_computation.1 | async-start | bytes 1572864 | tf_op jit(solution)/shard_map/all_to_all | solution.py:37
  97.7 11.9 %copy-start.1 = (f32[2,1024]{1,0:T(2,128)S(1)}, f32[2,1024]{1,0:T(2,128)}, u32[]{:S(2)}) copy-start(f32[2,1024]{1,0:T(2,128)} %param.14) | copy-start | bytes 24580
  97.7 11.9 %copy-start.2 = (f32[2,1024]{1,0:T(2,128)S(1)}, f32[2,1024]{1,0:T(2,128)}, u32[]{:S(2)}) copy-start(f32[2,1024]{1,0:T(2,128)} %param.15) | copy-start | bytes 24580
  105.0 19.9 %all-to-all-start.2 = ((bf16[8,8,64,128]{3,2,1,0:T(8,128)(2,1)}), bf16[8,8,64,128]{3,2,1,0:T(8,128)(2,1)}, u32[]{:S(2)}, u32[]{:S(2)}) async-start(bf16[8,8,64,128]{3,2,1,0:T(8,128)(2,1)} %bitcast.105), calls=%async_computation.2 | async-start | bytes 2097152 | tf_op jit(solution)/shard_map/all_to_all | solution.py:85
  109.2 77.9 %all-gather.8.cloned.1.call-start = ((), (), s32[]{:S(2)}) async-start(), calls=%async_computation.5 | async-start | bytes 4456448 | tf_op jit(solution)/shard_map/all_gather | solution.py:45
  187.6 4.9 %copy-start = (f32[1024,8,64]{0,2,1:T(8,128)S(1)}, f32[1024,8,64]{0,2,1:T(8,128)}, u32[]{:S(2)}) copy-start(f32[1024,8,64]{0,2,1:T(8,128)} %convert_reduce_fusion.2) | copy-start | bytes 6291460
Sparse Core Ops, SparseCore 0:
  36.8 71.0 all-gather.3
  109.6 38.0 all-gather.5
  149.4 37.7 all-gather.7

commit v9 on v4

--- a/solution.py
+++ b/solution.py
@@ -16,6 +16,22 @@
     center = values - jnp.mean(values, axis=-1, keepdims=True)
     spread = jnp.mean(center * center, axis=-1, keepdims=True)
     return center * lax.rsqrt(spread + EPSILON) * gain + shift
+
+
+def pair_gather(part, seq_axis):
+    core = lax.axis_index("seq") % 2
+    low_first = core == 0
+    pairs = [(index, index ^ 1) for index in range(seq_axis)]
+    groups = [[index for index in range(seq_axis) if index % 2 == side] for side in range(2)]
+    half = part.shape[1] // 2
+    other = lax.ppermute(part, "seq", pairs)
+    both = jnp.where(low_first, jnp.concatenate([part, other], 0),
+                     jnp.concatenate([other, part], 0))
+    mine = lax.dynamic_slice_in_dim(both, core * half, half, 1)
+    got = lax.all_gather(mine, "seq", axis=0, tiled=True, axis_index_groups=groups)
+    theirs = lax.ppermute(got, "seq", pairs)
+    return jnp.where(low_first, jnp.concatenate([got, theirs], 1),
+                     jnp.concatenate([theirs, got], 1))
 
 
 def regroup_weights(attn_in, attn_out, mlp_in, mlp_out, heads_axis, seq_axis):
@@ -37,10 +53,10 @@
     qkv_weight = lax.all_to_all(in_part, "seq", 0, 0, tiled=True)
     qkv_weight = qkv_weight.reshape(-1, 3, block_width)
     early_end = 3 * block_width + model_width + hidden_width
-    early = lax.all_gather(packed[:, 3 * block_width:early_end], "seq", axis=0, tiled=True)
+    early = pair_gather(packed[:, 3 * block_width:early_end], seq_axis)
     proj_weight_t = early[:, :model_width]
     up_weight = early[:, model_width:]
-    down_weight_t = lax.all_gather(packed[:, early_end:], "seq", axis=0, tiled=True)
+    down_weight_t = pair_gather(packed[:, early_end:], seq_axis)
     return qkv_weight, proj_weight_t, up_weight, down_weight_t
 
 

time: 184 us -> 380 us (2.07)
  waiting for transfers between devices: 27.9 us -> 200 us
  local copies, waits for them, and re-layouts: 24.4 us -> 36.3 us
  other arithmetic: 14 us -> 23.6 us
  starting transfers between devices: 12.2 us -> 16.7 us
    all_gather x2, waiting for transfers between devices: 1.52 us -> 196 us  [pair_gather(): lax.all_gather(mine, 'seq', axis=0, tiled=True, axis_index_groups=groups)]
    all_to_all x1, waiting for transfers between devices: 21.3 us -> 0.01 us  [regroup_weights(): qkv_weight = lax.all_to_all(in_part, 'seq', 0, 0, tiled=True)]
    select_n x0 -> x3, other arithmetic: none -> 9.67 us  [the longest x1 7.82 us: pair_gather(): jnp.where(low_first, jnp.concatenate([got, theirs], 1), jnp.concatenate([...]
    concatenate x0 -> x2, local copies, waits for them, and re-layouts: none -> 9.53 us  [pair_gather(): jnp.concatenate([got, theirs], 1)]
    all_to_all x1, waiting for transfers between devices: 5.07 us -> 0.01 us  [encode_chunk(): context_blocks = lax.all_to_all(context_blocks, 'head', 0, 0, tiled=True)]
    ppermute x0 -> x4, starting transfers between devices: none -> 4.62 us  [the longest x2 2.83 us: pair_gather(): other = lax.ppermute(part, 'seq', pairs)]
    unnamed x8 -> x22, local copies, waits for them, and re-layouts: 4.53 us -> 8.51 us
  transfers between devices with their start and end apart: 4 -> 8, of which waited for: 3 -> 4; matrix products, arithmetic and copies ran while one was open for 47% -> 18% of each run, Pallas kernels for 0% -> 0%
where the time goes in v9:
time: 380 us; the launch traced here: 379 us
  waiting for transfers between devices  200 us (53%)
  matrix products  63.9 us (17%)
  local copies, waits for them, and re-layouts  36.3 us (10%)
  blocking collectives  24.8 us (7%)
  other arithmetic  23.6 us (6%)
  starting transfers between devices  16.7 us (4%)
  between operations  14.3 us (4%)
    all_gather x2, waiting for transfers between devices, pair_gather(): lax.all_gather(mine, 'seq', axis=0, tiled=True, axis_index_groups=groups)  196 us
    all_to_all x1, blocking collectives, regroup_weights(): packed = lax.all_to_all(packed, 'head', 1, 0, tiled=True)  24.8 us
    dot_general x1, matrix products, encode_chunk(): jnp.einsum('pld,df->plf', normed_rows, up_weight, preferred_element_type=...  22.5 us
    sub x1, matrix products, encode_chunk(): raised = jnp.exp(scores - row_peak)  10.7 us
    unnamed x1, matrix products  10.3 us
    concatenate x2, local copies, waits for them, and re-layouts, pair_gather(): jnp.concatenate([got, theirs], 1)  9.53 us
    dot_general x1, matrix products, encode_chunk(): jnp.einsum('phqk,pkhd->pqhd', weights, value_heads, preferred_element_typ...  8.67 us
    unnamed x22, local copies, waits for them, and re-layouts  8.51 us
  transfers between devices with their start and end apart: 8, of which 4 were waited for; matrix products, arithmetic and copies ran while one was open for 18% of the time, Pallas kernels for 0%

profile of v9, /device:TPU:1, one launch (start us, length us, event | category | flops | bytes accessed | tf_op | source)
XLA Modules:
  0.0 379.3 jit_solution(1541772664587803355)
XLA Ops:
  7.2 0.0 copy-start.7
  7.2 0.0 all-gather.3.cloned.1.call-start
  7.2 0.9 convert_bitcast_fusion.1
  8.2 0.9 convert_element_type.59
  9.1 0.8 convert_bitcast_fusion.3
  9.8 0.9 copy_bitcast_fusion.3
  10.7 0.1 broadcast_in_dim.36
  10.8 0.1 pad_maximum_fusion
  10.9 24.8 %all_to_all.25 = bf16[8,8,9600]{2,0,1:T(8,128)(2,1)S(1)} all-to-all(bf16[8,8,9600]{2,0,1:T(8,128)(2,1)S(1)} %pad_maximum_fusion), channel_id=1, replica_groups=mesh['seq'=16,'head'=8] {'head'}, dimensions={1} | all-to-all | bytes 2457600 | tf_op jit(solution)/shard_map/all_to_all | solution.py:49
  35.8 2.4 collective-permute-start
  38.2 1.7 collective-permute-done
  39.9 0.9 fusion.35
  40.8 0.0 all-gather.3.cloned.1.call-update
  40.9 0.0 all-gather.5.cloned.1.call-start
  41.0 0.5 collective-permute-start.2
  41.4 1.5 collective-permute-done.2
  43.0 0.9 fusion.39
  43.9 0.0 all-gather.5.cloned.1.call-update
  43.9 1.0 broadcast_in_dim.37
  44.9 5.8 %all-to-all-start.1 = ((bf16[16,64,384]{2,1,0:T(8,128)(2,1)}), bf16[16,64,384]{2,1,0:T(8,128)(2,1)S(1)}, u32[]{:S(2)}, u32[]{:S(2)}) async-start(bf16[16,64,384]{2,1,0:T(8,128)(2,1)} %broadcast_in_dim.37), calls=%async_computation.1 | async-start | bytes 1572864 | tf_op jit(solution)/shard_map/all_to_all | solution.py:53
  50.7 107.1 %all-gather.3.cloned.1.call-done = bf16[1024,2560]{1,0:T(8,128)(2,1)} async-done(((bf16[128,2560]{1,0:T(8,128)(2,1)}), bf16[1024,2560]{1,0:T(8,128)(2,1)}) %all-gather.3.cloned.1.call-update) | async-done | bytes 5242896 | tf_op jit(solution)/shard_map/all_gather | solution.py:31
  157.8 0.9 collective-permute-start.1
  158.7 0.1 iota_compare_fusion
  158.7 0.7 constant_dynamic-slice_fusion
  159.4 0.6 fusion.46
  160.0 0.6 fusion.45
  160.6 0.0 all-to-all-done.1
  160.6 1.1 reshape.104
  161.7 89.4 %all-gather.5.cloned.1.call-done = bf16[1024,2048]{1,0:T(8,128)(2,1)} async-done(((bf16[128,2048]{1,0:T(8,128)(2,1)}), bf16[1024,2048]{1,0:T(8,128)(2,1)}) %all-gather.5.cloned.1.call-update) | async-done | bytes 4194320 | tf_op jit(solution)/shard_map/all_gather | solution.py:31
  251.1 0.9 collective-permute-start.3
  252.0 7.2 %convert_bitcast_fusion = bf16[8,512,3,128]{1,3,0,2:T(8,128)(2,1)S(1)} fusion(bf16[8,512,1024]{2,1,0:T(8,128)(2,1)} %param.8, bf16[1024,3,128,1]{2,1,0,3:T(4,128)(2,1)} %bitcast.100), kind=kOutput, calls=%fused_computation.47 | convolution fusion | flops 3222798336 | bytes 12320768 | tf_op jit(solution)/shard_map/pld,dte->plte/dot_general | solution.py:74
  259.2 1.8 fusion.44
  261.0 10.7 %fusion.47 = (f32[8,2,512]{2,1,0:T(2,128)S(1)}, f32[8,2,512,512]{2,3,1,0:T(8,128)}) fusion(pred[8,512]{1,0:T(8,128)(4,1)S(1)} %iota_compare_fusion, bf16[8,512,2,64]{1,3,2,0:T(8,128)(2,1)} %bitcast.103, bf16[8,512,2,64]{1,3,2,0:T(8,128)(2,1)} %bitcast.102), kind=kOutput, calls=%fused_computation.94 | convolution fusion | flops 553648640 | bytes 18911232 | tf_op jit(solution)/shard_map/sub | solution.py:89
  271.7 8.7 %fusion.31 = bf16[8,512,2,64]{1,3,2,0:T(8,128)(2,1)} fusion(bf16[8,512,2,64]{1,3,2,0:T(8,128)(2,1)} %bitcast.101, f32[8,2,512,512]{2,3,1,0:T(8,128)} %get-tuple-element.19, f32[8,2,512]{2,1,0:T(2,128)S(1)} %get-tuple-element.18), kind=kOutput, calls=%fused_computation.56 | convolution fusion | flops 545783808 | bytes 18907136 | tf_op jit(solution)/shard_map/phqk,pkhd->pqhd/dot_general | solution.py:91
  280.4 3.9 %reshape.105 = bf16[8,8,64,128]{2,1,3,0:T(8,128)(2,1)} reshape(bf16[8,512,2,64]{1,3,2,0:T(8,128)(2,1)} %fusion.31) | data formatting | bytes 2097152 | tf_op jit(solution)/shard_map/reshape | solution.py:94
  284.3 3.3 copy.25
  287.6 6.1 %all-to-all-start.2 = ((bf16[8,8,64,128]{3,2,1,0:T(8,128)(2,1)}), bf16[8,8,64,128]{3,2,1,0:T(8,128)(2,1)}, u32[]{:S(2)}, u32[]{:S(2)}) async-start(bf16[8,8,64,128]{3,2,1,0:T(8,128)(2,1)} %bitcast.93), calls=%async_computation.2 | async-start | bytes 2097152 | tf_op jit(solution)/shard_map/all_to_all | solution.py:98
  293.7 1.5 bitcast_select_fusion
  295.2 2.3 copy.33
  297.5 2.3 copy.34
  299.7 4.8 %copy.53 = bf16[128,4,8,512]{3,2,0,1:T(8,128)(2,1)} copy(bf16[128,4,8,512]{3,2,1,0:T(8,128)(2,1)} %bitcast.94) | data formatting | bytes 8388608 | tf_op jit(solution)/shard_map/concatenate | solution.py:33
  304.5 0.0 collective-permute-done.3
  304.5 4.7 %copy.52 = bf16[128,4,8,512]{3,2,0,1:T(8,128)(2,1)} copy(bf16[128,4,8,512]{3,2,1,0:T(8,128)(2,1)} %bitcast.38) | data formatting | bytes 8388608 | tf_op jit(solution)/shard_map/concatenate | solution.py:33
  309.3 0.0 collective-permute-done.1
  309.3 0.0 slice-done.1
  309.3 7.8 %maximum_select_fusion = bf16[1024,5120]{1,0:T(8,128)(2,1)S(1)} fusion(bf16[1024,2560]{1,0:T(8,128)(2,1)} %collective-permute-done.1, bf16[1024,2560]{1,0:T(8,128)(2,1)S(1)} %bitcast.89, pred[]{:T(512)S(6)} %eq.7), kind=kLoop, calls=%fused_computation.9 | loop fusion | flops 47185920 | bytes 20971520 | tf_op jit(solution)/shard_map/jit(_where)/select_n | solution.py:33
  317.1 0.0 copy-start
  317.1 4.0 %copy-done = bf16[1024,5120]{1,0:T(8,128)(2,1)} copy-done((bf16[1024,5120]{1,0:T(8,128)(2,1)}, bf16[1024,5120]{1,0:T(8,128)(2,1)S(1)}, u32[]{:S(2)}) %copy-start) | copy-done | bytes 10485784
  321.1 0.2 slice.53
  321.2 2.6 copy.26
  323.8 0.0 all-to-all-done.2
  323.8 4.5 %convert_reduce_fusion.1 = f32[8,64,1024]{2,1,0:T(8,128)S(1)} fusion(bf16[8,8,64,128]{3,2,1,0:T(8,128)(2,1)} %all-to-all-done.2, bf16[1024,8,128,1]{0,2,3,1:T(8,128)(2,1)} %bitcast.99), kind=kOutput, calls=%fused_computation.3 | convolution fusion | flops 1085800448 | bytes 5242880 | tf_op jit(solution)/shard_map/sprf,esf->spre/dot_general | solution.py:100
  328.3 1.5 fusion.37
  329.9 1.7 multiply_reduce_fusion.1
  331.6 1.7 add_convert_fusion
  333.4 22.5 %fusion.4 = bf16[8,64,4096]{2,1,0:T(8,128)(2,1)S(1)} fusion(bf16[8,64,1024]{2,1,0:T(8,128)(2,1)S(1)} %add_convert_fusion, bf16[1024,5120]{1,0:T(8,128)(2,1)S(1)} %copy-done.1), kind=kOutput, calls=%fused_computation.12 | convolution fusion | flops 4431282176 | bytes 13631488 | tf_op jit(solution)/shard_map/pld,df->plf/dot_general | solution.py:109
  355.9 2.4 copy.51
  358.4 10.3 %convert_reduce_fusion = f32[1024,8,64]{0,2,1:T(8,128)S(1)} fusion(bf16[8,512,512]{1,2,0:T(8,128)(2,1)} %bitcast.97, bf16[1024,4,512]{2,0,1:T(8,128)(2,1)} %bitcast.96, bf16[1024,4,512]{2,0,1:T(8,128)(2,1)} %bitcast.95, pred[]{:T(512)S(6)} %eq.7), kind=kOutput, calls=%fused_computation.2 | convolution fusion | flops 4319608832 | bytes 14680065
  368.7 0.3 fusion.32
  369.0 0.4 multiply_reduce_fusion
  369.4 0.0 copy-done.2
  369.4 0.0 copy-done.3
  369.4 0.0 copy-done.6
  369.4 3.1 select_convert_fusion
  (22 shorter events, 0.1 us)
Async XLA Ops:
  7.2 151.5 %copy-start.7 = (s32[8]{0:T(128)S(1)}, s32[8]{0:T(128)}, u32[]{:S(2)}) copy-start(s32[8]{0:T(128)} %param.9) | copy-start | bytes 100
  7.2 152.2 %copy-start.4 = (f32[2,1024]{1,0:T(2,128)S(1)}, f32[2,1024]{1,0:T(2,128)}, u32[]{:S(2)}) copy-start(f32[2,1024]{1,0:T(2,128)} %param.15) | copy-start | bytes 24580
  7.2 152.8 %copy-start.5 = (f32[2,1024]{1,0:T(2,128)S(1)}, f32[2,1024]{1,0:T(2,128)}, u32[]{:S(2)}) copy-start(f32[2,1024]{1,0:T(2,128)} %param.14) | copy-start | bytes 24580
  7.2 150.6 %all-gather.3.cloned.1.call-start = ((), (), s32[]{:S(2)}) async-start(), calls=%async_computation.3 | async-start | bytes 5898240 | tf_op jit(solution)/shard_map/all_gather | solution.py:31
  35.8 4.1 %collective-permute-start = (bf16[64,5120]{1,0:T(8,128)(2,1)S(1)}, bf16[64,5120]{1,0:T(8,128)(2,1)S(1)}, u32[]{:S(2)}, u32[]{:S(2)}) collective-permute-start(bf16[64,5120]{1,0:T(8,128)(2,1)S(1)} %slice.52), channel_id=1, source_target_pairs={{0,8},{8,0},{16,24},{24,16},{32,40},{40,32},{48,56},{56,48},{64,72... | collective-permute-start | bytes 1966088 | tf_op jit(solution)/shard_map/ppermute | solution.py:27
  40.9 210.2 %all-gather.5.cloned.1.call-start = ((), (), s32[]{:S(2)}) async-start(), calls=%async_computation.4 | async-start | bytes 4718592 | tf_op jit(solution)/shard_map/all_gather | solution.py:31
  41.0 2.0 collective-permute-start.2
  44.9 115.7 %all-to-all-start.1 = ((bf16[16,64,384]{2,1,0:T(8,128)(2,1)}), bf16[16,64,384]{2,1,0:T(8,128)(2,1)S(1)}, u32[]{:S(2)}, u32[]{:S(2)}) async-start(bf16[16,64,384]{2,1,0:T(8,128)(2,1)} %broadcast_in_dim.37), calls=%async_computation.1 | async-start | bytes 1572864 | tf_op jit(solution)/shard_map/all_to_all | solution.py:53
  157.8 151.5 %collective-permute-start.1 = (bf16[1024,2560]{1,0:T(8,128)(2,1)}, bf16[1024,2560]{1,0:T(8,128)(2,1)}, u32[]{:S(2)}, u32[]{:S(2)}) collective-permute-start(bf16[1024,2560]{1,0:T(8,128)(2,1)} %all-gather.3.cloned.1.call-done), channel_id=1, source_target_pairs={{0,8},{8,0},{16,24},{24,16},{32,40},{40,32},{48,56},{56,48},{64,72... | collective-permute-start | bytes 15728648 | tf_op jit(solution)/shard_map/ppermute | solution.py:32
  251.1 53.4 %collective-permute-start.3 = (bf16[1024,2048]{1,0:T(8,128)(2,1)}, bf16[1024,2048]{1,0:T(8,128)(2,1)}, u32[]{:S(2)}, u32[]{:S(2)}) collective-permute-start(bf16[1024,2048]{1,0:T(8,128)(2,1)} %all-gather.5.cloned.1.call-done), channel_id=1, source_target_pairs={{0,8},{8,0},{16,24},{24,16},{32,40},{40,32},{48,56},{56,48},{64,72... | collective-permute-start | bytes 12582920 | tf_op jit(solution)/shard_map/ppermute | solution.py:32
  287.6 36.2 %all-to-all-start.2 = ((bf16[8,8,64,128]{3,2,1,0:T(8,128)(2,1)}), bf16[8,8,64,128]{3,2,1,0:T(8,128)(2,1)}, u32[]{:S(2)}, u32[]{:S(2)}) async-start(bf16[8,8,64,128]{3,2,1,0:T(8,128)(2,1)} %bitcast.93), calls=%async_computation.2 | async-start | bytes 2097152 | tf_op jit(solution)/shard_map/all_to_all | solution.py:98
  299.7 9.5 %slice-start = ((s8[5242880]{0:T(1024)(128)(4,1)}), s8[4194304]{0:T(1024)(128)(4,1)S(1)}, s32[]{:S(2)}) async-start(s8[5242880]{0:T(1024)(128)(4,1)} %bitcast.88), calls=%async_computation.5 | async-start | bytes 8388608
  304.5 4.7 %slice-start.1 = ((s8[5242880]{0:T(1024)(128)(4,1)}), s8[1048576]{0:T(1024)(128)(4,1)S(1)}, s32[]{:S(2)}) async-start(s8[5242880]{0:T(1024)(128)(4,1)} %bitcast.88), calls=%async_computation.6 | async-start | bytes 2097152
  317.1 4.0 %copy-start = (bf16[1024,5120]{1,0:T(8,128)(2,1)}, bf16[1024,5120]{1,0:T(8,128)(2,1)S(1)}, u32[]{:S(2)}) copy-start(bf16[1024,5120]{1,0:T(8,128)(2,1)S(1)} %maximum_select_fusion) | copy-start | bytes 31457284
  323.8 9.5 %copy-start.1 = (bf16[1024,5120]{1,0:T(8,128)(2,1)S(1)}, bf16[1024,5120]{1,0:T(8,128)(2,1)}, u32[]{:S(2)}) copy-start(bf16[1024,5120]{1,0:T(8,128)(2,1)} %copy-done) | copy-start | bytes 31457284
  358.3 11.1 %copy-start.2 = (f32[1,1024]{1,0:T(1,128)S(1)}, f32[1,1024]{1,0:T(1,128)}, u32[]{:S(2)}) copy-start(f32[1,1024]{1,0:T(1,128)} %get-tuple-element.17) | copy-start | bytes 12292
  358.3 11.1 %copy-start.3 = (f32[1,1024]{1,0:T(1,128)S(1)}, f32[1,1024]{1,0:T(1,128)}, u32[]{:S(2)}) copy-start(f32[1,1024]{1,0:T(1,128)} %get-tuple-element.15) | copy-start | bytes 12292
  358.4 11.1 %copy-start.6 = (pred[8,64]{1,0:T(8,128)(4,1)S(1)}, pred[8,64]{1,0:T(8,128)(4,1)}, u32[]{:S(2)}) copy-start(pred[8,64]{1,0:T(8,128)(4,1)} %constant_dynamic-slice_fusion) | copy-start | bytes 1540
Sparse Core Ops, SparseCore 0:
  41.0 116.7 all-gather.2
  160.0 91.0 all-gather.4

commit v10 on v4

--- a/solution.py
+++ b/solution.py
@@ -26,8 +26,7 @@
     in_piece = attn_in.astype(jnp.bfloat16).reshape(rows, 3, heads_axis, block_width)
     in_piece = jnp.transpose(in_piece, (0, 2, 1, 3)).reshape(rows, heads_axis, 3 * block_width)
     whole_rows = jnp.concatenate(
-        [attn_out.astype(jnp.bfloat16).T, mlp_in.astype(jnp.bfloat16),
-         mlp_out.astype(jnp.bfloat16).T], axis=1)
+        [mlp_in.astype(jnp.bfloat16), mlp_out.astype(jnp.bfloat16).T], axis=1)
     whole_piece = jnp.broadcast_to(whole_rows[:, None], (rows, heads_axis, whole_rows.shape[1]))
     packed = jnp.concatenate([in_piece, whole_piece], axis=2)
     packed = lax.all_to_all(packed, "head", 1, 0, tiled=True)
@@ -36,11 +35,15 @@
     in_part = jnp.broadcast_to(in_part[None], (seq_axis,) + in_part.shape)
     qkv_weight = lax.all_to_all(in_part, "seq", 0, 0, tiled=True)
     qkv_weight = qkv_weight.reshape(-1, 3, block_width)
-    early_end = 3 * block_width + model_width + hidden_width
-    early = lax.all_gather(packed[:, 3 * block_width:early_end], "seq", axis=0, tiled=True)
-    proj_weight_t = early[:, :model_width]
-    up_weight = early[:, model_width:]
-    down_weight_t = lax.all_gather(packed[:, early_end:], "seq", axis=0, tiled=True)
+    up_end = 3 * block_width + hidden_width
+    up_weight = lax.all_gather(packed[:, 3 * block_width:up_end], "seq", axis=0, tiled=True)
+    down_weight_t = lax.all_gather(packed[:, up_end:], "seq", axis=0, tiled=True)
+    out_rows = attn_out.astype(jnp.bfloat16).T
+    out_rows = jnp.broadcast_to(out_rows[None], (seq_axis,) + out_rows.shape)
+    out_rows = lax.all_to_all(out_rows, "seq", 0, 0, tiled=True)
+    out_rows = jnp.broadcast_to(out_rows[None], (heads_axis,) + out_rows.shape)
+    out_rows = lax.all_to_all(out_rows, "head", 0, 0, tiled=True)
+    proj_weight_t = jnp.transpose(out_rows, (1, 0, 2, 3)).reshape(-1, model_width)
     return qkv_weight, proj_weight_t, up_weight, down_weight_t
 
 

time: 184 us -> 205 us (1.11)
  waiting for transfers between devices: 27.9 us -> 41.7 us
  starting transfers between devices: 12.2 us -> 22.8 us
    all_to_all x0 -> x2, starting transfers between devices: none -> 12 us  [the longest x1 7.7 us: regroup_weights(): out_rows = lax.all_to_all(out_rows, 'seq', 0, 0, tiled=True)]
    all_to_all x0 -> x2, waiting for transfers between devices: none -> 10.1 us  [the longest x1 10.1 us: regroup_weights(): out_rows = lax.all_to_all(out_rows, 'seq', 0, 0, tiled=True)]
    slice x4 -> x1, local copies, waits for them, and re-layouts: 6.05 us -> 1.1 us  [regroup_weights(): packed[:, up_end:]]
    all_to_all x1, waiting for transfers between devices: 5.07 us -> 9.22 us  [encode_chunk(): context_blocks = lax.all_to_all(context_blocks, 'head', 0, 0, tiled=True)]
    all_to_all x1, starting transfers between devices: 7.74 us -> 4.18 us  [regroup_weights(): qkv_weight = lax.all_to_all(in_part, 'seq', 0, 0, tiled=True)]
    broadcast_in_dim x0 -> x2, local copies, waits for them, and re-layouts: none -> 2.35 us  [the longest x1 1.62 us: regroup_weights(): out_rows = jnp.broadcast_to(out_rows[None], (heads_axis,) + out_rows.shape)]
    all_to_all x1, starting transfers between devices: 4.43 us -> 6.53 us  [encode_chunk(): context_blocks = lax.all_to_all(context_blocks, 'head', 0, 0, tiled=True)]
    unnamed x8 -> x11, local copies, waits for them, and re-layouts: 4.53 us -> 5.15 us
  transfers between devices with their start and end apart: 4 -> 6, of which waited for: 3 -> 3; matrix products, arithmetic and copies ran while one was open for 47% -> 41% of each run, Pallas kernels for 0% -> 0%
where the time goes in v10:
time: 205 us; the launch traced here: 203 us
  matrix products  63.5 us (31%)
  waiting for transfers between devices  41.7 us (20%)
  local copies, waits for them, and re-layouts  24.2 us (12%)
  blocking collectives  23.9 us (12%)
  starting transfers between devices  22.8 us (11%)
  between operations  14.2 us (7%)
  other arithmetic  13.1 us (6%)
    all_to_all x1, blocking collectives, regroup_weights(): packed = lax.all_to_all(packed, 'head', 1, 0, tiled=True)  23.9 us
    dot_general x1, matrix products, encode_chunk(): jnp.einsum('pld,df->plf', normed_rows, up_weight, preferred_element_type=...  23.9 us
    all_to_all x1, waiting for transfers between devices, regroup_weights(): qkv_weight = lax.all_to_all(in_part, 'seq', 0, 0, tiled=True)  21.6 us
    sub x1, matrix products, encode_chunk(): raised = jnp.exp(scores - row_peak)  10.7 us
    all_to_all x1, waiting for transfers between devices, regroup_weights(): out_rows = lax.all_to_all(out_rows, 'seq', 0, 0, tiled=True)  10.1 us
    unnamed x1, matrix products  9.23 us
    all_to_all x1, waiting for transfers between devices, encode_chunk(): context_blocks = lax.all_to_all(context_blocks, 'head', 0, 0, tiled=True)  9.22 us
    dot_general x1, matrix products, encode_chunk(): jnp.einsum('phqk,pkhd->pqhd', weights, value_heads, preferred_element_typ...  8.74 us
  transfers between devices with their start and end apart: 6, of which 3 were waited for; matrix products, arithmetic and copies ran while one was open for 41% of the time, Pallas kernels for 0%

profile of v10, /device:TPU:1, one launch (start us, length us, event | category | flops | bytes accessed | tf_op | source)
XLA Modules:
  0.0 203.4 jit_solution(6423954190132051730)
XLA Ops:
  7.2 0.0 copy-start
  7.2 0.0 copy-start.3
  7.2 0.0 all-gather.5.cloned.1.call-start
  7.2 0.9 convert_bitcast_fusion.1
  8.1 0.9 convert_element_type.58
  9.1 0.9 copy_bitcast_fusion.1
  10.0 0.1 broadcast_in_dim.40
  10.0 0.1 pad_maximum_fusion
  10.1 23.9 %all_to_all.35 = bf16[8,8,8576]{2,0,1:T(8,128)(2,1)S(1)} all-to-all(bf16[8,8,8576]{2,0,1:T(8,128)(2,1)S(1)} %pad_maximum_fusion), channel_id=1, replica_groups=mesh['seq'=16,'head'=8] {'head'}, dimensions={1} | all-to-all | bytes 2195456 | tf_op jit(solution)/shard_map/all_to_all | solution.py:32
  34.0 1.1 fusion.40
  35.1 0.0 all-gather.5.cloned.1.call-update
  35.2 0.0 all-gather.3.cloned.1.call-start
  35.2 0.7 all-gather.3.cloned.1.call-update
  35.9 0.0 copy-done
  35.9 0.7 broadcast_in_dim.44
  36.7 7.7 %all-to-all-start.3 = ((bf16[16,8,1024]{2,1,0:T(8,128)(2,1)}), bf16[16,8,1024]{2,1,0:T(8,128)(2,1)S(1)}, u32[]{:S(2)}, u32[]{:S(2)}) async-start(bf16[16,8,1024]{2,1,0:T(8,128)(2,1)} %broadcast_in_dim.44), calls=%async_computation.3 | async-start | bytes 524288 | tf_op jit(solution)/shard_map/all_to_all | solution.py:43
  44.4 10.1 %all-to-all-done.3 = bf16[16,8,1024]{2,1,0:T(8,128)(2,1)S(1)} async-done(((bf16[16,8,1024]{2,1,0:T(8,128)(2,1)}), bf16[16,8,1024]{2,1,0:T(8,128)(2,1)S(1)}, u32[]{:S(2)}, u32[]{:S(2)}) %all-to-all-start.3) | async-done | bytes 262176 | tf_op jit(solution)/shard_map/all_to_all | solution.py:43
  54.5 1.0 broadcast_in_dim.41
  55.5 4.2 %all-to-all-start.1 = ((bf16[16,64,384]{2,1,0:T(8,128)(2,1)}), bf16[16,64,384]{2,1,0:T(8,128)(2,1)S(1)}, u32[]{:S(2)}, u32[]{:S(2)}) async-start(bf16[16,64,384]{2,1,0:T(8,128)(2,1)} %broadcast_in_dim.41), calls=%async_computation.1 | async-start | bytes 1572864 | tf_op jit(solution)/shard_map/all_to_all | solution.py:36
  59.7 0.0 copy-done.3
  59.7 0.1 iota_compare_fusion
  59.7 21.6 %all-to-all-done.1 = bf16[16,64,384]{2,1,0:T(8,128)(2,1)S(1)} async-done(((bf16[16,64,384]{2,1,0:T(8,128)(2,1)}), bf16[16,64,384]{2,1,0:T(8,128)(2,1)S(1)}, u32[]{:S(2)}, u32[]{:S(2)}) %all-to-all-start.1) | async-done | bytes 786464 | tf_op jit(solution)/shard_map/all_to_all | solution.py:36
  81.3 1.6 broadcast_in_dim.45
  83.0 4.4 %all-to-all-start.4 = ((bf16[8,16,8,1024]{3,2,1,0:T(8,128)(2,1)}), bf16[8,16,8,1024]{3,2,1,0:T(8,128)(2,1)}, u32[]{:S(2)}, u32[]{:S(2)}) async-start(bf16[8,16,8,1024]{3,2,1,0:T(8,128)(2,1)} %broadcast_in_dim.45), calls=%async_computation.4 | async-start | bytes 4194304 | tf_op jit(solution)/shard_map/all_to_all | solution.py:45
  87.3 1.1 reshape.101
  88.4 7.2 %convert_bitcast_fusion = bf16[8,512,3,128]{1,3,0,2:T(8,128)(2,1)S(1)} fusion(bf16[8,512,1024]{2,1,0:T(8,128)(2,1)} %param.8, bf16[1024,3,128,1]{2,1,0,3:T(4,128)(2,1)} %bitcast.96), kind=kOutput, calls=%fused_computation.39 | convolution fusion | flops 3222798336 | bytes 12320768 | tf_op jit(solution)/shard_map/pld,dte->plte/dot_general | solution.py:61
  95.7 1.8 fusion.39
  97.4 10.7 %fusion.43 = (f32[8,2,512]{2,1,0:T(2,128)S(1)}, f32[8,2,512,512]{2,3,1,0:T(8,128)}) fusion(pred[8,512]{1,0:T(8,128)(4,1)S(1)} %iota_compare_fusion, bf16[8,512,2,64]{1,3,2,0:T(8,128)(2,1)} %bitcast.99, bf16[8,512,2,64]{1,3,2,0:T(8,128)(2,1)} %bitcast.98), kind=kOutput, calls=%fused_computation.73 | convolution fusion | flops 553648640 | bytes 18911232 | tf_op jit(solution)/shard_map/sub | solution.py:76
  108.2 8.7 %fusion.33 = bf16[8,512,2,64]{1,3,2,0:T(8,128)(2,1)} fusion(bf16[8,512,2,64]{1,3,2,0:T(8,128)(2,1)} %bitcast.97, f32[8,2,512,512]{2,3,1,0:T(8,128)} %get-tuple-element.24, f32[8,2,512]{2,1,0:T(2,128)S(1)} %get-tuple-element.23), kind=kOutput, calls=%fused_computation.49 | convolution fusion | flops 545783808 | bytes 18907136 | tf_op jit(solution)/shard_map/phqk,pkhd->pqhd/dot_general | solution.py:78
  116.9 0.0 copy-start.1
  116.9 0.0 copy-start.2
  116.9 3.9 %reshape.102 = bf16[8,8,64,128]{2,1,3,0:T(8,128)(2,1)} reshape(bf16[8,512,2,64]{1,3,2,0:T(8,128)(2,1)} %fusion.33) | data formatting | bytes 2097152 | tf_op jit(solution)/shard_map/reshape | solution.py:81
  120.9 3.3 %copy.31 = bf16[8,8,64,128]{3,2,0,1:T(8,128)(2,1)} copy(bf16[8,8,64,128]{2,1,3,0:T(8,128)(2,1)} %reshape.102) | data formatting | bytes 2097152 | tf_op jit(solution)/shard_map/reshape | solution.py:81
  124.2 0.0 all-to-all-done.4
  124.2 6.5 %all-to-all-start.2 = ((bf16[8,8,64,128]{3,2,1,0:T(8,128)(2,1)}), bf16[8,8,64,128]{3,2,1,0:T(8,128)(2,1)}, u32[]{:S(2)}, u32[]{:S(2)}) async-start(bf16[8,8,64,128]{3,2,1,0:T(8,128)(2,1)} %bitcast.92), calls=%async_computation.2 | async-start | bytes 2097152 | tf_op jit(solution)/shard_map/all_to_all | solution.py:85
  130.7 0.1 constant_dynamic-slice_fusion
  130.8 0.0 copy-done.1
  130.8 0.0 copy-done.2
  130.8 1.5 bitcast_select_fusion
  132.3 2.3 %copy.36 = bf16[8,512,128]{2,1,0:T(8,128)(2,1)} copy(bf16[8,512,128]{1,2,0:T(8,128)(2,1)} %get-tuple-element.13) | data formatting | bytes 2097152
  134.6 2.3 %copy.37 = bf16[8,512,128]{2,1,0:T(8,128)(2,1)} copy(bf16[8,512,128]{1,2,0:T(8,128)(2,1)} %get-tuple-element.12) | data formatting | bytes 2097152
  136.8 1.8 copy.32
  138.6 0.6 copy.47
  139.2 9.2 %all-to-all-done.2 = bf16[8,8,64,128]{3,2,1,0:T(8,128)(2,1)} async-done(((bf16[8,8,64,128]{3,2,1,0:T(8,128)(2,1)}), bf16[8,8,64,128]{3,2,1,0:T(8,128)(2,1)}, u32[]{:S(2)}, u32[]{:S(2)}) %all-to-all-start.2) | async-done | bytes 1048608 | tf_op jit(solution)/shard_map/all_to_all | solution.py:85
  148.4 3.7 %convert_reduce_fusion.1 = f32[8,64,1024]{2,1,0:T(8,128)S(1)} fusion(bf16[8,8,64,128]{3,2,1,0:T(8,128)(2,1)} %all-to-all-done.2, bf16[1024,8,128,1]{2,1,0,3:T(8,128)(2,1)S(1)} %bitcast.95), kind=kOutput, calls=%fused_computation.3 | convolution fusion | flops 1085800448 | bytes 5242880 | tf_op jit(solution)/shard_map/sprf,esf->spre/dot_general | solution.py:87
  152.1 1.5 fusion.36
  153.7 1.7 multiply_reduce_fusion.1
  155.4 1.7 add_convert_fusion
  157.1 0.0 all-gather.5.cloned.1.call-done
  157.1 23.9 %fusion.4 = bf16[8,64,4096]{2,1,0:T(8,128)(2,1)S(1)} fusion(bf16[8,64,1024]{2,1,0:T(8,128)(2,1)S(1)} %add_convert_fusion, bf16[1024,4096]{1,0:T(8,128)(2,1)} %all-gather.5.cloned.1.call-done), kind=kOutput, calls=%fused_computation.11 | convolution fusion | flops 4431282176 | bytes 13631488 | tf_op jit(solution)/shard_map/pld,df->plf/dot_general | solution.py:96
  181.0 2.6 %copy.62 = bf16[8,8,8,8,512]{4,3,1,0,2:T(8,128)(2,1)} copy(bf16[8,8,8,8,512]{4,3,2,1,0:T(8,128)(2,1)S(1)} %bitcast.94) | data formatting | bytes 8388608 | tf_op jit(solution)/shard_map/reshape | solution.py:99
  183.5 0.0 all-gather.3.cloned.1.call-done
  183.5 9.2 %convert_reduce_fusion = f32[1024,8,64]{0,2,1:T(8,128)S(1)} fusion(bf16[8,512,512]{1,2,0:T(8,128)(2,1)} %bitcast.93, bf16[128,8,8,512]{3,2,1,0:T(8,128)(2,1)} %bitcast.104), kind=kOutput, calls=%fused_computation.2 | convolution fusion | flops 4307025920 | bytes 14680064
  192.8 0.3 fusion.34
  193.1 0.4 multiply_reduce_fusion
  193.5 3.1 %select_convert_fusion = bf16[8,64,1024]{2,1,0:T(8,128)(2,1)} fusion(f32[1024]{0:T(1024)S(1)} %bitcast.101, f32[1024]{0:T(1024)S(1)} %bitcast.100, f32[8,64]{1,0:T(8,128)S(1)} %add_rsqrt_fusion, f32[8,64]{1,0:T(8,128)S(1)} %broadcast_multiply_fusion, pred[8,64]{1,0:T(8,128)(4,1)S(1)} %constant_dynamic-slice_fusion, ...), kind=kLoop, calls=%fused_computation.42 | loop fusion | flops 4194304 | bytes 4207104 | tf_op jit(solution)/shard_map/convert_element_type | solution.py:107
  (9 shorter events, 0.1 us)
Async XLA Ops:
  7.2 28.7 %copy-start = (f32[1024,8]{0,1:T(8,128)S(1)}, f32[1024,8]{0,1:T(8,128)}, u32[]{:S(2)}) copy-start(f32[1024,8]{0,1:T(8,128)} %param.11) | copy-start | bytes 98308
  7.2 52.5 %copy-start.3 = (s32[8]{0:T(128)S(1)}, s32[8]{0:T(128)}, u32[]{:S(2)}) copy-start(s32[8]{0:T(128)} %param.9) | copy-start | bytes 100
  7.2 149.9 %all-gather.5.cloned.1.call-start = ((), (), s32[]{:S(2)}) async-start(), calls=%async_computation.6 | async-start | bytes 8912896 | tf_op jit(solution)/shard_map/all_gather | solution.py:39
  35.2 148.4 %all-gather.3.cloned.1.call-start = ((), (), s32[]{:S(2)}) async-start(), calls=%async_computation.5 | async-start | bytes 8912896 | tf_op jit(solution)/shard_map/all_gather | solution.py:40
  36.7 17.8 %all-to-all-start.3 = ((bf16[16,8,1024]{2,1,0:T(8,128)(2,1)}), bf16[16,8,1024]{2,1,0:T(8,128)(2,1)S(1)}, u32[]{:S(2)}, u32[]{:S(2)}) async-start(bf16[16,8,1024]{2,1,0:T(8,128)(2,1)} %broadcast_in_dim.44), calls=%async_computation.3 | async-start | bytes 524288 | tf_op jit(solution)/shard_map/all_to_all | solution.py:43
  55.5 25.9 %all-to-all-start.1 = ((bf16[16,64,384]{2,1,0:T(8,128)(2,1)}), bf16[16,64,384]{2,1,0:T(8,128)(2,1)S(1)}, u32[]{:S(2)}, u32[]{:S(2)}) async-start(bf16[16,64,384]{2,1,0:T(8,128)(2,1)} %broadcast_in_dim.41), calls=%async_computation.1 | async-start | bytes 1572864 | tf_op jit(solution)/shard_map/all_to_all | solution.py:36
  83.0 41.2 %all-to-all-start.4 = ((bf16[8,16,8,1024]{3,2,1,0:T(8,128)(2,1)}), bf16[8,16,8,1024]{3,2,1,0:T(8,128)(2,1)}, u32[]{:S(2)}, u32[]{:S(2)}) async-start(bf16[8,16,8,1024]{3,2,1,0:T(8,128)(2,1)} %broadcast_in_dim.45), calls=%async_computation.4 | async-start | bytes 4194304 | tf_op jit(solution)/shard_map/all_to_all | solution.py:45
  116.9 13.9 %copy-start.1 = (f32[2,1024]{1,0:T(2,128)S(1)}, f32[2,1024]{1,0:T(2,128)}, u32[]{:S(2)}) copy-start(f32[2,1024]{1,0:T(2,128)} %param.14) | copy-start | bytes 24580
  116.9 13.9 %copy-start.2 = (f32[2,1024]{1,0:T(2,128)S(1)}, f32[2,1024]{1,0:T(2,128)}, u32[]{:S(2)}) copy-start(f32[2,1024]{1,0:T(2,128)} %param.15) | copy-start | bytes 24580
  124.2 24.2 %all-to-all-start.2 = ((bf16[8,8,64,128]{3,2,1,0:T(8,128)(2,1)}), bf16[8,8,64,128]{3,2,1,0:T(8,128)(2,1)}, u32[]{:S(2)}, u32[]{:S(2)}) async-start(bf16[8,8,64,128]{3,2,1,0:T(8,128)(2,1)} %bitcast.92), calls=%async_computation.2 | async-start | bytes 2097152 | tf_op jit(solution)/shard_map/all_to_all | solution.py:85
Sparse Core Ops, SparseCore 0:
  35.3 85.8 all-gather.4
  122.9 59.6 all-gather.2

commit v11 on v4

--- a/solution.py
+++ b/solution.py
@@ -81,10 +81,8 @@
     context_blocks = jnp.transpose(context, (1, 0, 2, 3))
     context_blocks = lax.all_to_all(context_blocks, "head", 0, 0, tiled=True)
     proj_blocks = proj_weight_t.reshape(model_width, heads_axis, block_width)
-    attn_blocks = jnp.einsum(
-        "sprf,esf->spre", context_blocks, proj_blocks, preferred_element_type=jnp.float32
-    ).astype(jnp.bfloat16)
-    attn_rows = jnp.sum(attn_blocks.astype(jnp.float32), axis=0)
+    attn_rows = jnp.einsum(
+        "sprf,esf->pre", context_blocks, proj_blocks, preferred_element_type=jnp.float32)
     token_rows = lax.dynamic_slice_in_dim(tokens, row_start, row_count, 1)
     normed_rows = layer_norm(
         token_rows.astype(jnp.float32) + attn_rows, norm_gain[0], norm_shift[0]
@@ -93,12 +91,8 @@
         jnp.einsum("pld,df->plf", normed_rows, up_weight, preferred_element_type=jnp.float32),
         approximate=False,
     ).astype(jnp.bfloat16)
-    hidden = hidden.reshape(prompts, row_count, heads_axis, hidden_block)
-    down_blocks = down_weight_t.reshape(model_width, heads_axis, hidden_block)
-    mlp_blocks = jnp.einsum(
-        "plbf,ebf->plbe", hidden, down_blocks, preferred_element_type=jnp.float32
-    ).astype(jnp.bfloat16)
-    mlp_rows = jnp.sum(mlp_blocks.astype(jnp.float32), axis=2)
+    mlp_rows = jnp.einsum(
+        "plf,ef->ple", hidden, down_weight_t, preferred_element_type=jnp.float32)
     finished = layer_norm(normed_rows.astype(jnp.float32) + mlp_rows, norm_gain[1], norm_shift[1])
     inside_rows = lax.dynamic_slice_in_dim(inside, row_start, row_count, 1)
     encoded = jnp.where(inside_rows[:, :, None], finished, 0.0).astype(jnp.bfloat16)

time: 184 us -> 199 us (1.082)
  waiting for transfers between devices: 27.9 us -> 49.2 us
  other arithmetic: 14 us -> 8.37 us
    dot_general x1 -> x2, matrix products: 4.43 us -> 28.8 us  [the longest x1 25 us: encode_chunk(): jnp.einsum('plf,ef->ple', hidden, down_weight_t, preferred_element_type=j...]
    all_gather x1, waiting for transfers between devices: 1.52 us -> 22.8 us  [regroup_weights(): lax.all_gather(packed[:, early_end:], 'seq', axis=0, tiled=True)]
    dot_general x1, matrix products: 23.8 us -> 9.15 us  [encode_chunk(): jnp.einsum('pld,df->plf', normed_rows, up_weight, preferred_element_type=...]
    unnamed x1 -> x0, matrix products: 9.23 us -> none
    reshape x2 -> x1, local copies, waits for them, and re-layouts: 7.3 us -> 3.97 us  [encode_chunk(): context.astype(jnp.bfloat16)]
    transpose x0 -> x1, local copies, waits for them, and re-layouts: none -> 3.33 us  [encode_chunk(): context_blocks = jnp.transpose(context, (1, 0, 2, 3))]
    reshape x1 -> x0, local copies, waits for them, and re-layouts: 2.54 us -> none  [encode_chunk(): hidden = hidden.reshape(prompts, row_count, heads_axis, hidden_block)]
    unnamed x8 -> x10, local copies, waits for them, and re-layouts: 4.53 us -> 5.93 us
  transfers between devices with their start and end apart: 4 -> 4, of which waited for: 3 -> 3; matrix products, arithmetic and copies ran while one was open for 47% -> 32% of each run, Pallas kernels for 0% -> 0%
where the time goes in v11:
time: 199 us; the launch traced here: 197 us
  matrix products  65.1 us (33%)
  waiting for transfers between devices  49.2 us (25%)
  blocking collectives  24.8 us (12%)
  local copies, waits for them, and re-layouts  23.3 us (12%)
  between operations  14.2 us (7%)
  starting transfers between devices  12.2 us (6%)
  other arithmetic  8.37 us (4%)
    dot_general x1, matrix products, encode_chunk(): jnp.einsum('plf,ef->ple', hidden, down_weight_t, preferred_element_type=j...  25 us
    all_to_all x1, blocking collectives, regroup_weights(): packed = lax.all_to_all(packed, 'head', 1, 0, tiled=True)  24.8 us
    all_gather x1, waiting for transfers between devices, regroup_weights(): lax.all_gather(packed[:, early_end:], 'seq', axis=0, tiled=True)  22.8 us
    all_to_all x1, waiting for transfers between devices, regroup_weights(): qkv_weight = lax.all_to_all(in_part, 'seq', 0, 0, tiled=True)  21.3 us
    sub x1, matrix products, encode_chunk(): raised = jnp.exp(scores - row_peak)  10.8 us
    dot_general x1, matrix products, encode_chunk(): jnp.einsum('pld,df->plf', normed_rows, up_weight, preferred_element_type=...  9.15 us
    dot_general x1, matrix products, encode_chunk(): jnp.einsum('phqk,pkhd->pqhd', weights, value_heads, preferred_element_typ...  9.01 us
    all_to_all x1, starting transfers between devices, regroup_weights(): qkv_weight = lax.all_to_all(in_part, 'seq', 0, 0, tiled=True)  7.74 us
  transfers between devices with their start and end apart: 4, of which 3 were waited for; matrix products, arithmetic and copies ran while one was open for 32% of the time, Pallas kernels for 0%

profile of v11, /device:TPU:1, one launch (start us, length us, event | category | flops | bytes accessed | tf_op | source)
XLA Modules:
  0.0 197.2 jit_solution(14664804762032076210)
XLA Ops:
  7.2 0.0 copy-start.3
  7.2 0.0 all-gather.3.cloned.1.call-start
  7.2 0.9 convert_bitcast_fusion.1
  8.1 0.9 convert_element_type.45
  9.0 0.8 convert_bitcast_fusion.3
  9.8 0.9 copy_bitcast_fusion
  10.7 0.1 broadcast_in_dim.36
  10.8 0.1 pad_maximum_fusion
  10.9 24.8 %all_to_all.25 = bf16[8,8,9600]{2,0,1:T(8,128)(2,1)S(1)} all-to-all(bf16[8,8,9600]{2,0,1:T(8,128)(2,1)S(1)} %pad_maximum_fusion), channel_id=1, replica_groups=mesh['seq'=16,'head'=8] {'head'}, dimensions={1} | all-to-all | bytes 2457600 | tf_op jit(solution)/shard_map/all_to_all | solution.py:33
  35.7 0.9 slice.52
  36.6 0.0 all-gather.3.cloned.1.call-update
  36.6 0.0 all-gather.5.cloned.1.call-start
  36.7 0.8 slice.55
  37.5 0.0 all-gather.5.cloned.1.call-update
  37.6 1.0 broadcast_in_dim.37
  38.5 7.7 %all-to-all-start.1 = ((bf16[16,64,384]{2,1,0:T(8,128)(2,1)}), bf16[16,64,384]{2,1,0:T(8,128)(2,1)S(1)}, u32[]{:S(2)}, u32[]{:S(2)}) async-start(bf16[16,64,384]{2,1,0:T(8,128)(2,1)} %broadcast_in_dim.37), calls=%async_computation.1 | async-start | bytes 1572864 | tf_op jit(solution)/shard_map/all_to_all | solution.py:37
  46.3 0.0 copy-done.3
  46.3 0.1 iota_compare_fusion
  46.4 21.3 %all-to-all-done.1 = bf16[16,64,384]{2,1,0:T(8,128)(2,1)S(1)} async-done(((bf16[16,64,384]{2,1,0:T(8,128)(2,1)}), bf16[16,64,384]{2,1,0:T(8,128)(2,1)S(1)}, u32[]{:S(2)}, u32[]{:S(2)}) %all-to-all-start.1) | async-done | bytes 786464 | tf_op jit(solution)/shard_map/all_to_all | solution.py:37
  67.6 1.1 reshape.96
  68.7 7.4 %convert_bitcast_fusion = bf16[8,512,3,128]{1,3,0,2:T(8,128)(2,1)S(1)} fusion(bf16[8,512,1024]{2,1,0:T(8,128)(2,1)} %param.8, bf16[1024,3,128,1]{2,1,0,3:T(4,128)(2,1)} %bitcast.73), kind=kOutput, calls=%fused_computation.68 | convolution fusion | flops 3222798336 | bytes 12320768 | tf_op jit(solution)/shard_map/pld,dte->plte/dot_general | solution.py:58
  76.1 1.8 fusion.100
  77.9 10.8 %fusion.103 = (f32[8,2,512]{2,1,0:T(2,128)S(1)}, f32[8,2,512,512]{2,3,1,0:T(8,128)}) fusion(pred[8,512]{1,0:T(8,128)(4,1)S(1)} %iota_compare_fusion, bf16[8,512,2,64]{1,3,2,0:T(8,128)(2,1)} %bitcast.76, bf16[8,512,2,64]{1,3,2,0:T(8,128)(2,1)} %bitcast.75), kind=kOutput, calls=%fused_computation.133 | convolution fusion | flops 553648640 | bytes 18911232 | tf_op jit(solution)/shard_map/sub | solution.py:73
  88.7 9.0 %fusion.63 = bf16[8,512,2,64]{1,3,2,0:T(8,128)(2,1)} fusion(bf16[8,512,2,64]{1,3,2,0:T(8,128)(2,1)} %bitcast.74, f32[8,2,512,512]{2,3,1,0:T(8,128)} %get-tuple-element.24, f32[8,2,512]{2,1,0:T(2,128)S(1)} %get-tuple-element.23), kind=kOutput, calls=%fused_computation.79 | convolution fusion | flops 545783808 | bytes 18907136 | tf_op jit(solution)/shard_map/phqk,pkhd->pqhd/dot_general | solution.py:75
  97.7 0.0 copy-start.1
  97.7 0.0 copy-start.2
  97.7 4.0 %reshape.97 = bf16[8,8,64,128]{2,1,3,0:T(8,128)(2,1)} reshape(bf16[8,512,2,64]{1,3,2,0:T(8,128)(2,1)} %fusion.63) | data formatting | bytes 2097152 | tf_op jit(solution)/shard_map/reshape | solution.py:78
  101.7 3.3 %copy.28 = bf16[8,8,64,128]{3,2,1,0:T(8,128)(2,1)} copy(bf16[8,8,64,128]{2,0,3,1:T(8,128)(2,1)} %bitcast.68) | data formatting | bytes 2097152 | tf_op jit(solution)/shard_map/transpose | solution.py:81
  105.0 4.4 %all-to-all-start.2 = ((bf16[8,8,64,128]{3,2,1,0:T(8,128)(2,1)}), bf16[8,8,64,128]{3,2,1,0:T(8,128)(2,1)}, u32[]{:S(2)}, u32[]{:S(2)}) async-start(bf16[8,8,64,128]{3,2,1,0:T(8,128)(2,1)} %copy.28), calls=%async_computation.2 | async-start | bytes 2097152 | tf_op jit(solution)/shard_map/all_to_all | solution.py:82
  109.4 0.1 constant_dynamic-slice_fusion
  109.5 0.0 copy-done.1
  109.5 0.0 copy-done.2
  109.6 1.5 bitcast_select_fusion
  111.0 2.3 %copy.32 = bf16[8,512,128]{2,1,0:T(8,128)(2,1)} copy(bf16[8,512,128]{1,2,0:T(8,128)(2,1)} %get-tuple-element.15) | data formatting | bytes 2097152
  113.3 2.3 %copy.33 = bf16[8,512,128]{2,1,0:T(8,128)(2,1)} copy(bf16[8,512,128]{1,2,0:T(8,128)(2,1)} %get-tuple-element.14) | data formatting | bytes 2097152
  115.5 0.0 all-gather.3.cloned.1.call-done
  115.5 1.8 slice.53
  117.3 2.6 %copy.29 = bf16[1024,1024]{0,1:T(8,128)(2,1)} copy(bf16[1024,1024]{1,0:T(8,128)(2,1)S(1)} %slice.53) | data formatting | bytes 4194304 | tf_op jit(solution)/shard_map/slice | solution.py:41
  119.9 5.1 %all-to-all-done.2 = bf16[8,8,64,128]{3,2,1,0:T(8,128)(2,1)} async-done(((bf16[8,8,64,128]{3,2,1,0:T(8,128)(2,1)}), bf16[8,8,64,128]{3,2,1,0:T(8,128)(2,1)}, u32[]{:S(2)}, u32[]{:S(2)}) %all-to-all-start.2) | async-done | bytes 1048608 | tf_op jit(solution)/shard_map/all_to_all | solution.py:82
  125.0 0.0 copy-start
  125.0 3.7 %fusion.104 = (f32[8,64]{1,0:T(8,128)S(1)}, f32[8,64,1024]{2,1,0:T(8,128)S(1)}) fusion(bf16[8,8,64,128]{3,2,1,0:T(8,128)(2,1)} %all-to-all-done.2, bf16[1024,8,128,1]{0,2,3,1:T(8,128)(2,1)} %bitcast.72, bf16[8,512,1024]{2,1,0:T(8,128)(2,1)} %param.8, s32[]{:T(128)S(6)} %select_n.19), kind=kOutput, calls=%fused_computation.134 | convolution fusion | flops 1075314176 | bytes 6293508 | tf_op jit(solution)/shard_map/sprf,esf->pre/dot_general | solution.py:84
  128.7 0.3 multiply_reduce_fusion.1
  129.1 1.4 copy-done
  130.5 9.1 %fusion.55 = (u8[64,4096]{1,0:T(8,128)(4,1)S(1)}, u8[64,4096]{1,0:T(8,128)(4,1)S(1)}, f32[8,64,4096]{2,1,0:T(8,128)}) fusion(bf16[1024,5120]{1,0:T(8,128)(2,1)S(1)} %copy-done, f32[8,64,1024]{2,1,0:T(8,128)S(1)} %get-tuple-element.26, f32[1024]{0:T(1024)S(1)} %bitcast.81, f32[1024]{0:T(1024)S(1)} %bitcast.79, f32[8,64]{1,0:T(8,128)S(1)} %add_rsqrt_fusion.1, ...), kind=kOutput, calls=%fused_computation.76 | convolution fusion | flops 4324327424 | bytes 19415040 | tf_op jit(solution)/shard_map/pld,df->plf/dot_general | solution.py:91
  139.6 22.8 %all-gather.5.cloned.1.call-done = bf16[1024,4096]{1,0:T(8,128)(2,1)} async-done(((bf16[64,4096]{1,0:T(8,128)(2,1)}), bf16[1024,4096]{1,0:T(8,128)(2,1)}) %all-gather.5.cloned.1.call-update) | async-done | bytes 8388624 | tf_op jit(solution)/shard_map/all_gather | solution.py:43
  162.4 25.0 %fusion.105 = (f32[8,64]{1,0:T(8,128)S(1)}, f32[8,64,1024]{2,1,0:T(8,128)S(1)}) fusion(bf16[1024,4096]{1,0:T(8,128)(2,1)} %all-gather.5.cloned.1.call-done, f32[8,64,4096]{2,1,0:T(8,128)} %get-tuple-element.27, u8[64,4096]{1,0:T(8,128)(4,1)S(1)} %get-tuple-element.13, u8[64,4096]{1,0:T(8,128)(4,1)S(1)} %get-tuple-element.12, f32[1024]{0:T(1024)S(1)} %bitcast.82, ...), kind=kOutput, calls=%fused_computation.135 | convolution fusion | flops 4445961728 | bytes 21510144 | tf_op jit(solution)/shard_map/plf,ef->ple/dot_general | solution.py:94
  187.4 0.3 multiply_reduce_fusion
  187.8 2.6 %select_convert_fusion = bf16[8,64,1024]{2,1,0:T(8,128)(2,1)} fusion(f32[8,64,1024]{2,1,0:T(8,128)S(1)} %get-tuple-element.29, f32[1024]{0:T(1024)S(1)} %bitcast.78, f32[1024]{0:T(1024)S(1)} %bitcast.77, f32[8,64]{1,0:T(8,128)S(1)} %add_rsqrt_fusion, f32[8,64]{1,0:T(8,128)S(1)} %broadcast_multiply_fusion, pred[8,64]{1,0:T(8,128)(4,1)S(1)} %constant_dynamic-slice_fusion), kind=kLoop, calls=%fused_computation.70 | loop fusion | flops 3145728 | bytes 3158528 | tf_op jit(solution)/shard_map/convert_element_type | solution.py:98
  (8 shorter events, 0.1 us)
Async XLA Ops:
  7.2 39.1 %copy-start.3 = (s32[8]{0:T(128)S(1)}, s32[8]{0:T(128)}, u32[]{:S(2)}) copy-start(s32[8]{0:T(128)} %param.9) | copy-start | bytes 100
  7.2 108.4 %all-gather.3.cloned.1.call-start = ((), (), s32[]{:S(2)}) async-start(), calls=%async_computation.3 | async-start | bytes 11141120 | tf_op jit(solution)/shard_map/all_gather | solution.py:40
  36.6 125.8 %all-gather.5.cloned.1.call-start = ((), (), s32[]{:S(2)}) async-start(), calls=%async_computation.4 | async-start | bytes 8912896 | tf_op jit(solution)/shard_map/all_gather | solution.py:43
  38.5 29.1 %all-to-all-start.1 = ((bf16[16,64,384]{2,1,0:T(8,128)(2,1)}), bf16[16,64,384]{2,1,0:T(8,128)(2,1)S(1)}, u32[]{:S(2)}, u32[]{:S(2)}) async-start(bf16[16,64,384]{2,1,0:T(8,128)(2,1)} %broadcast_in_dim.37), calls=%async_computation.1 | async-start | bytes 1572864 | tf_op jit(solution)/shard_map/all_to_all | solution.py:37
  97.7 11.8 %copy-start.1 = (f32[2,1024]{1,0:T(2,128)S(1)}, f32[2,1024]{1,0:T(2,128)}, u32[]{:S(2)}) copy-start(f32[2,1024]{1,0:T(2,128)} %param.14) | copy-start | bytes 24580
  97.7 11.8 %copy-start.2 = (f32[2,1024]{1,0:T(2,128)S(1)}, f32[2,1024]{1,0:T(2,128)}, u32[]{:S(2)}) copy-start(f32[2,1024]{1,0:T(2,128)} %param.15) | copy-start | bytes 24580
  105.0 20.0 %all-to-all-start.2 = ((bf16[8,8,64,128]{3,2,1,0:T(8,128)(2,1)}), bf16[8,8,64,128]{3,2,1,0:T(8,128)(2,1)}, u32[]{:S(2)}, u32[]{:S(2)}) async-start(bf16[8,8,64,128]{3,2,1,0:T(8,128)(2,1)} %copy.28), calls=%async_computation.2 | async-start | bytes 2097152 | tf_op jit(solution)/shard_map/all_to_all | solution.py:82
  125.0 5.5 %copy-start = (bf16[1024,5120]{1,0:T(8,128)(2,1)S(1)}, bf16[1024,5120]{1,0:T(8,128)(2,1)}, u32[]{:S(2)}) copy-start(bf16[1024,5120]{1,0:T(8,128)(2,1)} %all-gather.3.cloned.1.call-done) | copy-start | bytes 31457284
Sparse Core Ops, SparseCore 0:
  36.8 71.0 all-gather.2
  109.6 52.7 all-gather.4

commit v12 on v11

--- a/solution.py
+++ b/solution.py
@@ -81,8 +81,10 @@
     context_blocks = jnp.transpose(context, (1, 0, 2, 3))
     context_blocks = lax.all_to_all(context_blocks, "head", 0, 0, tiled=True)
     proj_blocks = proj_weight_t.reshape(model_width, heads_axis, block_width)
-    attn_rows = jnp.einsum(
-        "sprf,esf->pre", context_blocks, proj_blocks, preferred_element_type=jnp.float32)
+    attn_blocks = jnp.einsum(
+        "sprf,esf->spre", context_blocks, proj_blocks, preferred_element_type=jnp.float32
+    ).astype(jnp.bfloat16)
+    attn_rows = jnp.sum(attn_blocks.astype(jnp.float32), axis=0)
     token_rows = lax.dynamic_slice_in_dim(tokens, row_start, row_count, 1)
     normed_rows = layer_norm(
         token_rows.astype(jnp.float32) + attn_rows, norm_gain[0], norm_shift[0]
@@ -91,6 +93,7 @@
         jnp.einsum("pld,df->plf", normed_rows, up_weight, preferred_element_type=jnp.float32),
         approximate=False,
     ).astype(jnp.bfloat16)
+    hidden = lax.optimization_barrier(hidden)
     mlp_rows = jnp.einsum(
         "plf,ef->ple", hidden, down_weight_t, preferred_element_type=jnp.float32)
     finished = layer_norm(normed_rows.astype(jnp.float32) + mlp_rows, norm_gain[1], norm_shift[1])

time: 199 us -> 182 us (0.915)
  waiting for transfers between devices: 49.2 us -> 29.7 us
  other arithmetic: 8.37 us -> 13.1 us
    all_gather x1, waiting for transfers between devices: 22.8 us -> 3.33 us  [regroup_weights(): lax.all_gather(packed[:, early_end:], 'seq', axis=0, tiled=True)]
    dot_general x1, matrix products: 25 us -> 8.37 us  [encode_chunk(): jnp.einsum('plf,ef->ple', hidden, down_weight_t, preferred_element_type=j...]
    dot_general x1, matrix products: 9.15 us -> 24.6 us  [encode_chunk(): jnp.einsum('pld,df->plf', normed_rows, up_weight, preferred_element_type=...]
    reshape x1 -> x2, local copies, waits for them, and re-layouts: 3.97 us -> 7.3 us  [encode_chunk(): context.astype(jnp.bfloat16)]
    transpose x1 -> x0, local copies, waits for them, and re-layouts: 3.33 us -> none  [encode_chunk(): context_blocks = jnp.transpose(context, (1, 0, 2, 3))]
    unnamed x10 -> x8, local copies, waits for them, and re-layouts: 5.93 us -> 4.53 us
  transfers between devices with their start and end apart: 4 -> 4, of which waited for: 3 -> 3; matrix products, arithmetic and copies ran while one was open for 32% -> 46% of each run, Pallas kernels for 0% -> 0%
where the time goes in v12:
time: 182 us; the launch traced here: 181 us
  matrix products  64.6 us (35%)
  waiting for transfers between devices  29.7 us (16%)
  blocking collectives  24.8 us (14%)
  local copies, waits for them, and re-layouts  21.9 us (12%)
  between operations  14.2 us (8%)
  other arithmetic  13.1 us (7%)
  starting transfers between devices  12.2 us (7%)
    all_to_all x1, blocking collectives, regroup_weights(): packed = lax.all_to_all(packed, 'head', 1, 0, tiled=True)  24.8 us
    dot_general x1, matrix products, encode_chunk(): jnp.einsum('pld,df->plf', normed_rows, up_weight, preferred_element_type=...  24.6 us
    all_to_all x1, waiting for transfers between devices, regroup_weights(): qkv_weight = lax.all_to_all(in_part, 'seq', 0, 0, tiled=True)  21.3 us
    sub x1, matrix products, encode_chunk(): raised = jnp.exp(scores - row_peak)  10.8 us
    dot_general x1, matrix products, encode_chunk(): jnp.einsum('phqk,pkhd->pqhd', weights, value_heads, preferred_element_typ...  9.01 us
    dot_general x1, matrix products, encode_chunk(): jnp.einsum('plf,ef->ple', hidden, down_weight_t, preferred_element_type=j...  8.37 us
    all_to_all x1, starting transfers between devices, regroup_weights(): qkv_weight = lax.all_to_all(in_part, 'seq', 0, 0, tiled=True)  7.74 us
    dot_general x1, matrix products, encode_chunk(): jnp.einsum('pld,dte->plte', tokens, qkv_weight, preferred_element_type=jn...  7.39 us
  transfers between devices with their start and end apart: 4, of which 3 were waited for; matrix products, arithmetic and copies ran while one was open for 46% of the time, Pallas kernels for 0%

profile of v12, /device:TPU:1, one launch (start us, length us, event | category | flops | bytes accessed | tf_op | source)
XLA Modules:
  0.0 180.6 jit_solution(1297860315983872580)
XLA Ops:
  7.2 0.0 copy-start.2
  7.2 0.0 all-gather.3.cloned.1.call-start
  7.2 0.9 convert_bitcast_fusion.1
  8.1 0.9 convert_element_type.51
  9.0 0.8 convert_bitcast_fusion.3
  9.8 0.9 copy_bitcast_fusion
  10.7 0.1 broadcast_in_dim.36
  10.8 0.1 pad_maximum_fusion
  10.9 24.8 %all_to_all.25 = bf16[8,8,9600]{2,0,1:T(8,128)(2,1)S(1)} all-to-all(bf16[8,8,9600]{2,0,1:T(8,128)(2,1)S(1)} %pad_maximum_fusion), channel_id=1, replica_groups=mesh['seq'=16,'head'=8] {'head'}, dimensions={1} | all-to-all | bytes 2457600 | tf_op jit(solution)/shard_map/all_to_all | solution.py:33
  35.7 0.9 slice.52
  36.6 0.0 all-gather.3.cloned.1.call-update
  36.6 0.0 all-gather.5.cloned.1.call-start
  36.7 0.8 slice.55
  37.5 0.0 all-gather.5.cloned.1.call-update
  37.6 1.0 broadcast_in_dim.37
  38.5 7.7 %all-to-all-start.1 = ((bf16[16,64,384]{2,1,0:T(8,128)(2,1)}), bf16[16,64,384]{2,1,0:T(8,128)(2,1)S(1)}, u32[]{:S(2)}, u32[]{:S(2)}) async-start(bf16[16,64,384]{2,1,0:T(8,128)(2,1)} %broadcast_in_dim.37), calls=%async_computation.1 | async-start | bytes 1572864 | tf_op jit(solution)/shard_map/all_to_all | solution.py:37
  46.3 0.0 copy-done.2
  46.3 0.1 iota_compare_fusion
  46.4 21.3 %all-to-all-done.1 = bf16[16,64,384]{2,1,0:T(8,128)(2,1)S(1)} async-done(((bf16[16,64,384]{2,1,0:T(8,128)(2,1)}), bf16[16,64,384]{2,1,0:T(8,128)(2,1)S(1)}, u32[]{:S(2)}, u32[]{:S(2)}) %all-to-all-start.1) | async-done | bytes 786464 | tf_op jit(solution)/shard_map/all_to_all | solution.py:37
  67.6 1.1 reshape.96
  68.7 7.4 %convert_bitcast_fusion = bf16[8,512,3,128]{1,3,0,2:T(8,128)(2,1)S(1)} fusion(bf16[8,512,1024]{2,1,0:T(8,128)(2,1)} %param.8, bf16[1024,3,128,1]{2,1,0,3:T(4,128)(2,1)} %bitcast.73), kind=kOutput, calls=%fused_computation.35 | convolution fusion | flops 3222798336 | bytes 12320768 | tf_op jit(solution)/shard_map/pld,dte->plte/dot_general | solution.py:58
  76.1 1.8 fusion.33
  77.9 10.8 %fusion.36 = (f32[8,2,512]{2,1,0:T(2,128)S(1)}, f32[8,2,512,512]{2,3,1,0:T(8,128)}) fusion(pred[8,512]{1,0:T(8,128)(4,1)S(1)} %iota_compare_fusion, bf16[8,512,2,64]{1,3,2,0:T(8,128)(2,1)} %bitcast.76, bf16[8,512,2,64]{1,3,2,0:T(8,128)(2,1)} %bitcast.75), kind=kOutput, calls=%fused_computation.66 | convolution fusion | flops 553648640 | bytes 18911232 | tf_op jit(solution)/shard_map/sub | solution.py:73
  88.7 9.0 %fusion.28 = bf16[8,512,2,64]{1,3,2,0:T(8,128)(2,1)} fusion(bf16[8,512,2,64]{1,3,2,0:T(8,128)(2,1)} %bitcast.74, f32[8,2,512,512]{2,3,1,0:T(8,128)} %get-tuple-element.19, f32[8,2,512]{2,1,0:T(2,128)S(1)} %get-tuple-element.18), kind=kOutput, calls=%fused_computation.44 | convolution fusion | flops 545783808 | bytes 18907136 | tf_op jit(solution)/shard_map/phqk,pkhd->pqhd/dot_general | solution.py:75
  97.7 0.0 copy-start
  97.7 0.0 copy-start.1
  97.7 4.0 %reshape.97 = bf16[8,8,64,128]{2,1,3,0:T(8,128)(2,1)} reshape(bf16[8,512,2,64]{1,3,2,0:T(8,128)(2,1)} %fusion.28) | data formatting | bytes 2097152 | tf_op jit(solution)/shard_map/reshape | solution.py:78
  101.7 3.3 %copy.20 = bf16[8,8,64,128]{3,2,0,1:T(8,128)(2,1)} copy(bf16[8,8,64,128]{2,1,3,0:T(8,128)(2,1)} %reshape.97) | data formatting | bytes 2097152 | tf_op jit(solution)/shard_map/reshape | solution.py:78
  105.0 4.4 %all-to-all-start.2 = ((bf16[8,8,64,128]{3,2,1,0:T(8,128)(2,1)}), bf16[8,8,64,128]{3,2,1,0:T(8,128)(2,1)}, u32[]{:S(2)}, u32[]{:S(2)}) async-start(bf16[8,8,64,128]{3,2,1,0:T(8,128)(2,1)} %bitcast.71), calls=%async_computation.2 | async-start | bytes 2097152 | tf_op jit(solution)/shard_map/all_to_all | solution.py:82
  109.4 0.1 constant_dynamic-slice_fusion
  109.5 0.0 copy-done
  109.5 0.0 copy-done.1
  109.6 1.5 bitcast_select_fusion
  111.0 2.3 %copy.23 = bf16[8,512,128]{2,1,0:T(8,128)(2,1)} copy(bf16[8,512,128]{1,2,0:T(8,128)(2,1)} %get-tuple-element.10) | data formatting | bytes 2097152
  113.3 2.3 %copy.24 = bf16[8,512,128]{2,1,0:T(8,128)(2,1)} copy(bf16[8,512,128]{1,2,0:T(8,128)(2,1)} %get-tuple-element.9) | data formatting | bytes 2097152
  115.5 0.0 all-gather.3.cloned.1.call-done
  115.5 1.8 slice.53
  117.3 2.6 %copy.21 = bf16[1024,1024]{0,1:T(8,128)(2,1)} copy(bf16[1024,1024]{1,0:T(8,128)(2,1)S(1)} %slice.53) | data formatting | bytes 4194304 | tf_op jit(solution)/shard_map/slice | solution.py:41
  119.9 5.1 %all-to-all-done.2 = bf16[8,8,64,128]{3,2,1,0:T(8,128)(2,1)} async-done(((bf16[8,8,64,128]{3,2,1,0:T(8,128)(2,1)}), bf16[8,8,64,128]{3,2,1,0:T(8,128)(2,1)}, u32[]{:S(2)}, u32[]{:S(2)}) %all-to-all-start.2) | async-done | bytes 1048608 | tf_op jit(solution)/shard_map/all_to_all | solution.py:82
  125.0 4.4 %convert_reduce_fusion = f32[8,64,1024]{2,1,0:T(8,128)S(1)} fusion(bf16[8,8,64,128]{3,2,1,0:T(8,128)(2,1)} %all-to-all-done.2, bf16[1024,8,128,1]{0,2,3,1:T(8,128)(2,1)} %bitcast.72), kind=kOutput, calls=%fused_computation.1 | convolution fusion | flops 1085800448 | bytes 5242880 | tf_op jit(solution)/shard_map/sprf,esf->spre/dot_general | solution.py:84
  129.4 1.5 fusion.30
  131.0 1.7 multiply_reduce_fusion.1
  132.7 1.8 %add_convert_fusion = bf16[8,64,1024]{2,1,0:T(8,128)(2,1)S(1)} fusion(f32[1024]{0:T(1024)S(1)} %bitcast.80, f32[1024]{0:T(1024)S(1)} %bitcast.79, f32[8,64]{1,0:T(8,128)S(1)} %add_rsqrt_fusion.1, f32[8,64]{1,0:T(8,128)S(1)} %broadcast_multiply_fusion.1, f32[8,64,1024]{2,1,0:T(8,128)S(1)} %convert_reduce_fusion, bf16[8,512,1024]{2,1,0:T(8,128)(2,1)} %param.8, ...), kind=kLoop, calls=%fused_computation.39 | loop fusion | flops 3670016 | bytes 4206596 | tf_op jit(solution)/shard_map/convert_element_type | solution.py:91
  134.5 24.6 %fusion.4 = bf16[8,64,4096]{2,1,0:T(8,128)(2,1)} fusion(bf16[8,64,1024]{2,1,0:T(8,128)(2,1)S(1)} %add_convert_fusion, bf16[1024,5120]{1,0:T(8,128)(2,1)} %all-gather.3.cloned.1.call-done), kind=kOutput, calls=%fused_computation.9 | convolution fusion | flops 4431282176 | bytes 13631488 | tf_op jit(solution)/shard_map/pld,df->plf/dot_general | solution.py:93
  159.1 3.3 %all-gather.5.cloned.1.call-done = bf16[1024,4096]{1,0:T(8,128)(2,1)} async-done(((bf16[64,4096]{1,0:T(8,128)(2,1)}), bf16[1024,4096]{1,0:T(8,128)(2,1)}) %all-gather.5.cloned.1.call-update) | async-done | bytes 8388624 | tf_op jit(solution)/shard_map/all_gather | solution.py:43
  162.4 8.4 %fusion.37 = (f32[8,64]{1,0:T(8,128)S(1)}, f32[8,64,1024]{2,1,0:T(8,128)S(1)}) fusion(bf16[8,64,4096]{2,1,0:T(8,128)(2,1)} %fusion.4, bf16[1024,4096]{1,0:T(8,128)(2,1)} %all-gather.5.cloned.1.call-done, bf16[8,64,1024]{2,1,0:T(8,128)(2,1)S(1)} %add_convert_fusion), kind=kOutput, calls=%fused_computation.67 | convolution fusion | flops 4296539648 | bytes 15730688 | tf_op jit(solution)/shard_map/plf,ef->ple/dot_general | solution.py:97
  170.8 0.3 multiply_reduce_fusion
  171.2 2.6 %select_convert_fusion = bf16[8,64,1024]{2,1,0:T(8,128)(2,1)} fusion(f32[8,64,1024]{2,1,0:T(8,128)S(1)} %get-tuple-element.21, f32[1024]{0:T(1024)S(1)} %bitcast.78, f32[1024]{0:T(1024)S(1)} %bitcast.77, f32[8,64]{1,0:T(8,128)S(1)} %add_rsqrt_fusion, f32[8,64]{1,0:T(8,128)S(1)} %broadcast_multiply_fusion, pred[8,64]{1,0:T(8,128)(4,1)S(1)} %constant_dynamic-slice_fusion), kind=kLoop, calls=%fused_computation.36 | loop fusion | flops 3145728 | bytes 3158528 | tf_op jit(solution)/shard_map/convert_element_type | solution.py:101
  (8 shorter events, 0.1 us)
Async XLA Ops:
  7.2 39.1 %copy-start.2 = (s32[8]{0:T(128)S(1)}, s32[8]{0:T(128)}, u32[]{:S(2)}) copy-start(s32[8]{0:T(128)} %param.9) | copy-start | bytes 100
  7.2 108.4 %all-gather.3.cloned.1.call-start = ((), (), s32[]{:S(2)}) async-start(), calls=%async_computation.3 | async-start | bytes 11141120 | tf_op jit(solution)/shard_map/all_gather | solution.py:40
  36.6 125.8 %all-gather.5.cloned.1.call-start = ((), (), s32[]{:S(2)}) async-start(), calls=%async_computation.4 | async-start | bytes 8912896 | tf_op jit(solution)/shard_map/all_gather | solution.py:43
  38.5 29.1 %all-to-all-start.1 = ((bf16[16,64,384]{2,1,0:T(8,128)(2,1)}), bf16[16,64,384]{2,1,0:T(8,128)(2,1)S(1)}, u32[]{:S(2)}, u32[]{:S(2)}) async-start(bf16[16,64,384]{2,1,0:T(8,128)(2,1)} %broadcast_in_dim.37), calls=%async_computation.1 | async-start | bytes 1572864 | tf_op jit(solution)/shard_map/all_to_all | solution.py:37
  97.7 11.8 %copy-start = (f32[2,1024]{1,0:T(2,128)S(1)}, f32[2,1024]{1,0:T(2,128)}, u32[]{:S(2)}) copy-start(f32[2,1024]{1,0:T(2,128)} %param.14) | copy-start | bytes 24580
  97.7 11.8 %copy-start.1 = (f32[2,1024]{1,0:T(2,128)S(1)}, f32[2,1024]{1,0:T(2,128)}, u32[]{:S(2)}) copy-start(f32[2,1024]{1,0:T(2,128)} %param.15) | copy-start | bytes 24580
  105.0 20.0 %all-to-all-start.2 = ((bf16[8,8,64,128]{3,2,1,0:T(8,128)(2,1)}), bf16[8,8,64,128]{3,2,1,0:T(8,128)(2,1)}, u32[]{:S(2)}, u32[]{:S(2)}) async-start(bf16[8,8,64,128]{3,2,1,0:T(8,128)(2,1)} %bitcast.71), calls=%async_computation.2 | async-start | bytes 2097152 | tf_op jit(solution)/shard_map/all_to_all | solution.py:82
Sparse Core Ops, SparseCore 0:
  36.8 71.0 all-gather.2
  109.6 52.7 all-gather.4

commit v13 on v11

--- a/solution.py
+++ b/solution.py
@@ -91,6 +91,7 @@
         jnp.einsum("pld,df->plf", normed_rows, up_weight, preferred_element_type=jnp.float32),
         approximate=False,
     ).astype(jnp.bfloat16)
+    hidden = lax.optimization_barrier(hidden)
     mlp_rows = jnp.einsum(
         "plf,ef->ple", hidden, down_weight_t, preferred_element_type=jnp.float32)
     finished = layer_norm(normed_rows.astype(jnp.float32) + mlp_rows, norm_gain[1], norm_shift[1])

time: 199 us -> 182 us (0.915)
  waiting for transfers between devices: 49.2 us -> 34.9 us
  matrix products: 65.1 us -> 62.8 us
    dot_general x1, matrix products: 25 us -> 8.41 us  [encode_chunk(): jnp.einsum('plf,ef->ple', hidden, down_weight_t, preferred_element_type=j...]
    all_gather x1, waiting for transfers between devices: 22.8 us -> 8.47 us  [regroup_weights(): lax.all_gather(packed[:, early_end:], 'seq', axis=0, tiled=True)]
    dot_general x1, matrix products: 9.15 us -> 23.4 us  [encode_chunk(): jnp.einsum('pld,df->plf', normed_rows, up_weight, preferred_element_type=...]
  transfers between devices with their start and end apart: 4 -> 4, of which waited for: 3 -> 3; matrix products, arithmetic and copies ran while one was open for 32% -> 43% of each run, Pallas kernels for 0% -> 0%
where the time goes in v13:
time: 182 us; the launch traced here: 181 us
  matrix products  62.8 us (35%)
  waiting for transfers between devices  34.9 us (19%)
  blocking collectives  24.8 us (14%)
  local copies, waits for them, and re-layouts  23.2 us (13%)
  between operations  14.2 us (8%)
  starting transfers between devices  12.2 us (7%)
  other arithmetic  8.38 us (5%)
    all_to_all x1, blocking collectives, regroup_weights(): packed = lax.all_to_all(packed, 'head', 1, 0, tiled=True)  24.8 us
    dot_general x1, matrix products, encode_chunk(): jnp.einsum('pld,df->plf', normed_rows, up_weight, preferred_element_type=...  23.4 us
    all_to_all x1, waiting for transfers between devices, regroup_weights(): qkv_weight = lax.all_to_all(in_part, 'seq', 0, 0, tiled=True)  21.3 us
    sub x1, matrix products, encode_chunk(): raised = jnp.exp(scores - row_peak)  10.8 us
    dot_general x1, matrix products, encode_chunk(): jnp.einsum('phqk,pkhd->pqhd', weights, value_heads, preferred_element_typ...  9.01 us
    all_gather x1, waiting for transfers between devices, regroup_weights(): lax.all_gather(packed[:, early_end:], 'seq', axis=0, tiled=True)  8.47 us
    dot_general x1, matrix products, encode_chunk(): jnp.einsum('plf,ef->ple', hidden, down_weight_t, preferred_element_type=j...  8.41 us
    all_to_all x1, starting transfers between devices, regroup_weights(): qkv_weight = lax.all_to_all(in_part, 'seq', 0, 0, tiled=True)  7.74 us
  transfers between devices with their start and end apart: 4, of which 3 were waited for; matrix products, arithmetic and copies ran while one was open for 43% of the time, Pallas kernels for 0%

profile of v13, /device:TPU:1, one launch (start us, length us, event | category | flops | bytes accessed | tf_op | source)
XLA Modules:
  0.0 180.6 jit_solution(4619803239640551789)
XLA Ops:
  7.2 0.0 copy-start.3
  7.2 0.0 all-gather.3.cloned.1.call-start
  7.2 0.9 convert_bitcast_fusion.1
  8.1 0.9 convert_element_type.45
  9.0 0.8 convert_bitcast_fusion.3
  9.8 0.9 copy_bitcast_fusion
  10.7 0.1 broadcast_in_dim.36
  10.8 0.1 pad_maximum_fusion
  10.9 24.8 %all_to_all.25 = bf16[8,8,9600]{2,0,1:T(8,128)(2,1)S(1)} all-to-all(bf16[8,8,9600]{2,0,1:T(8,128)(2,1)S(1)} %pad_maximum_fusion), channel_id=1, replica_groups=mesh['seq'=16,'head'=8] {'head'}, dimensions={1} | all-to-all | bytes 2457600 | tf_op jit(solution)/shard_map/all_to_all | solution.py:33
  35.7 0.9 slice.52
  36.6 0.0 all-gather.3.cloned.1.call-update
  36.6 0.0 all-gather.5.cloned.1.call-start
  36.7 0.8 slice.55
  37.5 0.0 all-gather.5.cloned.1.call-update
  37.5 1.0 broadcast_in_dim.37
  38.5 7.7 %all-to-all-start.1 = ((bf16[16,64,384]{2,1,0:T(8,128)(2,1)}), bf16[16,64,384]{2,1,0:T(8,128)(2,1)S(1)}, u32[]{:S(2)}, u32[]{:S(2)}) async-start(bf16[16,64,384]{2,1,0:T(8,128)(2,1)} %broadcast_in_dim.37), calls=%async_computation.1 | async-start | bytes 1572864 | tf_op jit(solution)/shard_map/all_to_all | solution.py:37
  46.3 0.0 copy-done.3
  46.3 0.1 iota_compare_fusion
  46.3 21.3 %all-to-all-done.1 = bf16[16,64,384]{2,1,0:T(8,128)(2,1)S(1)} async-done(((bf16[16,64,384]{2,1,0:T(8,128)(2,1)}), bf16[16,64,384]{2,1,0:T(8,128)(2,1)S(1)}, u32[]{:S(2)}, u32[]{:S(2)}) %all-to-all-start.1) | async-done | bytes 786464 | tf_op jit(solution)/shard_map/all_to_all | solution.py:37
  67.6 1.1 reshape.96
  68.7 7.4 %convert_bitcast_fusion = bf16[8,512,3,128]{1,3,0,2:T(8,128)(2,1)S(1)} fusion(bf16[8,512,1024]{2,1,0:T(8,128)(2,1)} %param.8, bf16[1024,3,128,1]{2,1,0,3:T(4,128)(2,1)} %bitcast.74), kind=kOutput, calls=%fused_computation.34 | convolution fusion | flops 3222798336 | bytes 12320768 | tf_op jit(solution)/shard_map/pld,dte->plte/dot_general | solution.py:58
  76.1 1.8 fusion.32
  77.9 10.8 %fusion.35 = (f32[8,2,512]{2,1,0:T(2,128)S(1)}, f32[8,2,512,512]{2,3,1,0:T(8,128)}) fusion(pred[8,512]{1,0:T(8,128)(4,1)S(1)} %iota_compare_fusion, bf16[8,512,2,64]{1,3,2,0:T(8,128)(2,1)} %bitcast.77, bf16[8,512,2,64]{1,3,2,0:T(8,128)(2,1)} %bitcast.76), kind=kOutput, calls=%fused_computation.64 | convolution fusion | flops 553648640 | bytes 18911232 | tf_op jit(solution)/shard_map/sub | solution.py:73
  88.7 9.0 %fusion.28 = bf16[8,512,2,64]{1,3,2,0:T(8,128)(2,1)} fusion(bf16[8,512,2,64]{1,3,2,0:T(8,128)(2,1)} %bitcast.75, f32[8,2,512,512]{2,3,1,0:T(8,128)} %get-tuple-element.22, f32[8,2,512]{2,1,0:T(2,128)S(1)} %get-tuple-element.21), kind=kOutput, calls=%fused_computation.43 | convolution fusion | flops 545783808 | bytes 18907136 | tf_op jit(solution)/shard_map/phqk,pkhd->pqhd/dot_general | solution.py:75
  97.7 0.0 copy-start.1
  97.7 0.0 copy-start.2
  97.7 3.9 %reshape.97 = bf16[8,8,64,128]{2,1,3,0:T(8,128)(2,1)} reshape(bf16[8,512,2,64]{1,3,2,0:T(8,128)(2,1)} %fusion.28) | data formatting | bytes 2097152 | tf_op jit(solution)/shard_map/reshape | solution.py:78
  101.7 3.3 %copy.28 = bf16[8,8,64,128]{3,2,1,0:T(8,128)(2,1)} copy(bf16[8,8,64,128]{2,0,3,1:T(8,128)(2,1)} %bitcast.69) | data formatting | bytes 2097152 | tf_op jit(solution)/shard_map/transpose | solution.py:81
  105.0 4.4 %all-to-all-start.2 = ((bf16[8,8,64,128]{3,2,1,0:T(8,128)(2,1)}), bf16[8,8,64,128]{3,2,1,0:T(8,128)(2,1)}, u32[]{:S(2)}, u32[]{:S(2)}) async-start(bf16[8,8,64,128]{3,2,1,0:T(8,128)(2,1)} %copy.28), calls=%async_computation.2 | async-start | bytes 2097152 | tf_op jit(solution)/shard_map/all_to_all | solution.py:82
  109.4 0.1 constant_dynamic-slice_fusion
  109.5 0.0 copy-done.1
  109.5 0.0 copy-done.2
  109.5 1.5 bitcast_select_fusion
  111.0 2.3 %copy.32 = bf16[8,512,128]{2,1,0:T(8,128)(2,1)} copy(bf16[8,512,128]{1,2,0:T(8,128)(2,1)} %get-tuple-element.13) | data formatting | bytes 2097152
  113.3 2.3 %copy.33 = bf16[8,512,128]{2,1,0:T(8,128)(2,1)} copy(bf16[8,512,128]{1,2,0:T(8,128)(2,1)} %get-tuple-element.12) | data formatting | bytes 2097152
  115.5 0.0 all-gather.3.cloned.1.call-done
  115.5 1.8 slice.53
  117.3 2.6 %copy.29 = bf16[1024,1024]{0,1:T(8,128)(2,1)} copy(bf16[1024,1024]{1,0:T(8,128)(2,1)S(1)} %slice.53) | data formatting | bytes 4194304 | tf_op jit(solution)/shard_map/slice | solution.py:41
  119.9 5.1 %all-to-all-done.2 = bf16[8,8,64,128]{3,2,1,0:T(8,128)(2,1)} async-done(((bf16[8,8,64,128]{3,2,1,0:T(8,128)(2,1)}), bf16[8,8,64,128]{3,2,1,0:T(8,128)(2,1)}, u32[]{:S(2)}, u32[]{:S(2)}) %all-to-all-start.2) | async-done | bytes 1048608 | tf_op jit(solution)/shard_map/all_to_all | solution.py:82
  125.0 0.0 copy-start
  125.0 3.7 %fusion.36 = (f32[8,64]{1,0:T(8,128)S(1)}, f32[8,64,1024]{2,1,0:T(8,128)S(1)}) fusion(bf16[8,8,64,128]{3,2,1,0:T(8,128)(2,1)} %all-to-all-done.2, bf16[1024,8,128,1]{0,2,3,1:T(8,128)(2,1)} %bitcast.73, bf16[8,512,1024]{2,1,0:T(8,128)(2,1)} %param.8, s32[]{:T(128)S(6)} %select_n.19), kind=kOutput, calls=%fused_computation.65 | convolution fusion | flops 1075314176 | bytes 6293508 | tf_op jit(solution)/shard_map/sprf,esf->pre/dot_general | solution.py:84
  128.7 0.3 multiply_reduce_fusion.1
  129.1 1.4 copy-done
  130.5 23.4 %fusion.4 = bf16[8,64,4096]{2,1,0:T(8,128)(2,1)} fusion(bf16[1024,5120]{1,0:T(8,128)(2,1)S(1)} %copy-done, f32[8,64,1024]{2,1,0:T(8,128)S(1)} %get-tuple-element.24, f32[1024]{0:T(1024)S(1)} %bitcast.82, f32[1024]{0:T(1024)S(1)} %bitcast.80, f32[8,64]{1,0:T(8,128)S(1)} %add_rsqrt_fusion.1, f32[8,64]{1,0:T(8,128)S(1)} %broadcast_multiply_fusion.1), kind=kOutput, calls=%fused_computation.8 | convolution fusion | flops 4433903616 | bytes 14696448 | tf_op jit(solution)/shard_map/pld,df->plf/dot_general | solution.py:91
  153.9 8.5 %all-gather.5.cloned.1.call-done = bf16[1024,4096]{1,0:T(8,128)(2,1)} async-done(((bf16[64,4096]{1,0:T(8,128)(2,1)}), bf16[1024,4096]{1,0:T(8,128)(2,1)}) %all-gather.5.cloned.1.call-update) | async-done | bytes 8388624 | tf_op jit(solution)/shard_map/all_gather | solution.py:43
  162.4 8.4 %fusion.37 = (f32[8,64]{1,0:T(8,128)S(1)}, f32[8,64,1024]{2,1,0:T(8,128)S(1)}) fusion(bf16[8,64,4096]{2,1,0:T(8,128)(2,1)} %fusion.4, bf16[1024,4096]{1,0:T(8,128)(2,1)} %all-gather.5.cloned.1.call-done, f32[1024]{0:T(1024)S(1)} %bitcast.83, f32[1024]{0:T(1024)S(1)} %bitcast.81, f32[8,64]{1,0:T(8,128)S(1)} %add_rsqrt_fusion.1, ...), kind=kOutput, calls=%fused_computation.66 | convolution fusion | flops 4299161088 | bytes 16791552 | tf_op jit(solution)/shard_map/plf,ef->ple/dot_general | solution.py:95
  170.8 0.3 multiply_reduce_fusion
  171.2 2.6 %select_convert_fusion = bf16[8,64,1024]{2,1,0:T(8,128)(2,1)} fusion(f32[8,64,1024]{2,1,0:T(8,128)S(1)} %get-tuple-element.26, f32[1024]{0:T(1024)S(1)} %bitcast.79, f32[1024]{0:T(1024)S(1)} %bitcast.78, f32[8,64]{1,0:T(8,128)S(1)} %add_rsqrt_fusion, f32[8,64]{1,0:T(8,128)S(1)} %broadcast_multiply_fusion, pred[8,64]{1,0:T(8,128)(4,1)S(1)} %constant_dynamic-slice_fusion), kind=kLoop, calls=%fused_computation.36 | loop fusion | flops 3145728 | bytes 3158528 | tf_op jit(solution)/shard_map/convert_element_type | solution.py:99
  (8 shorter events, 0.1 us)
Async XLA Ops:
  7.2 39.1 %copy-start.3 = (s32[8]{0:T(128)S(1)}, s32[8]{0:T(128)}, u32[]{:S(2)}) copy-start(s32[8]{0:T(128)} %param.9) | copy-start | bytes 100
  7.2 108.4 %all-gather.3.cloned.1.call-start = ((), (), s32[]{:S(2)}) async-start(), calls=%async_computation.3 | async-start | bytes 11141120 | tf_op jit(solution)/shard_map/all_gather | solution.py:40
  36.6 125.7 %all-gather.5.cloned.1.call-start = ((), (), s32[]{:S(2)}) async-start(), calls=%async_computation.4 | async-start | bytes 8912896 | tf_op jit(solution)/shard_map/all_gather | solution.py:43
  38.5 29.1 %all-to-all-start.1 = ((bf16[16,64,384]{2,1,0:T(8,128)(2,1)}), bf16[16,64,384]{2,1,0:T(8,128)(2,1)S(1)}, u32[]{:S(2)}, u32[]{:S(2)}) async-start(bf16[16,64,384]{2,1,0:T(8,128)(2,1)} %broadcast_in_dim.37), calls=%async_computation.1 | async-start | bytes 1572864 | tf_op jit(solution)/shard_map/all_to_all | solution.py:37
  97.7 11.8 %copy-start.1 = (f32[2,1024]{1,0:T(2,128)S(1)}, f32[2,1024]{1,0:T(2,128)}, u32[]{:S(2)}) copy-start(f32[2,1024]{1,0:T(2,128)} %param.14) | copy-start | bytes 24580
  97.7 11.8 %copy-start.2 = (f32[2,1024]{1,0:T(2,128)S(1)}, f32[2,1024]{1,0:T(2,128)}, u32[]{:S(2)}) copy-start(f32[2,1024]{1,0:T(2,128)} %param.15) | copy-start | bytes 24580
  105.0 20.0 %all-to-all-start.2 = ((bf16[8,8,64,128]{3,2,1,0:T(8,128)(2,1)}), bf16[8,8,64,128]{3,2,1,0:T(8,128)(2,1)}, u32[]{:S(2)}, u32[]{:S(2)}) async-start(bf16[8,8,64,128]{3,2,1,0:T(8,128)(2,1)} %copy.28), calls=%async_computation.2 | async-start | bytes 2097152 | tf_op jit(solution)/shard_map/all_to_all | solution.py:82
  125.0 5.5 %copy-start = (bf16[1024,5120]{1,0:T(8,128)(2,1)S(1)}, bf16[1024,5120]{1,0:T(8,128)(2,1)}, u32[]{:S(2)}) copy-start(bf16[1024,5120]{1,0:T(8,128)(2,1)} %all-gather.3.cloned.1.call-done) | copy-start | bytes 31457284
Sparse Core Ops, SparseCore 0:
  36.8 71.0 all-gather.2
  109.6 52.7 all-gather.4
